TPU v7x, 256 devices: a whole 4x4x8 slice. The times are simulated.
256 devices in a mesh: feat: 32 (over z, x), blk: 8 (over y, core).
Axes of the slice: x: 4, y: 4, z: 8, core: 2. Of those that a mesh axis runs over, the one named last changes fastest.
Arguments:
- features: bfloat16 [1024, 32, 8192], P('feat', None, 'blk'), may hold values from -6 to 6
- adj_local: bfloat16 [262144, 1024], P(('feat', 'blk')), may hold values from 0.049804688 to 1
- adj_remote: bfloat16 [262144, 1792], P(('feat', 'blk')), may hold values from 0.049804688 to 1
- tile_mask: int32 [2048, 22], P(('feat', 'blk')), may hold values from 0 to 1, as said below
- w_self: bfloat16 [1024, 256], replicated, may hold values from -0.1875 to 0.1875
- w_neigh: bfloat16 [1024, 256], replicated, may hold values from -0.1875 to 0.1875
- out_bias: float32 [256], replicated, may hold values from -4 to 4
Outputs:
- hidden_out: bfloat16 [262144, 256], P(('feat', 'blk'))
Inputs may be any that keep to these rules, and one draw needn't show every extreme that they name: `tile_mask`: 0 or 1 for each tile; the 128 x 128 tiles on the diagonal of every node's adj_local block are 1.
All inputs are finite; a program needn't handle non-finite values.
Results may differ from a plain program's by a relative error of at most 0.0035.
Values may be sent and summed in bfloat16 or wider, within the bound.
No kernel may reach another device: no remote copies, remote signals or barrier semaphores. Data moves between devices by JAX's collectives and lax.ppermute only.
A program may use at most 128 MiB of HBM per device.

v0:
```python
import jax
import jax.numpy as jnp
from jax import lax
from jax.sharding import PartitionSpec as P

TILE = 128


def passed_along(x, axis, by):
    peers = lax.axis_size(axis)
    return lax.ppermute(x, axis, [(i, (i + by) % peers) for i in range(peers)])


def expand_tiles(adjacency, tile_flags):
    row_total, col_total = adjacency.shape
    blocked = adjacency.reshape(row_total // TILE, TILE, col_total // TILE, TILE)
    blocked = blocked * tile_flags.astype(jnp.bfloat16)[:, None, :, None]
    return blocked.reshape(row_total, col_total)


def shards(features, adj_local, adj_remote, tile_mask, w_self, w_neigh, out_bias):
    cycle_size = lax.axis_size("blk")
    node_count = adj_local.shape[0]
    halo_len = adj_remote.shape[1] // (cycle_size - 1)
    local_tiles = node_count // TILE
    live_local = expand_tiles(adj_local, tile_mask[:, :local_tiles])
    live_remote = expand_tiles(adj_remote, tile_mask[:, local_tiles:])
    degree = jnp.sum(live_local, axis=1, dtype=jnp.float32) + jnp.sum(
        live_remote, axis=1, dtype=jnp.float32
    )
    contract_first = (((0,), (0,)), ((), ()))
    contract_last = (((1,), (1,)), ((), ()))
    regrouped = lax.all_to_all(features, "feat", split_axis=1, concat_axis=0, tiled=True)
    own_feats = regrouped.reshape(regrouped.shape[0], node_count)
    summed = lax.dot_general(
        live_local, own_feats, contract_last, preferred_element_type=jnp.float32
    )
    halo_panel = own_feats[:, :halo_len]
    for offset in range(1, cycle_size):
        halo_panel = passed_along(halo_panel, "blk", 1)
        accumulate_weight_piece = live_remote[:, (offset - 1) * halo_len : offset * halo_len]
        summed = summed + lax.dot_general(
            accumulate_weight_piece, halo_panel, contract_last, preferred_element_type=jnp.float32
        )
    neigh_term = (
        jnp.dot(summed, w_neigh.astype(jnp.float32), precision=lax.Precision.HIGHEST)
        / jnp.sqrt(degree)[:, None]
    )
    self_term = lax.dot_general(
        own_feats, w_self, contract_first, preferred_element_type=jnp.float32
    )
    return jax.nn.relu(self_term + neigh_term + out_bias[None, :]).astype(jnp.bfloat16)


def solution(mesh):
    placed = (
        P("feat", None, "blk"),
        P(("feat", "blk"), None),
        P(("feat", "blk"), None),
        P(("feat", "blk"), None),
        P(),
        P(),
        P(),
    )
    return jax.shard_map(
        shards, mesh=mesh, in_specs=placed, out_specs=P(("feat", "blk"), None), check_vma=False
    )
```

profile of v0, /device:TPU:2, one launch (start us, length us, event | category | flops | bytes accessed | tf_op | source)
XLA Modules:
  0.0 152.3 jit_solution(7084699367673244187)
XLA Ops:
  0.0 0.0 copy-start
  0.0 2.8 %copy.8 = bf16[32,32,1024]{2,0,1:T(8,128)(2,1)S(1)} copy(bf16[32,32,1024]{2,1,0:T(8,128)(2,1)} %param.7) | data formatting | bytes 4194304 | tf_op args[0]
  2.8 0.0 copy-start.3
  2.8 62.0 %all_to_all.15 = bf16[32,32,1024]{2,0,1:T(8,128)(2,1)S(1)} all-to-all(bf16[32,32,1024]{2,0,1:T(8,128)(2,1)S(1)} %copy.8), channel_id=1, replica_groups=mesh['feat'=32,'blk'=8] {'feat'}, dimensions={1} | all-to-all | bytes 4194304 | tf_op jit(solution)/shard_map/all_to_all | solution.py:33
  64.8 0.9 slice.43
  65.6 0.0 collective-permute-start
  65.6 0.0 copy-done.3
  65.6 0.1 slice.33
  65.7 0.1 copy.9
  65.8 6.0 %copy.10 = bf16[1024,1792]{0,1:T(8,128)(2,1)} copy(bf16[1024,1792]{1,0:T(8,128)(2,1)} %param.9) | data formatting | bytes 7340032 | tf_op args[2]
  71.8 0.0 copy-start.1
  71.8 3.9 %collective-permute-done = bf16[1024,256]{1,0:T(8,128)(2,1)S(1)} collective-permute-done((bf16[1024,256]{1,0:T(8,128)(2,1)}, bf16[1024,256]{1,0:T(8,128)(2,1)S(1)}, u32[]{:S(2)}, u32[]{:S(2)}) %collective-permute-start) | collective-permute-done | bytes 524320 | tf_op jit(solution)/shard_map/ppermute | solution.py:11
  75.7 0.0 collective-permute-start.1
  75.7 0.5 mul.25
  76.2 0.0 copy-done.1
  76.2 0.0 copy-start.2
  76.2 2.2 %convert_reduce_fusion = (f32[1024]{0:T(1024)S(1)}, bf16[1024,1792]{0,1:T(8,128)(2,1)S(1)}) fusion(bf16[1024,1792]{0,1:T(8,128)(2,1)S(1)} %copy-done.1, bf16[224,8,8,128]{3,2,1,0:T(8,128)(2,1)S(1)} %bitcast.31), kind=kLoop, calls=%fused_computation | loop fusion | flops 5504000 | bytes 11014144 | tf_op jit(solution)/shard_map/reduce_sum | solution.py:28
  78.4 7.1 %collective-permute-done.1 = bf16[1024,256]{1,0:T(8,128)(2,1)S(1)} collective-permute-done((bf16[1024,256]{1,0:T(8,128)(2,1)S(1)}, bf16[1024,256]{1,0:T(8,128)(2,1)S(1)}, u32[]{:S(2)}, u32[]{:S(2)}) %collective-permute-start.1) | collective-permute-done | bytes 524320 | tf_op jit(solution)/shard_map/ppermute | solution.py:11
  85.5 0.0 collective-permute-start.2
  85.5 0.3 mul.22
  85.8 0.0 copy-done.2
  85.8 0.6 convert_reduce_fusion.1
  86.5 8.8 %collective-permute-done.2 = bf16[1024,256]{1,0:T(8,128)(2,1)S(1)} collective-permute-done((bf16[1024,256]{1,0:T(8,128)(2,1)S(1)}, bf16[1024,256]{1,0:T(8,128)(2,1)S(1)}, u32[]{:S(2)}, u32[]{:S(2)}) %collective-permute-start.2) | collective-permute-done | bytes 524320 | tf_op jit(solution)/shard_map/ppermute | solution.py:11
  95.3 0.0 collective-permute-start.3
  95.3 4.3 %fusion.14 = f32[1024,1024]{1,0:T(8,128)} fusion(bf16[1024,1024]{1,0:T(8,128)(2,1)S(1)} %bitcast.35, bf16[1024,1024]{1,0:T(8,128)(2,1)S(1)} %copy-done.2, bf16[128,8,8,128]{3,2,1,0:T(8,128)(2,1)S(1)} %bitcast.33), kind=kOutput, calls=%fused_computation.17 | convolution fusion | flops 2148532224 | bytes 10485760 | tf_op jit(solution)/shard_map/dot_general | solution.py:35
  99.6 5.5 %collective-permute-done.3 = bf16[1024,256]{1,0:T(8,128)(2,1)S(1)} collective-permute-done((bf16[1024,256]{1,0:T(8,128)(2,1)S(1)}, bf16[1024,256]{1,0:T(8,128)(2,1)S(1)}, u32[]{:S(2)}, u32[]{:S(2)}) %collective-permute-start.3) | collective-permute-done | bytes 524320 | tf_op jit(solution)/shard_map/ppermute | solution.py:11
  105.1 0.0 collective-permute-start.4
  105.1 0.8 fusion.27
  105.9 0.8 fusion.25
  106.6 8.3 %collective-permute-done.4 = bf16[1024,256]{1,0:T(8,128)(2,1)S(1)} collective-permute-done((bf16[1024,256]{1,0:T(8,128)(2,1)S(1)}, bf16[1024,256]{1,0:T(8,128)(2,1)S(1)}, u32[]{:S(2)}, u32[]{:S(2)}) %collective-permute-start.4) | collective-permute-done | bytes 524320 | tf_op jit(solution)/shard_map/ppermute | solution.py:11
  114.9 0.0 collective-permute-start.5
  114.9 0.8 fusion.23
  115.7 2.7 %fusion.21 = f32[1024,1024]{1,0:T(8,128)} fusion(bf16[1024,256]{1,0:T(8,128)(2,1)S(1)} %collective-permute-done.3, bf16[1024,1792]{0,1:T(8,128)(2,1)S(1)} %get-tuple-element.6), kind=kOutput, calls=%fused_computation.24 | convolution fusion | flops 536870912 | bytes 5242880 | tf_op jit(solution)/shard_map/dot_general | solution.py:42
  118.4 6.4 %collective-permute-done.5 = bf16[1024,256]{1,0:T(8,128)(2,1)S(1)} collective-permute-done((bf16[1024,256]{1,0:T(8,128)(2,1)S(1)}, bf16[1024,256]{1,0:T(8,128)(2,1)S(1)}, u32[]{:S(2)}, u32[]{:S(2)}) %collective-permute-start.5) | collective-permute-done | bytes 524320 | tf_op jit(solution)/shard_map/ppermute | solution.py:11
  124.7 0.0 collective-permute-start.6
  124.7 2.7 %fusion.19 = f32[1024,1024]{1,0:T(8,128)} fusion(bf16[1024,256]{1,0:T(8,128)(2,1)S(1)} %collective-permute-done.4, bf16[1024,1792]{0,1:T(8,128)(2,1)S(1)} %get-tuple-element.6), kind=kOutput, calls=%fused_computation.22 | convolution fusion | flops 536870912 | bytes 5242880 | tf_op jit(solution)/shard_map/dot_general | solution.py:42
  127.5 2.7 %fusion.17 = f32[1024,1024]{1,0:T(8,128)} fusion(bf16[1024,256]{1,0:T(8,128)(2,1)S(1)} %collective-permute-done.5, bf16[1024,1792]{0,1:T(8,128)(2,1)S(1)} %get-tuple-element.6), kind=kOutput, calls=%fused_computation.20 | convolution fusion | flops 536870912 | bytes 5242880 | tf_op jit(solution)/shard_map/dot_general | solution.py:42
  130.2 4.4 %collective-permute-done.6 = bf16[1024,256]{1,0:T(8,128)(2,1)S(1)} collective-permute-done((bf16[1024,256]{1,0:T(8,128)(2,1)S(1)}, bf16[1024,256]{1,0:T(8,128)(2,1)S(1)}, u32[]{:S(2)}, u32[]{:S(2)}) %collective-permute-start.6) | collective-permute-done | bytes 524320 | tf_op jit(solution)/shard_map/ppermute | solution.py:11
  134.6 2.7 %fusion.15 = f32[1024,1024]{1,0:T(8,128)} fusion(bf16[1024,256]{1,0:T(8,128)(2,1)S(1)} %collective-permute-done.6, bf16[1024,1792]{0,1:T(8,128)(2,1)S(1)} %get-tuple-element.6), kind=kOutput, calls=%fused_computation.18 | convolution fusion | flops 536870912 | bytes 5242880 | tf_op jit(solution)/shard_map/dot_general | solution.py:42
  137.3 0.0 copy-done
  137.3 0.0 copy-start.4
  137.3 0.0 copy-start.5
  137.3 12.3 %fusion.11 = f32[1024,256]{1,0:T(8,128)} fusion(bf16[1024,256]{1,0:T(8,128)(2,1)S(1)} %copy-done, f32[1024,1024]{1,0:T(8,128)} %fusion.15, f32[1024,1024]{1,0:T(8,128)} %fusion.17, f32[1024,1024]{1,0:T(8,128)} %fusion.19, f32[1024,1024]{1,0:T(8,128)} %fusion.21, f32[1024,1024]{1,0:T(8,128)S(1)} %fusion.23, f32[1024,1024]{1,0:T(8,128)S(1)} %fusion.25, ...), kind=kOutput, calls=%fused_computation.16 | convolution fusion | flops 3228827648 | bytes 35131392 | tf_op jit(solution)/shard_map/dot_general | solution.py:46
  149.5 0.0 copy-done.4
  149.5 0.0 copy-done.5
  149.5 2.8 %fusion.10 = bf16[1024,256]{1,0:T(8,128)(2,1)} fusion(f32[1024,256]{1,0:T(8,128)} %fusion.11, bf16[1024,1024]{1,0:T(8,128)(2,1)S(1)} %bitcast.36, bf16[1024,256]{1,0:T(8,128)(2,1)S(1)} %copy-done.4, f32[256]{0:T(256)S(1)} %copy-done.5), kind=kOutput, calls=%fused_computation.15 | convolution fusion | flops 537919488 | bytes 4195328 | tf_op jit(solution)/shard_map/dot_general | solution.py:49
  (2 shorter events, 0.0 us)
Async XLA Ops:
  0.0 137.3 %copy-start = (bf16[1024,256]{1,0:T(8,128)(2,1)S(1)}, bf16[1024,256]{1,0:T(8,128)(2,1)}, u32[]{:S(2)}) copy-start(bf16[1024,256]{1,0:T(8,128)(2,1)} %param.12) | copy-start | bytes 1572868
  2.8 62.8 %copy-start.3 = (s32[8,22]{1,0:T(8,128)S(1)}, s32[8,22]{1,0:T(8,128)}, u32[]{:S(2)}) copy-start(s32[8,22]{1,0:T(8,128)} %param.10) | copy-start | bytes 2116
  65.6 10.0 %collective-permute-start = (bf16[1024,256]{1,0:T(8,128)(2,1)}, bf16[1024,256]{1,0:T(8,128)(2,1)S(1)}, u32[]{:S(2)}, u32[]{:S(2)}) collective-permute-start(bf16[1024,256]{1,0:T(8,128)(2,1)} %slice.43), channel_id=1, source_target_pairs={{0,1},{1,2},{2,3},{3,4},{4,5},{5,6},{6,7},{7,0},{8,9},{9,10},{10,1... | collective-permute-start | bytes 1572872 | tf_op jit(solution)/shard_map/ppermute | solution.py:11
  71.8 4.4 %copy-start.1 = (bf16[1024,1792]{0,1:T(8,128)(2,1)S(1)}, bf16[1024,1792]{0,1:T(8,128)(2,1)}, u32[]{:S(2)}) copy-start(bf16[1024,1792]{0,1:T(8,128)(2,1)} %copy.10) | copy-start | bytes 11010052
  75.7 9.8 %collective-permute-start.1 = (bf16[1024,256]{1,0:T(8,128)(2,1)S(1)}, bf16[1024,256]{1,0:T(8,128)(2,1)S(1)}, u32[]{:S(2)}, u32[]{:S(2)}) collective-permute-start(bf16[1024,256]{1,0:T(8,128)(2,1)S(1)} %collective-permute-done), channel_id=1, source_target_pairs={{0,1},{1,2},{2,3},{3,4},{4,5},{5,6},{6,7},{7,0},{8,9},{9,10},{10,1... | collective-permute-start | bytes 1572872 | tf_op jit(solution)/shard_map/ppermute | solution.py:11
  76.2 9.6 %copy-start.2 = (bf16[1024,1024]{1,0:T(8,128)(2,1)S(1)}, bf16[1024,1024]{1,0:T(8,128)(2,1)}, u32[]{:S(2)}) copy-start(bf16[1024,1024]{1,0:T(8,128)(2,1)} %param.8) | copy-start | bytes 6291460
  85.5 9.8 %collective-permute-start.2 = (bf16[1024,256]{1,0:T(8,128)(2,1)S(1)}, bf16[1024,256]{1,0:T(8,128)(2,1)S(1)}, u32[]{:S(2)}, u32[]{:S(2)}) collective-permute-start(bf16[1024,256]{1,0:T(8,128)(2,1)S(1)} %collective-permute-done.1), channel_id=1, source_target_pairs={{0,1},{1,2},{2,3},{3,4},{4,5},{5,6},{6,7},{7,0},{8,9},{9,10},{10,1... | collective-permute-start | bytes 1572872 | tf_op jit(solution)/shard_map/ppermute | solution.py:11
  95.3 9.8 %collective-permute-start.3 = (bf16[1024,256]{1,0:T(8,128)(2,1)S(1)}, bf16[1024,256]{1,0:T(8,128)(2,1)S(1)}, u32[]{:S(2)}, u32[]{:S(2)}) collective-permute-start(bf16[1024,256]{1,0:T(8,128)(2,1)S(1)} %collective-permute-done.2), channel_id=1, source_target_pairs={{0,1},{1,2},{2,3},{3,4},{4,5},{5,6},{6,7},{7,0},{8,9},{9,10},{10,1... | collective-permute-start | bytes 1572872 | tf_op jit(solution)/shard_map/ppermute | solution.py:11
  105.1 9.8 %collective-permute-start.4 = (bf16[1024,256]{1,0:T(8,128)(2,1)S(1)}, bf16[1024,256]{1,0:T(8,128)(2,1)S(1)}, u32[]{:S(2)}, u32[]{:S(2)}) collective-permute-start(bf16[1024,256]{1,0:T(8,128)(2,1)S(1)} %collective-permute-done.3), channel_id=1, source_target_pairs={{0,1},{1,2},{2,3},{3,4},{4,5},{5,6},{6,7},{7,0},{8,9},{9,10},{10,1... | collective-permute-start | bytes 1572872 | tf_op jit(solution)/shard_map/ppermute | solution.py:11
  114.9 9.8 %collective-permute-start.5 = (bf16[1024,256]{1,0:T(8,128)(2,1)S(1)}, bf16[1024,256]{1,0:T(8,128)(2,1)S(1)}, u32[]{:S(2)}, u32[]{:S(2)}) collective-permute-start(bf16[1024,256]{1,0:T(8,128)(2,1)S(1)} %collective-permute-done.4), channel_id=1, source_target_pairs={{0,1},{1,2},{2,3},{3,4},{4,5},{5,6},{6,7},{7,0},{8,9},{9,10},{10,1... | collective-permute-start | bytes 1572872 | tf_op jit(solution)/shard_map/ppermute | solution.py:11
  124.7 9.8 %collective-permute-start.6 = (bf16[1024,256]{1,0:T(8,128)(2,1)S(1)}, bf16[1024,256]{1,0:T(8,128)(2,1)S(1)}, u32[]{:S(2)}, u32[]{:S(2)}) collective-permute-start(bf16[1024,256]{1,0:T(8,128)(2,1)S(1)} %collective-permute-done.5), channel_id=1, source_target_pairs={{0,1},{1,2},{2,3},{3,4},{4,5},{5,6},{6,7},{7,0},{8,9},{9,10},{10,1... | collective-permute-start | bytes 1572872 | tf_op jit(solution)/shard_map/ppermute | solution.py:11
  137.3 12.3 %copy-start.4 = (bf16[1024,256]{1,0:T(8,128)(2,1)S(1)}, bf16[1024,256]{1,0:T(8,128)(2,1)}, u32[]{:S(2)}) copy-start(bf16[1024,256]{1,0:T(8,128)(2,1)} %param.11) | copy-start | bytes 1572868
  137.3 12.3 %copy-start.5 = (f32[256]{0:T(256)S(1)}, f32[256]{0:T(256)}, u32[]{:S(2)}) copy-start(f32[256]{0:T(256)} %param.13) | copy-start | bytes 3076
where the time goes:
time: 153 us; the launch traced here: 152 us
  blocking collectives  62 us (41%)
  waiting for transfers between devices  44.3 us (29%)
  matrix products  32.5 us (21%)
  local copies, waits for them, and re-layouts  10.7 us (7%)
  other arithmetic  2.8 us (2%)
    all_to_all x1, blocking collectives, shards(): lax.all_to_all(features, 'feat', split_axis=1, concat_axis=0, tiled=True)  62 us
    ppermute x7, waiting for transfers between devices, passed_along(): return lax.ppermute(x, axis, [(i, (i + by) % peers) for i in range(peers)])  44.3 us
    dot_general x7, matrix products, shards(): lax.dot_general(accumulate_weight_piece, halo_panel, contract_last, prefe...  13.1 us
    dot_general x1, matrix products, shards(): jnp.dot(summed, w_neigh.astype(jnp.float32), precision=lax.Precision.HIGH...  12.3 us
    unnamed x14, local copies, waits for them, and re-layouts  8.79 us
    dot_general x1, matrix products, shards(): lax.dot_general(live_local, own_feats, contract_last, preferred_element_t...  4.3 us
  transfers between devices with their start and end apart: 7, of which 7 were waited for; matrix products, arithmetic and copies ran while one was open for 16% of the time, Pallas kernels for 0%

commit v1 on v0

v1 whole, which is shorter than its diff:
```python
import jax
import jax.numpy as jnp
from jax import lax
from jax.experimental import pallas as pl
from jax.experimental.pallas import tpu as pltpu
from jax.sharding import PartitionSpec as P

TILE = 128
NZ = 8
NX = 4
BF = jnp.bfloat16
F32 = jnp.float32


VM = pltpu.CompilerParams(vmem_limit_bytes=16 << 20)


def full(shape):
    return pl.BlockSpec(shape, lambda *_: (0,) * len(shape))


def feat_shift(dz, dx):
    return [
        (z * NX + x, (z + dz) % NZ * NX + (x + dx) % NX) for z in range(NZ) for x in range(NX)
    ]


def blk_shift(dy, dc):
    return [(y * 2 + c, (y + dy) % 4 * 2 + (c + dc) % 2) for y in range(4) for c in range(2)]


def head_kernel(me_ref, x_ref, *rest):
    outs, turned = rest[:-1], rest[-1]
    turned[...] = jnp.swapaxes(x_ref[...], 0, 1)
    z, x = me_ref[0] // NX, me_ref[0] % NX
    for dz in range(NZ):
        for j in range(NX):
            outs[dz][j] = turned[(z + dz) % NZ * NX + (x + j) % NX]


def split_head(me, features, halo):
    f, g, _ = features.shape
    return pl.pallas_call(
        head_kernel,
        grid_spec=pltpu.PrefetchScalarGridSpec(
            num_scalar_prefetch=1,
            grid=(1,),
            in_specs=[full((f, g, halo))],
            out_specs=[full((NX, f, halo))] * NZ,
            scratch_shapes=[pltpu.VMEM((g, f, halo), BF)],
        ),
        out_shape=[jax.ShapeDtypeStruct((NX, f, halo), BF)] * NZ,
        compiler_params=VM,
        name="split_head",
    )(me, features)


def tail_kernel(x_ref, o_ref):
    o_ref[...] = jnp.swapaxes(x_ref[...], 0, 1)


def split_tail(features, halo):
    f, g, n = features.shape
    return pl.pallas_call(
        tail_kernel,
        grid=(n // halo - 1,),
        in_specs=[pl.BlockSpec((f, g, halo), lambda i: (0, 0, i + 1))],
        out_specs=pl.BlockSpec((g, f, halo), lambda i: (0, 0, i)),
        out_shape=jax.ShapeDtypeStruct((g, f, n - halo), BF),
        compiler_params=VM,
        name="split_tail",
    )(features)


def regroup_kernel(*refs):
    ins, outs = refs[:NZ], refs[NZ:]
    f = ins[0].shape[1]
    for j in range(NX):
        for dz in range(NZ):
            outs[j][dz * f : (dz + 1) * f, :] = ins[dz][j]


def regroup(parts):
    _, f, halo = parts[0].shape
    return pl.pallas_call(
        regroup_kernel,
        grid=(1,),
        in_specs=[full((NX, f, halo))] * NZ,
        out_specs=[full((NZ * f, halo))] * NX,
        out_shape=[jax.ShapeDtypeStruct((NZ * f, halo), BF)] * NX,
        compiler_params=VM,
        name="regroup",
    )(*parts)


def halo_kernel(me_ref, a, b, c, d, ws_ref, wn_ref, self_ref, h_ref, w_ref):
    z, x = me_ref[0] // NX, me_ref[0] % NX
    rows, hid = a.shape[0], ws_ref.shape[1]
    f = rows // NZ
    total = None
    for j, part in enumerate((a, b, c, d)):
        for dz in range(NZ):
            src = ((z + (NZ - dz)) % NZ * NX + (x + (NX - j)) % NX) * f
            src = pl.multiple_of(src, f)
            w_ref[dz * f : (dz + 1) * f, :hid] = ws_ref[pl.ds(src, f), :]
            w_ref[dz * f : (dz + 1) * f, hid:] = wn_ref[pl.ds(src, f), :]
        one = lax.dot_general(
            part[...], w_ref[...], (((0,), (0,)), ((), ())), preferred_element_type=F32
        )
        total = one if total is None else total + one
    self_ref[...] = total[:, :hid]
    h = total[:, hid:]
    high = h.astype(BF)
    h_ref[:, :hid] = high
    h_ref[:, hid:] = (h - high.astype(F32)).astype(BF)


def halo_hidden(me, parts, w_self, w_neigh):
    rows, halo = parts[0].shape
    total, hid = w_self.shape
    return pl.pallas_call(
        halo_kernel,
        grid_spec=pltpu.PrefetchScalarGridSpec(
            num_scalar_prefetch=1,
            grid=(1,),
            in_specs=[full((rows, halo))] * NX + [full((total, hid))] * 2,
            out_specs=[full((halo, hid)), full((halo, 2 * hid))],
            scratch_shapes=[pltpu.VMEM((rows, 2 * hid), BF)],
        ),
        out_shape=[
            jax.ShapeDtypeStruct((halo, hid), F32),
            jax.ShapeDtypeStruct((halo, 2 * hid), BF),
        ],
        compiler_params=VM,
        name="halo_hidden",
    )(me, *parts, w_self, w_neigh)


def mask_kernel(mask_ref, al_ref, ar_ref, head_ref, tail_ref, remote_ref, scale_ref):
    row = pl.program_id(0)
    local, halo = al_ref.shape[1] // TILE, head_ref.shape[1]
    degree = jnp.zeros((TILE, TILE), F32)
    for t in range(local + ar_ref.shape[1] // TILE):
        flag = mask_ref[row, t].astype(F32)
        if t < local:
            at = t * TILE
            tile = al_ref[:, at : at + TILE].astype(F32) * flag
            if at < halo:
                head_ref[:, at : at + TILE] = tile.astype(BF)
            else:
                tail_ref[:, at - halo : at - halo + TILE] = tile.astype(BF)
        else:
            at = (t - local) * TILE
            tile = ar_ref[:, at : at + TILE].astype(F32) * flag
            remote_ref[:, at : at + TILE] = tile.astype(BF)
        degree = degree + tile
    whole = jnp.sum(degree, axis=1, keepdims=True)
    scale_ref[...] = jnp.broadcast_to(1.0 / jnp.sqrt(whole), (TILE, TILE))


def mask_tiles(tile_mask, adj_local, adj_remote, halo):
    rows, n = adj_local.shape
    r = adj_remote.shape[1]
    line = lambda w: pl.BlockSpec((TILE, w), lambda i, _: (i, 0))
    return pl.pallas_call(
        mask_kernel,
        grid_spec=pltpu.PrefetchScalarGridSpec(
            num_scalar_prefetch=1,
            grid=(rows // TILE,),
            in_specs=[line(n), line(r)],
            out_specs=[line(halo), line(n - halo), line(r), line(TILE)],
        ),
        out_shape=[
            jax.ShapeDtypeStruct((rows, halo), BF),
            jax.ShapeDtypeStruct((rows, n - halo), BF),
            jax.ShapeDtypeStruct((rows, r), BF),
            jax.ShapeDtypeStruct((rows, TILE), F32),
        ],
        compiler_params=VM,
        name="mask_tiles",
    )(tile_mask, adj_local, adj_remote)


def gather_kernel(core_ref, head_ref, remote_ref, *rest):
    slots, o_ref = rest[:-1], rest[-1]
    core = core_ref[0]
    halo, hid = slots[0].shape[0], o_ref.shape[1]
    total = jnp.dot(head_ref[...], slots[0][...], preferred_element_type=F32)
    for s in range(1, len(slots)):
        dy = s if s < 4 else s - 4
        column = 2 * dy - 1 if s < 4 else (2 * dy + 2 * core + 7) % 8 - 1
        at = column * halo if s < 4 else pl.multiple_of(column * halo, halo)
        total = total + jnp.dot(
            remote_ref[:, pl.ds(at, halo)], slots[s][...], preferred_element_type=F32
        )
    o_ref[...] = total[:, :hid] + total[:, hid:]


def gather_halo(core, head, remote, slots):
    rows, halo = head.shape
    hid = slots[0].shape[1] // 2
    block = 256
    line = lambda w: pl.BlockSpec((block, w), lambda i, _: (i, 0))
    return pl.pallas_call(
        gather_kernel,
        grid_spec=pltpu.PrefetchScalarGridSpec(
            num_scalar_prefetch=1,
            grid=(rows // block,),
            in_specs=[line(halo), line(remote.shape[1])] + [full((halo, 2 * hid))] * len(slots),
            out_specs=line(hid),
        ),
        out_shape=jax.ShapeDtypeStruct((rows, hid), F32),
        compiler_params=VM,
        name="gather_halo",
    )(core, head, remote, *slots)


def last_kernel(x_ref, ws_ref, wn_ref, tail_ref, acc_ref, scale_ref, sh_ref, bias_ref, o_ref, h_ref, s_ref):
    halo, hid = sh_ref.shape
    first = (((0,), (0,)), ((), ()))
    s_ref[:halo, :] = sh_ref[...]
    s_ref[halo:, :] = lax.dot_general(x_ref[...], ws_ref[...], first, preferred_element_type=F32)
    h = lax.dot_general(x_ref[...], wn_ref[...], first, preferred_element_type=F32)
    high = h.astype(BF)
    h_ref[:, :hid] = high
    h_ref[:, hid:] = (h - high.astype(F32)).astype(BF)
    rows, block = o_ref.shape[0], 256
    for i in range(0, rows, block):
        at = slice(i, i + block)
        both = jnp.dot(tail_ref[at, :], h_ref[...], preferred_element_type=F32)
        summed = acc_ref[at, :] + both[:, :hid] + both[:, hid:]
        scale = jnp.concatenate([scale_ref[at, :]] * (hid // TILE), axis=1)
        o_ref[at, :] = jnp.maximum(s_ref[at, :] + summed * scale + bias_ref[...], 0.0).astype(BF)


def last_step(x, w_self, w_neigh, tail, acc, scale, self_head, bias):
    rows, hid = acc.shape
    args = (x, w_self, w_neigh, tail, acc, scale, self_head, bias)
    return pl.pallas_call(
        last_kernel,
        grid=(1,),
        in_specs=[full(a.shape) for a in args],
        out_specs=full((rows, hid)),
        scratch_shapes=[pltpu.VMEM((x.shape[1], 2 * hid), BF), pltpu.VMEM((rows, hid), F32)],
        out_shape=jax.ShapeDtypeStruct((rows, hid), BF),
        compiler_params=VM,
        name="last_step",
    )(*args)


def shards(features, adj_local, adj_remote, tile_mask, w_self, w_neigh, out_bias):
    halo = adj_remote.shape[1] // (lax.axis_size("blk") - 1)
    me = lax.axis_index("feat").reshape(1)
    core = (lax.axis_index("blk") % 2).reshape(1)

    head = split_head(me, features, halo)
    landed = [head[0]]
    for dz in range(1, NZ):
        landed.append(lax.ppermute(head[dz], "feat", feat_shift(dz, 0)))
    rest = split_tail(features, halo)
    rest = lax.all_to_all(rest, "feat", split_axis=0, concat_axis=0, tiled=True)
    rest = rest.reshape(-1, rest.shape[-1])

    live_head, live_tail, live_remote, scale = mask_tiles(tile_mask, adj_local, adj_remote, halo)
    rows = regroup(landed)
    parts = [rows[0]] + [lax.ppermute(rows[j], "feat", feat_shift(0, j)) for j in (1, 2, 3)]
    self_head, h_head = halo_hidden(me, parts, w_self, w_neigh)
    same = [h_head] + [lax.ppermute(h_head, "blk", blk_shift(dy, 0)) for dy in (1, 2, 3)]
    other = [lax.ppermute(h, "blk", blk_shift(0, 1)) for h in same]
    acc = gather_halo(core, live_head, live_remote, same + other)
    return last_step(
        rest, w_self, w_neigh, live_tail, acc, scale, self_head, out_bias[None, :]
    )


def solution(mesh):
    placed = (
        P("feat", None, "blk"),
        P(("feat", "blk"), None),
        P(("feat", "blk"), None),
        P(("feat", "blk"), None),
        P(),
        P(),
        P(),
    )

    return jax.shard_map(
        shards, mesh=mesh, in_specs=placed, out_specs=P(("feat", "blk"), None), check_vma=False
    )
```

time: 153 us -> 110 us (0.72)
  blocking collectives: 62 us -> 0 us
  starting transfers between devices: 0.02 us -> 38.2 us
  matrix products: 32.5 us -> 0 us
  Pallas kernels: 0 us -> 13.5 us
  waiting for transfers between devices: 44.3 us -> 48.3 us
  other arithmetic: 2.8 us -> 0 us
  local copies, waits for them, and re-layouts: 10.7 us -> 8.15 us
    all_to_all x1 -> x0, blocking collectives: 62 us -> none  [shards(): lax.all_to_all(features, 'feat', split_axis=1, concat_axis=0, tiled=True)]
    dot_general x10 -> x0, matrix products: 32.5 us -> none  [the longest x7 13.1 us: shards(): lax.dot_general(accumulate_weight_piece, halo_panel, contract_last, prefe...]
    ppermute x7 -> x17, starting transfers between devices: 0.02 us -> 26.4 us  [the longest x7 15.3 us: shards(): landed.append(lax.ppermute(head[dz], 'feat', feat_shift(dz, 0)))]
    pallas_call x0 -> x7, Pallas kernels: none -> 13.5 us  [the longest x1 4.5 us: gather_halo(): pl.pallas_call(gather_kernel, grid_spec=pltpu.PrefetchScalarGridSpec(num_...]
    all_to_all x0 -> x1, starting transfers between devices: none -> 11.8 us  [shards(): rest = lax.all_to_all(rest, 'feat', split_axis=0, concat_axis=0, tiled=True)]
    ppermute x7 -> x17, waiting for transfers between devices: 44.3 us -> 48.3 us  [the longest x7 33.9 us: shards(): landed.append(lax.ppermute(head[dz], 'feat', feat_shift(dz, 0)))]
    reduce_sum x2 -> x0, other arithmetic: 2.79 us -> none  [the longest x1 2.18 us: shards(): jnp.sum(live_remote, axis=1, dtype=jnp.float32)]
    unnamed x14 -> x26, local copies, waits for them, and re-layouts: 8.79 us -> 8.15 us
  transfers between devices with their start and end apart: 7 -> 18, of which waited for: 7 -> 9; matrix products, arithmetic and copies ran while one was open for 16% -> 0% of each run, Pallas kernels for 0% -> 8%
where the time goes in v1:
time: 110 us; the launch traced here: 108 us
  waiting for transfers between devices  48.3 us (44%)
  starting transfers between devices  38.2 us (35%)
  Pallas kernels  13.5 us (12%)
  local copies, waits for them, and re-layouts  8.15 us (7%)
    ppermute x7, waiting for transfers between devices, shards(): landed.append(lax.ppermute(head[dz], 'feat', feat_shift(dz, 0)))  33.9 us
    ppermute x7, starting transfers between devices, shards(): landed.append(lax.ppermute(head[dz], 'feat', feat_shift(dz, 0)))  15.3 us
    all_to_all x1, starting transfers between devices, shards(): rest = lax.all_to_all(rest, 'feat', split_axis=0, concat_axis=0, tiled=True)  11.8 us
    ppermute x3, waiting for transfers between devices, shards(): lax.ppermute(h_head, 'blk', blk_shift(dy, 0))  9.44 us
    unnamed x26, local copies, waits for them, and re-layouts  8.15 us
    ppermute x3, starting transfers between devices, shards(): lax.ppermute(h_head, 'blk', blk_shift(dy, 0))  5.82 us
    ppermute x3, waiting for transfers between devices, shards(): lax.ppermute(rows[j], 'feat', feat_shift(0, j))  4.96 us
    ppermute x3, starting transfers between devices, shards(): lax.ppermute(rows[j], 'feat', feat_shift(0, j))  4.76 us
  transfers between devices with their start and end apart: 18, of which 9 were waited for; matrix products, arithmetic and copies ran while one was open for 0% of the time, Pallas kernels for 8%

profile of v1, /device:TPU:2, one launch (start us, length us, event | category | flops | bytes accessed | tf_op | source)
XLA Modules:
  0.0 108.4 jit_solution(5142551731305381539)
XLA Ops:
  0.0 1.6 %copy-done = bf16[32,32,1024]{2,1,0:T(8,128)(2,1)S(1)} copy-done((bf16[32,32,1024]{2,1,0:T(8,128)(2,1)S(1)}, bf16[32,32,1024]{2,1,0:T(8,128)(2,1)}, u32[]{:S(2)}) %copy-start) | copy-done | bytes 2097176
  1.6 0.8 split_tail.1
  2.4 1.1 %copy-done.2 = bf16[32,32,768]{2,1,0:T(8,128)(2,1)} copy-done((bf16[32,32,768]{2,1,0:T(8,128)(2,1)}, bf16[32,32,768]{2,1,0:T(8,128)(2,1)S(1)}, u32[]{:S(2)}) %copy-start.2) | copy-done | bytes 1572888
  3.5 11.8 %all-to-all-start = ((bf16[32,32,768]{2,1,0:T(8,128)(2,1)}), bf16[32,32,768]{2,1,0:T(8,128)(2,1)}, u32[]{:S(2)}, u32[]{:S(2)}) async-start(bf16[32,32,768]{2,1,0:T(8,128)(2,1)} %copy-done.2), calls=%async_computation | async-start | bytes 3145728 | tf_op jit(solution)/shard_map/all_to_all | solution.py:261
  15.3 0.0 copy-start.5
  15.3 0.0 copy-start.6
  15.4 0.0 copy-start.11
  15.4 0.2 split_head.1
  15.6 0.0 copy-start.4
  15.6 1.5 %collective-permute-start = (bf16[4,32,256]{2,1,0:T(8,128)(2,1)S(1)}, bf16[4,32,256]{2,1,0:T(8,128)(2,1)S(1)}, u32[]{:S(2)}, u32[]{:S(2)}) collective-permute-start(bf16[4,32,256]{2,1,0:T(8,128)(2,1)S(1)} %get-tuple-element.27), channel_id=1, source_target_pairs={{0,32},{8,40},{16,48},{24,56},{32,64},{40,72},{48,80},{56,88},{64,... | collective-permute-start | bytes 196616 | tf_op jit(solution)/shard_map/ppermute | solution.py:259
  17.1 2.4 %collective-permute-start.1 = (bf16[4,32,256]{2,1,0:T(8,128)(2,1)S(1)}, bf16[4,32,256]{2,1,0:T(8,128)(2,1)S(1)}, u32[]{:S(2)}, u32[]{:S(2)}) collective-permute-start(bf16[4,32,256]{2,1,0:T(8,128)(2,1)S(1)} %get-tuple-element.28), channel_id=1, source_target_pairs={{0,64},{8,72},{16,80},{24,88},{32,96},{40,104},{48,112},{56,120},{... | collective-permute-start | bytes 196616 | tf_op jit(solution)/shard_map/ppermute | solution.py:259
  19.5 2.7 %collective-permute-start.2 = (bf16[4,32,256]{2,1,0:T(8,128)(2,1)S(1)}, bf16[4,32,256]{2,1,0:T(8,128)(2,1)S(1)}, u32[]{:S(2)}, u32[]{:S(2)}) collective-permute-start(bf16[4,32,256]{2,1,0:T(8,128)(2,1)S(1)} %get-tuple-element.29), channel_id=1, source_target_pairs={{0,96},{8,104},{16,112},{24,120},{32,128},{40,136},{48,144},{56,15... | collective-permute-start | bytes 196616 | tf_op jit(solution)/shard_map/ppermute | solution.py:259
  22.2 2.3 %collective-permute-start.3 = (bf16[4,32,256]{2,1,0:T(8,128)(2,1)S(1)}, bf16[4,32,256]{2,1,0:T(8,128)(2,1)S(1)}, u32[]{:S(2)}, u32[]{:S(2)}) collective-permute-start(bf16[4,32,256]{2,1,0:T(8,128)(2,1)S(1)} %get-tuple-element.30), channel_id=1, source_target_pairs={{0,128},{8,136},{16,144},{24,152},{32,160},{40,168},{48,176},{56,1... | collective-permute-start | bytes 196616 | tf_op jit(solution)/shard_map/ppermute | solution.py:259
  24.5 2.8 %collective-permute-start.4 = (bf16[4,32,256]{2,1,0:T(8,128)(2,1)S(1)}, bf16[4,32,256]{2,1,0:T(8,128)(2,1)S(1)}, u32[]{:S(2)}, u32[]{:S(2)}) collective-permute-start(bf16[4,32,256]{2,1,0:T(8,128)(2,1)S(1)} %get-tuple-element.31), channel_id=1, source_target_pairs={{0,160},{8,168},{16,176},{24,184},{32,192},{40,200},{48,208},{56,2... | collective-permute-start | bytes 196616 | tf_op jit(solution)/shard_map/ppermute | solution.py:259
  27.3 27.3 %collective-permute-done.refs_1_ = bf16[4,32,256]{2,1,0:T(8,128)(2,1)S(1)} collective-permute-done((bf16[4,32,256]{2,1,0:T(8,128)(2,1)S(1)}, bf16[4,32,256]{2,1,0:T(8,128)(2,1)S(1)}, u32[]{:S(2)}, u32[]{:S(2)}) %collective-permute-start) | collective-permute-done | bytes 65568 | tf_op jit(solution)/shard_map/ppermute | solution.py:259
  54.5 2.4 %collective-permute-start.5 = (bf16[4,32,256]{2,1,0:T(8,128)(2,1)S(1)}, bf16[4,32,256]{2,1,0:T(8,128)(2,1)S(1)}, u32[]{:S(2)}, u32[]{:S(2)}) collective-permute-start(bf16[4,32,256]{2,1,0:T(8,128)(2,1)S(1)} %get-tuple-element.32), channel_id=1, source_target_pairs={{0,192},{8,200},{16,208},{24,216},{32,224},{40,232},{48,240},{56,2... | collective-permute-start | bytes 196616 | tf_op jit(solution)/shard_map/ppermute | solution.py:259
  56.9 2.0 %collective-permute-done.1.refs_2_ = bf16[4,32,256]{2,1,0:T(8,128)(2,1)S(1)} collective-permute-done((bf16[4,32,256]{2,1,0:T(8,128)(2,1)S(1)}, bf16[4,32,256]{2,1,0:T(8,128)(2,1)S(1)}, u32[]{:S(2)}, u32[]{:S(2)}) %collective-permute-start.1) | collective-permute-done | bytes 65568 | tf_op jit(solution)/shard_map/ppermute | solution.py:259
  59.0 1.2 %collective-permute-start.6 = (bf16[4,32,256]{2,1,0:T(8,128)(2,1)S(1)}, bf16[4,32,256]{2,1,0:T(8,128)(2,1)S(1)}, u32[]{:S(2)}, u32[]{:S(2)}) collective-permute-start(bf16[4,32,256]{2,1,0:T(8,128)(2,1)S(1)} %get-tuple-element.33), channel_id=1, source_target_pairs={{0,224},{8,232},{16,240},{24,248},{32,0},{40,8},{48,16},{56,24},{6... | collective-permute-start | bytes 196616 | tf_op jit(solution)/shard_map/ppermute | solution.py:259
  60.2 0.8 collective-permute-done.2.refs_3_
  61.0 3.8 %collective-permute-done.3.refs_4_ = bf16[4,32,256]{2,1,0:T(8,128)(2,1)S(1)} collective-permute-done((bf16[4,32,256]{2,1,0:T(8,128)(2,1)S(1)}, bf16[4,32,256]{2,1,0:T(8,128)(2,1)S(1)}, u32[]{:S(2)}, u32[]{:S(2)}) %collective-permute-start.3) | collective-permute-done | bytes 65568 | tf_op jit(solution)/shard_map/ppermute | solution.py:259
  64.8 0.0 collective-permute-done.4.refs_5_
  64.8 0.0 collective-permute-done.5.refs_6_
  64.8 0.0 collective-permute-done.6.refs_7_
  64.9 1.5 %collective-permute-start.7 = (bf16[256,256]{1,0:T(8,128)(2,1)S(1)}, bf16[256,256]{1,0:T(8,128)(2,1)S(1)}, u32[]{:S(2)}, u32[]{:S(2)}) collective-permute-start(bf16[256,256]{1,0:T(8,128)(2,1)S(1)} %get-tuple-element.35), channel_id=1, source_target_pairs={{0,8},{8,16},{16,24},{24,0},{32,40},{40,48},{48,56},{56,32},{64,72... | collective-permute-start | bytes 393224 | tf_op jit(solution)/shard_map/ppermute | solution.py:266
  66.4 0.9 collective-permute-start.8
  67.3 2.3 %collective-permute-start.9 = (bf16[256,256]{1,0:T(8,128)(2,1)S(1)}, bf16[256,256]{1,0:T(8,128)(2,1)S(1)}, u32[]{:S(2)}, u32[]{:S(2)}) collective-permute-start(bf16[256,256]{1,0:T(8,128)(2,1)S(1)} %get-tuple-element.37), channel_id=1, source_target_pairs={{0,24},{8,0},{16,8},{24,16},{32,56},{40,32},{48,40},{56,48},{64,88... | collective-permute-start | bytes 393224 | tf_op jit(solution)/shard_map/ppermute | solution.py:266
  69.6 0.7 collective-permute-done.7.b
  70.3 3.7 %collective-permute-done.8.c = bf16[256,256]{1,0:T(8,128)(2,1)S(1)} collective-permute-done((bf16[256,256]{1,0:T(8,128)(2,1)S(1)}, bf16[256,256]{1,0:T(8,128)(2,1)S(1)}, u32[]{:S(2)}, u32[]{:S(2)}) %collective-permute-start.8) | collective-permute-done | bytes 131104 | tf_op jit(solution)/shard_map/ppermute | solution.py:266
  74.0 0.6 collective-permute-done.9.d
  74.6 1.2 %halo_hidden.1 = (f32[256,256]{1,0:T(8,128)S(1)}, bf16[256,512]{1,0:T(8,128)(2,1)}) custom-call(s32[1]{0:T(128)} %bitcast.2.me_ref, bf16[256,256]{1,0:T(8,128)(2,1)S(1)} %get-tuple-element.34.a, bf16[256,256]{1,0:T(8,128)(2,1)S(1)} %collective-permute-done.7.b, bf16[256,256]{1,0:T(8,128)(2,1)S(1)} %collective-permute-done.8.c, ...), custom_call_target="tpu_custom_call" | custom-call | tf_op jit(solution)/shard_map/halo_hidden/pallas_call | solution.py:121
  75.8 1.6 %collective-permute-start.10 = (bf16[256,512]{1,0:T(8,128)(2,1)}, bf16[256,512]{1,0:T(8,128)(2,1)}, u32[]{:S(2)}, u32[]{:S(2)}) collective-permute-start(bf16[256,512]{1,0:T(8,128)(2,1)} %get-tuple-element.38.rest_0_), channel_id=1, source_target_pairs={{0,2},{1,3},{2,4},{3,5},{4,6},{5,7},{6,0},{7,1},{8,10},{9,11},{10,... | collective-permute-start | bytes 786440 | tf_op jit(solution)/shard_map/ppermute | solution.py:268
  77.3 2.9 %collective-permute-start.11 = (bf16[256,512]{1,0:T(8,128)(2,1)}, bf16[256,512]{1,0:T(8,128)(2,1)}, u32[]{:S(2)}, u32[]{:S(2)}) collective-permute-start(bf16[256,512]{1,0:T(8,128)(2,1)} %get-tuple-element.38.rest_0_), channel_id=1, source_target_pairs={{0,4},{1,5},{2,6},{3,7},{4,0},{5,1},{6,2},{7,3},{8,12},{9,13},{10,... | collective-permute-start | bytes 786440 | tf_op jit(solution)/shard_map/ppermute | solution.py:268
  80.2 1.3 %collective-permute-start.12 = (bf16[256,512]{1,0:T(8,128)(2,1)}, bf16[256,512]{1,0:T(8,128)(2,1)}, u32[]{:S(2)}, u32[]{:S(2)}) collective-permute-start(bf16[256,512]{1,0:T(8,128)(2,1)} %get-tuple-element.38.rest_0_), channel_id=1, source_target_pairs={{0,6},{1,7},{2,0},{3,1},{4,2},{5,3},{6,4},{7,5},{8,14},{9,15},{10,... | collective-permute-start | bytes 786440 | tf_op jit(solution)/shard_map/ppermute | solution.py:268
  81.6 0.0 collective-permute-start.13
  81.6 3.7 %collective-permute-done.10.rest_1_ = bf16[256,512]{1,0:T(8,128)(2,1)} collective-permute-done((bf16[256,512]{1,0:T(8,128)(2,1)}, bf16[256,512]{1,0:T(8,128)(2,1)}, u32[]{:S(2)}, u32[]{:S(2)}) %collective-permute-start.10) | collective-permute-done | bytes 262176 | tf_op jit(solution)/shard_map/ppermute | solution.py:268
  85.4 5.7 %collective-permute-done.11.rest_2_ = bf16[256,512]{1,0:T(8,128)(2,1)} collective-permute-done((bf16[256,512]{1,0:T(8,128)(2,1)}, bf16[256,512]{1,0:T(8,128)(2,1)}, u32[]{:S(2)}, u32[]{:S(2)}) %collective-permute-start.11) | collective-permute-done | bytes 262176 | tf_op jit(solution)/shard_map/ppermute | solution.py:268
  91.0 0.0 collective-permute-start.15
  91.0 0.0 collective-permute-done.12.rest_3_
  91.1 0.5 collective-permute-start.16
  91.6 2.0 %copy-done.3 = bf16[1024,1792]{1,0:T(8,128)(2,1)S(1)} copy-done((bf16[1024,1792]{1,0:T(8,128)(2,1)S(1)}, bf16[1024,1792]{1,0:T(8,128)(2,1)}, u32[]{:S(2)}) %copy-start.3) | copy-done | bytes 3670040
  93.6 2.8 %mask_tiles.1 = (bf16[1024,256]{1,0:T(8,128)(2,1)S(1)}, bf16[1024,768]{1,0:T(8,128)(2,1)S(1)}, bf16[1024,1792]{1,0:T(8,128)(2,1)S(1)}, f32[1024,128]{1,0:T(8,128)S(1)}) custom-call(s32[8,22]{1,0:T(8,128)S(1)} %copy-done.11, bf16[1024,1024]{1,0:T(8,128)(2,1)S(1)} %copy-done.4, bf16[1024,1792]{1,0:T(8,128)(2,1)S(1)} %copy-done.3), custom_call_target="tpu_custom_call" | custom-call | tf_op jit(solution)/shard_map/mask_tiles/pallas_call | solution.py:165
  96.4 1.1 %copy-done.7 = bf16[1024,768]{1,0:T(8,128)(2,1)} copy-done((bf16[1024,768]{1,0:T(8,128)(2,1)}, bf16[1024,768]{1,0:T(8,128)(2,1)S(1)}, u32[]{:S(2)}) %copy-start.7) | copy-done | bytes 1572888
  97.6 0.8 copy-done.9
  98.4 0.0 copy-start.10
  98.4 0.0 copy-start.12
  98.4 4.5 %gather_halo.1.acc_ref = f32[1024,256]{1,0:T(8,128)S(1)} custom-call(s32[1]{0:T(128)} %bitcast.1.core_ref, bf16[1024,256]{1,0:T(8,128)(2,1)S(1)} %get-tuple-element.24.head_ref, bf16[1024,1792]{1,0:T(8,128)(2,1)S(1)} %get-tuple-element.25.remote_ref, bf16[256,512]{1,0:T(8,128)(2,1)} %get-tuple-element.38.rest_0_, ...), custom_call_target="tpu_custom_call" | custom-call | tf_op jit(solution)/shard_map/gather_halo/pallas_call | solution.py:204
  102.9 1.4 %copy-done.8 = bf16[1024,768]{1,0:T(8,128)(2,1)S(1)} copy-done((bf16[1024,768]{1,0:T(8,128)(2,1)S(1)}, bf16[1024,768]{1,0:T(8,128)(2,1)}, u32[]{:S(2)}) %copy-start.8) | copy-done | bytes 1572888
  104.3 4.1 %last_step.1 = bf16[1024,256]{1,0:T(8,128)(2,1)} custom-call(bf16[1024,768]{1,0:T(8,128)(2,1)} %bitcast.x_ref, bf16[1024,256]{1,0:T(8,128)(2,1)S(1)} %copy-done.5, bf16[1024,256]{1,0:T(8,128)(2,1)S(1)} %copy-done.6, bf16[1024,768]{1,0:T(8,128)(2,1)S(1)} %copy-done.8, f32[1024,256]{1,0:T(8,128)S(1)} %gather_halo.1.acc_ref, f32[1024,128]{1,0:T(8,128)S(1)} %copy-done.10, ...), custom_call_target="tpu_custom_call" | custom-call | tf_op jit(solution)/shard_map/last_step/pallas_call | solution.py:239
  (21 shorter events, 0.1 us)
Async XLA Ops:
  0.0 1.6 %copy-start = (bf16[32,32,1024]{2,1,0:T(8,128)(2,1)S(1)}, bf16[32,32,1024]{2,1,0:T(8,128)(2,1)}, u32[]{:S(2)}) copy-start(bf16[32,32,1024]{2,1,0:T(8,128)(2,1)} %x_ref.3) | copy-start | bytes 6291460
  2.4 1.1 %copy-start.2 = (bf16[32,32,768]{2,1,0:T(8,128)(2,1)}, bf16[32,32,768]{2,1,0:T(8,128)(2,1)S(1)}, u32[]{:S(2)}) copy-start(bf16[32,32,768]{2,1,0:T(8,128)(2,1)S(1)} %split_tail.1) | copy-start | bytes 4718596
  3.5 11.8 %copy-start.1 = (bf16[32,32,1024]{2,1,0:T(8,128)(2,1)S(1)}, bf16[32,32,1024]{2,1,0:T(8,128)(2,1)}, u32[]{:S(2)}) copy-start(bf16[32,32,1024]{2,1,0:T(8,128)(2,1)} %x_ref.3) | copy-start | bytes 6291460
  3.5 99.4 %all-to-all-start = ((bf16[32,32,768]{2,1,0:T(8,128)(2,1)}), bf16[32,32,768]{2,1,0:T(8,128)(2,1)}, u32[]{:S(2)}, u32[]{:S(2)}) async-start(bf16[32,32,768]{2,1,0:T(8,128)(2,1)} %copy-done.2), calls=%async_computation | async-start | bytes 3145728 | tf_op jit(solution)/shard_map/all_to_all | solution.py:261
  15.3 59.3 %copy-start.5 = (bf16[1024,256]{1,0:T(8,128)(2,1)S(1)}, bf16[1024,256]{1,0:T(8,128)(2,1)}, u32[]{:S(2)}) copy-start(bf16[1024,256]{1,0:T(8,128)(2,1)} %ws_ref.3) | copy-start | bytes 1572868
  15.3 59.3 %copy-start.6 = (bf16[1024,256]{1,0:T(8,128)(2,1)S(1)}, bf16[1024,256]{1,0:T(8,128)(2,1)}, u32[]{:S(2)}) copy-start(bf16[1024,256]{1,0:T(8,128)(2,1)} %wn_ref.3) | copy-start | bytes 1572868
  15.4 76.2 %copy-start.11 = (s32[8,22]{1,0:T(8,128)S(1)}, s32[8,22]{1,0:T(8,128)}, u32[]{:S(2)}) copy-start(s32[8,22]{1,0:T(8,128)} %mask_ref.1) | copy-start | bytes 2116
  15.6 76.0 %copy-start.4 = (bf16[1024,1024]{1,0:T(8,128)(2,1)S(1)}, bf16[1024,1024]{1,0:T(8,128)(2,1)}, u32[]{:S(2)}) copy-start(bf16[1024,1024]{1,0:T(8,128)(2,1)} %al_ref.1) | copy-start | bytes 6291460
  15.6 38.9 %collective-permute-start = (bf16[4,32,256]{2,1,0:T(8,128)(2,1)S(1)}, bf16[4,32,256]{2,1,0:T(8,128)(2,1)S(1)}, u32[]{:S(2)}, u32[]{:S(2)}) collective-permute-start(bf16[4,32,256]{2,1,0:T(8,128)(2,1)S(1)} %get-tuple-element.27), channel_id=1, source_target_pairs={{0,32},{8,40},{16,48},{24,56},{32,64},{40,72},{48,80},{56,88},{64,... | collective-permute-start | bytes 196616 | tf_op jit(solution)/shard_map/ppermute | solution.py:259
  17.1 41.8 %collective-permute-start.1 = (bf16[4,32,256]{2,1,0:T(8,128)(2,1)S(1)}, bf16[4,32,256]{2,1,0:T(8,128)(2,1)S(1)}, u32[]{:S(2)}, u32[]{:S(2)}) collective-permute-start(bf16[4,32,256]{2,1,0:T(8,128)(2,1)S(1)} %get-tuple-element.28), channel_id=1, source_target_pairs={{0,64},{8,72},{16,80},{24,88},{32,96},{40,104},{48,112},{56,120},{... | collective-permute-start | bytes 196616 | tf_op jit(solution)/shard_map/ppermute | solution.py:259
  19.5 41.5 %collective-permute-start.2 = (bf16[4,32,256]{2,1,0:T(8,128)(2,1)S(1)}, bf16[4,32,256]{2,1,0:T(8,128)(2,1)S(1)}, u32[]{:S(2)}, u32[]{:S(2)}) collective-permute-start(bf16[4,32,256]{2,1,0:T(8,128)(2,1)S(1)} %get-tuple-element.29), channel_id=1, source_target_pairs={{0,96},{8,104},{16,112},{24,120},{32,128},{40,136},{48,144},{56,15... | collective-permute-start | bytes 196616 | tf_op jit(solution)/shard_map/ppermute | solution.py:259
  22.2 42.6 %collective-permute-start.3 = (bf16[4,32,256]{2,1,0:T(8,128)(2,1)S(1)}, bf16[4,32,256]{2,1,0:T(8,128)(2,1)S(1)}, u32[]{:S(2)}, u32[]{:S(2)}) collective-permute-start(bf16[4,32,256]{2,1,0:T(8,128)(2,1)S(1)} %get-tuple-element.30), channel_id=1, source_target_pairs={{0,128},{8,136},{16,144},{24,152},{32,160},{40,168},{48,176},{56,1... | collective-permute-start | bytes 196616 | tf_op jit(solution)/shard_map/ppermute | solution.py:259
  24.5 40.3 %collective-permute-start.4 = (bf16[4,32,256]{2,1,0:T(8,128)(2,1)S(1)}, bf16[4,32,256]{2,1,0:T(8,128)(2,1)S(1)}, u32[]{:S(2)}, u32[]{:S(2)}) collective-permute-start(bf16[4,32,256]{2,1,0:T(8,128)(2,1)S(1)} %get-tuple-element.31), channel_id=1, source_target_pairs={{0,160},{8,168},{16,176},{24,184},{32,192},{40,200},{48,208},{56,2... | collective-permute-start | bytes 196616 | tf_op jit(solution)/shard_map/ppermute | solution.py:259
  54.5 10.3 %collective-permute-start.5 = (bf16[4,32,256]{2,1,0:T(8,128)(2,1)S(1)}, bf16[4,32,256]{2,1,0:T(8,128)(2,1)S(1)}, u32[]{:S(2)}, u32[]{:S(2)}) collective-permute-start(bf16[4,32,256]{2,1,0:T(8,128)(2,1)S(1)} %get-tuple-element.32), channel_id=1, source_target_pairs={{0,192},{8,200},{16,208},{24,216},{32,224},{40,232},{48,240},{56,2... | collective-permute-start | bytes 196616 | tf_op jit(solution)/shard_map/ppermute | solution.py:259
  59.0 5.9 %collective-permute-start.6 = (bf16[4,32,256]{2,1,0:T(8,128)(2,1)S(1)}, bf16[4,32,256]{2,1,0:T(8,128)(2,1)S(1)}, u32[]{:S(2)}, u32[]{:S(2)}) collective-permute-start(bf16[4,32,256]{2,1,0:T(8,128)(2,1)S(1)} %get-tuple-element.33), channel_id=1, source_target_pairs={{0,224},{8,232},{16,240},{24,248},{32,0},{40,8},{48,16},{56,24},{6... | collective-permute-start | bytes 196616 | tf_op jit(solution)/shard_map/ppermute | solution.py:259
  64.9 5.5 %collective-permute-start.7 = (bf16[256,256]{1,0:T(8,128)(2,1)S(1)}, bf16[256,256]{1,0:T(8,128)(2,1)S(1)}, u32[]{:S(2)}, u32[]{:S(2)}) collective-permute-start(bf16[256,256]{1,0:T(8,128)(2,1)S(1)} %get-tuple-element.35), channel_id=1, source_target_pairs={{0,8},{8,16},{16,24},{24,0},{32,40},{40,48},{48,56},{56,32},{64,72... | collective-permute-start | bytes 393224 | tf_op jit(solution)/shard_map/ppermute | solution.py:266
  66.4 7.7 %collective-permute-start.8 = (bf16[256,256]{1,0:T(8,128)(2,1)S(1)}, bf16[256,256]{1,0:T(8,128)(2,1)S(1)}, u32[]{:S(2)}, u32[]{:S(2)}) collective-permute-start(bf16[256,256]{1,0:T(8,128)(2,1)S(1)} %get-tuple-element.36), channel_id=1, source_target_pairs={{0,16},{8,24},{16,0},{24,8},{32,48},{40,56},{48,32},{56,40},{64,80... | collective-permute-start | bytes 393224 | tf_op jit(solution)/shard_map/ppermute | solution.py:266
  67.3 7.3 %collective-permute-start.9 = (bf16[256,256]{1,0:T(8,128)(2,1)S(1)}, bf16[256,256]{1,0:T(8,128)(2,1)S(1)}, u32[]{:S(2)}, u32[]{:S(2)}) collective-permute-start(bf16[256,256]{1,0:T(8,128)(2,1)S(1)} %get-tuple-element.37), channel_id=1, source_target_pairs={{0,24},{8,0},{16,8},{24,16},{32,56},{40,32},{48,40},{56,48},{64,88... | collective-permute-start | bytes 393224 | tf_op jit(solution)/shard_map/ppermute | solution.py:266
  75.8 9.6 %collective-permute-start.10 = (bf16[256,512]{1,0:T(8,128)(2,1)}, bf16[256,512]{1,0:T(8,128)(2,1)}, u32[]{:S(2)}, u32[]{:S(2)}) collective-permute-start(bf16[256,512]{1,0:T(8,128)(2,1)} %get-tuple-element.38.rest_0_), channel_id=1, source_target_pairs={{0,2},{1,3},{2,4},{3,5},{4,6},{5,7},{6,0},{7,1},{8,10},{9,11},{10,... | collective-permute-start | bytes 786440 | tf_op jit(solution)/shard_map/ppermute | solution.py:268
  77.3 13.7 %collective-permute-start.11 = (bf16[256,512]{1,0:T(8,128)(2,1)}, bf16[256,512]{1,0:T(8,128)(2,1)}, u32[]{:S(2)}, u32[]{:S(2)}) collective-permute-start(bf16[256,512]{1,0:T(8,128)(2,1)} %get-tuple-element.38.rest_0_), channel_id=1, source_target_pairs={{0,4},{1,5},{2,6},{3,7},{4,0},{5,1},{6,2},{7,3},{8,12},{9,13},{10,... | collective-permute-start | bytes 786440 | tf_op jit(solution)/shard_map/ppermute | solution.py:268
  80.2 10.8 %collective-permute-start.12 = (bf16[256,512]{1,0:T(8,128)(2,1)}, bf16[256,512]{1,0:T(8,128)(2,1)}, u32[]{:S(2)}, u32[]{:S(2)}) collective-permute-start(bf16[256,512]{1,0:T(8,128)(2,1)} %get-tuple-element.38.rest_0_), channel_id=1, source_target_pairs={{0,6},{1,7},{2,0},{3,1},{4,2},{5,3},{6,4},{7,5},{8,14},{9,15},{10,... | collective-permute-start | bytes 786440 | tf_op jit(solution)/shard_map/ppermute | solution.py:268
  81.6 16.8 %collective-permute-start.13 = (bf16[256,512]{1,0:T(8,128)(2,1)}, bf16[256,512]{1,0:T(8,128)(2,1)}, u32[]{:S(2)}, u32[]{:S(2)}) collective-permute-start(bf16[256,512]{1,0:T(8,128)(2,1)} %get-tuple-element.38.rest_0_), channel_id=1, source_target_pairs={{0,1},{1,0},{2,3},{3,2},{4,5},{5,4},{6,7},{7,6},{8,9},{9,8},{10,11... | collective-permute-start | bytes 786440 | tf_op jit(solution)/shard_map/ppermute | solution.py:269
  85.3 13.0 %collective-permute-start.14 = (bf16[256,512]{1,0:T(8,128)(2,1)}, bf16[256,512]{1,0:T(8,128)(2,1)}, u32[]{:S(2)}, u32[]{:S(2)}) collective-permute-start(bf16[256,512]{1,0:T(8,128)(2,1)} %collective-permute-done.10.rest_1_), channel_id=1, source_target_pairs={{0,1},{1,0},{2,3},{3,2},{4,5},{5,4},{6,7},{7,6},{8,9},{9,8},{10,11... | collective-permute-start | bytes 786440 | tf_op jit(solution)/shard_map/ppermute | solution.py:269
  91.0 7.3 %collective-permute-start.15 = (bf16[256,512]{1,0:T(8,128)(2,1)}, bf16[256,512]{1,0:T(8,128)(2,1)}, u32[]{:S(2)}, u32[]{:S(2)}) collective-permute-start(bf16[256,512]{1,0:T(8,128)(2,1)} %collective-permute-done.11.rest_2_), channel_id=1, source_target_pairs={{0,1},{1,0},{2,3},{3,2},{4,5},{5,4},{6,7},{7,6},{8,9},{9,8},{10,11... | collective-permute-start | bytes 786440 | tf_op jit(solution)/shard_map/ppermute | solution.py:269
  91.1 7.3 %collective-permute-start.16 = (bf16[256,512]{1,0:T(8,128)(2,1)}, bf16[256,512]{1,0:T(8,128)(2,1)}, u32[]{:S(2)}, u32[]{:S(2)}) collective-permute-start(bf16[256,512]{1,0:T(8,128)(2,1)} %collective-permute-done.12.rest_3_), channel_id=1, source_target_pairs={{0,1},{1,0},{2,3},{3,2},{4,5},{5,4},{6,7},{7,6},{8,9},{9,8},{10,11... | collective-permute-start | bytes 786440 | tf_op jit(solution)/shard_map/ppermute | solution.py:269
  91.6 2.0 %copy-start.3 = (bf16[1024,1792]{1,0:T(8,128)(2,1)S(1)}, bf16[1024,1792]{1,0:T(8,128)(2,1)}, u32[]{:S(2)}) copy-start(bf16[1024,1792]{1,0:T(8,128)(2,1)} %ar_ref.1) | copy-start | bytes 11010052
  96.4 1.2 %copy-start.7 = (bf16[1024,768]{1,0:T(8,128)(2,1)}, bf16[1024,768]{1,0:T(8,128)(2,1)S(1)}, u32[]{:S(2)}) copy-start(bf16[1024,768]{1,0:T(8,128)(2,1)S(1)} %get-tuple-element.23.tail_ref) | copy-start | bytes 4718596
  97.6 0.8 copy-start.9
  98.4 4.5 %copy-start.10 = (f32[1024,128]{1,0:T(8,128)S(1)}, f32[1024,128]{1,0:T(8,128)}, u32[]{:S(2)}) copy-start(f32[1024,128]{1,0:T(8,128)} %copy-done.9) | copy-start | bytes 1572868
  98.4 4.5 %copy-start.12 = (f32[256]{0:T(256)S(1)}, f32[256]{0:T(256)}, u32[]{:S(2)}) copy-start(f32[256]{0:T(256)} %param.13) | copy-start | bytes 3076
  102.9 1.4 %copy-start.8 = (bf16[1024,768]{1,0:T(8,128)(2,1)S(1)}, bf16[1024,768]{1,0:T(8,128)(2,1)}, u32[]{:S(2)}) copy-start(bf16[1024,768]{1,0:T(8,128)(2,1)} %copy-done.7) | copy-start | bytes 4718596

commit v2 on v1

--- a/solution.py
+++ b/solution.py
@@ -8,6 +8,7 @@
 TILE = 128
 NZ = 8
 NX = 4
+NB = 8
 BF = jnp.bfloat16
 F32 = jnp.float32
 
@@ -29,10 +30,23 @@
     return [(y * 2 + c, (y + dy) % 4 * 2 + (c + dc) % 2) for y in range(4) for c in range(2)]
 
 
+def place(me_ref):
+    feat = me_ref[0] // NB
+    return feat // NX, feat % NX
+
+
+def in_hbm(x):
+    return pltpu.with_memory_space_constraint(x, pltpu.HBM)
+
+
+def hbm(shape, dtype):
+    return pltpu.HBM(shape, dtype)
+
+
 def head_kernel(me_ref, x_ref, *rest):
     outs, turned = rest[:-1], rest[-1]
     turned[...] = jnp.swapaxes(x_ref[...], 0, 1)
-    z, x = me_ref[0] // NX, me_ref[0] % NX
+    z, x = place(me_ref)
     for dz in range(NZ):
         for j in range(NX):
             outs[dz][j] = turned[(z + dz) % NZ * NX + (x + j) % NX]
@@ -66,7 +80,7 @@
         grid=(n // halo - 1,),
         in_specs=[pl.BlockSpec((f, g, halo), lambda i: (0, 0, i + 1))],
         out_specs=pl.BlockSpec((g, f, halo), lambda i: (0, 0, i)),
-        out_shape=jax.ShapeDtypeStruct((g, f, n - halo), BF),
+        out_shape=hbm((g, f, n - halo), BF),
         compiler_params=VM,
         name="split_tail",
     )(features)
@@ -94,7 +108,7 @@
 
 
 def halo_kernel(me_ref, a, b, c, d, ws_ref, wn_ref, self_ref, h_ref, w_ref):
-    z, x = me_ref[0] // NX, me_ref[0] % NX
+    z, x = place(me_ref)
     rows, hid = a.shape[0], ws_ref.shape[1]
     f = rows // NZ
     total = None
@@ -128,7 +142,7 @@
             scratch_shapes=[pltpu.VMEM((rows, 2 * hid), BF)],
         ),
         out_shape=[
-            jax.ShapeDtypeStruct((halo, hid), F32),
+            hbm((halo, hid), F32),
             jax.ShapeDtypeStruct((halo, 2 * hid), BF),
         ],
         compiler_params=VM,
@@ -171,59 +185,76 @@
             out_specs=[line(halo), line(n - halo), line(r), line(TILE)],
         ),
         out_shape=[
-            jax.ShapeDtypeStruct((rows, halo), BF),
-            jax.ShapeDtypeStruct((rows, n - halo), BF),
-            jax.ShapeDtypeStruct((rows, r), BF),
-            jax.ShapeDtypeStruct((rows, TILE), F32),
+            hbm((rows, halo), BF),
+            hbm((rows, n - halo), BF),
+            hbm((rows, r), BF),
+            hbm((rows, TILE), F32),
         ],
         compiler_params=VM,
         name="mask_tiles",
-    )(tile_mask, adj_local, adj_remote)
-
-
-def gather_kernel(core_ref, head_ref, remote_ref, *rest):
-    slots, o_ref = rest[:-1], rest[-1]
-    core = core_ref[0]
-    halo, hid = slots[0].shape[0], o_ref.shape[1]
-    total = jnp.dot(head_ref[...], slots[0][...], preferred_element_type=F32)
-    for s in range(1, len(slots)):
-        dy = s if s < 4 else s - 4
-        column = 2 * dy - 1 if s < 4 else (2 * dy + 2 * core + 7) % 8 - 1
-        at = column * halo if s < 4 else pl.multiple_of(column * halo, halo)
+    )(tile_mask, in_hbm(adj_local), in_hbm(adj_remote))
+
+
+def near_kernel(head_ref, remote_ref, a, b, c, d, o_ref):
+    halo = a.shape[0]
+    total = jnp.dot(head_ref[...], a[...], preferred_element_type=F32)
+    for dy, part in ((1, b), (2, c), (3, d)):
+        at = (2 * dy - 1) * halo
         total = total + jnp.dot(
-            remote_ref[:, pl.ds(at, halo)], slots[s][...], preferred_element_type=F32
+            remote_ref[:, at : at + halo], part[...], preferred_element_type=F32
         )
+    hid = o_ref.shape[1]
     o_ref[...] = total[:, :hid] + total[:, hid:]
 
 
-def gather_halo(core, head, remote, slots):
-    rows, halo = head.shape
-    hid = slots[0].shape[1] // 2
+def far_kernel(me_ref, acc_ref, remote_ref, a, b, c, d, o_ref):
+    core = me_ref[0] % 2
+    halo, hid = a.shape[0], o_ref.shape[1]
+    total = None
+    for dy, part in enumerate((a, b, c, d)):
+        at = pl.multiple_of(((2 * dy + 2 * core + 7) % NB - 1) * halo, halo)
+        one = jnp.dot(remote_ref[:, pl.ds(at, halo)], part[...], preferred_element_type=F32)
+        total = one if total is None else total + one
+    o_ref[...] = acc_ref[...] + total[:, :hid] + total[:, hid:]
+
+
+def gather_halo(kernel, scalars, arrays, parts, out):
+    rows = arrays[0].shape[0]
+    hid = parts[0].shape[1] // 2
     block = 256
-    line = lambda w: pl.BlockSpec((block, w), lambda i, _: (i, 0))
-    return pl.pallas_call(
-        gather_kernel,
+    line = lambda w: pl.BlockSpec((block, w), lambda i, *_: (i, 0))
+    return pl.pallas_call(
+        kernel,
         grid_spec=pltpu.PrefetchScalarGridSpec(
-            num_scalar_prefetch=1,
+            num_scalar_prefetch=len(scalars),
             grid=(rows // block,),
-            in_specs=[line(halo), line(remote.shape[1])] + [full((halo, 2 * hid))] * len(slots),
+            in_specs=[line(a.shape[1]) for a in arrays] + [full(p.shape) for p in parts],
             out_specs=line(hid),
         ),
-        out_shape=jax.ShapeDtypeStruct((rows, hid), F32),
-        compiler_params=VM,
-        name="gather_halo",
-    )(core, head, remote, *slots)
-
-
-def last_kernel(x_ref, ws_ref, wn_ref, tail_ref, acc_ref, scale_ref, sh_ref, bias_ref, o_ref, h_ref, s_ref):
-    halo, hid = sh_ref.shape
+        out_shape=out((rows, hid), F32),
+        compiler_params=VM,
+    )(*scalars, *arrays, *parts)
+
+
+def last_kernel(x_ref, ws_ref, wn_ref, tail_hbm, acc_hbm, scale_hbm, sh_hbm, bias_ref, o_ref,
+                h_ref, s_ref, tail_ref, acc_ref, scale_ref, sem):
+    halo, hid = sh_hbm.shape
+    copies = [
+        pltpu.make_async_copy(sh_hbm, s_ref.at[:halo], sem.at[0]),
+        pltpu.make_async_copy(tail_hbm, tail_ref, sem.at[1]),
+        pltpu.make_async_copy(acc_hbm, acc_ref, sem.at[2]),
+        pltpu.make_async_copy(scale_hbm, scale_ref, sem.at[3]),
+    ]
+    for copy in copies:
+        copy.start()
     first = (((0,), (0,)), ((), ()))
-    s_ref[:halo, :] = sh_ref[...]
-    s_ref[halo:, :] = lax.dot_general(x_ref[...], ws_ref[...], first, preferred_element_type=F32)
     h = lax.dot_general(x_ref[...], wn_ref[...], first, preferred_element_type=F32)
     high = h.astype(BF)
     h_ref[:, :hid] = high
     h_ref[:, hid:] = (h - high.astype(F32)).astype(BF)
+    s_ref[halo:, :] = lax.dot_general(x_ref[...], ws_ref[...], first, preferred_element_type=F32)
+    for copy in copies:
+        copy.wait()
     rows, block = o_ref.shape[0], 256
     for i in range(0, rows, block):
         at = slice(i, i + block)
@@ -235,23 +266,30 @@
 
 def last_step(x, w_self, w_neigh, tail, acc, scale, self_head, bias):
     rows, hid = acc.shape
-    args = (x, w_self, w_neigh, tail, acc, scale, self_head, bias)
+    away = pl.BlockSpec(memory_space=pltpu.HBM)
     return pl.pallas_call(
         last_kernel,
         grid=(1,),
-        in_specs=[full(a.shape) for a in args],
+        in_specs=[full(x.shape), full(w_self.shape), full(w_neigh.shape), away, away, away, away, full(bias.shape)],
         out_specs=full((rows, hid)),
-        scratch_shapes=[pltpu.VMEM((x.shape[1], 2 * hid), BF), pltpu.VMEM((rows, hid), F32)],
+        scratch_shapes=[
+            pltpu.VMEM((x.shape[1], 2 * hid), BF),
+            pltpu.VMEM((rows, hid), F32),
+            pltpu.VMEM(tail.shape, BF),
+            pltpu.VMEM(acc.shape, F32),
+            pltpu.VMEM(scale.shape, F32),
+            pltpu.SemaphoreType.DMA((4,)),
+        ],
         out_shape=jax.ShapeDtypeStruct((rows, hid), BF),
         compiler_params=VM,
         name="last_step",
-    )(*args)
+    )(x, w_self, w_neigh, in_hbm(tail), in_hbm(acc), in_hbm(scale), in_hbm(self_head), bias)
 
 
 def shards(features, adj_local, adj_remote, tile_mask, w_self, w_neigh, out_bias):
     halo = adj_remote.shape[1] // (lax.axis_size("blk") - 1)
-    me = lax.axis_index("feat").reshape(1)
-    core = (lax.axis_index("blk") % 2).reshape(1)
+    me = lax.axis_index(("feat", "blk")).reshape(1)
+    features = in_hbm(features)
 
     head = split_head(me, features, halo)
     landed = [head[0]]
@@ -263,11 +301,14 @@
 
     live_head, live_tail, live_remote, scale = mask_tiles(tile_mask, adj_local, adj_remote, halo)
     rows = regroup(landed)
-    parts = [rows[0]] + [lax.ppermute(rows[j], "feat", feat_shift(0, j)) for j in (1, 2, 3)]
+    parts = [rows[0]]
+    for j in range(1, NX):
+        parts.append(lax.ppermute(rows[j], "feat", feat_shift(0, j)))
     self_head, h_head = halo_hidden(me, parts, w_self, w_neigh)
     same = [h_head] + [lax.ppermute(h_head, "blk", blk_shift(dy, 0)) for dy in (1, 2, 3)]
     other = [lax.ppermute(h, "blk", blk_shift(0, 1)) for h in same]
-    acc = gather_halo(core, live_head, live_remote, same + other)
+    acc = gather_halo(near_kernel, (), (live_head, live_remote), same, jax.ShapeDtypeStruct)
+    acc = gather_halo(far_kernel, (me,), (acc, live_remote), other, hbm)
     return last_step(
         rest, w_self, w_neigh, live_tail, acc, scale, self_head, out_bias[None, :]
     )

time: 110 us -> 114 us (1.036)
  Pallas kernels: 13.5 us -> 23.8 us
  local copies, waits for them, and re-layouts: 8.15 us -> 3.3 us
  waiting for transfers between devices: 48.3 us -> 47 us
    pallas_call x1, Pallas kernels: 2.8 us -> 8.67 us  [mask_tiles(): pl.pallas_call(mask_kernel, grid_spec=pltpu.PrefetchScalarGridSpec(num_sc...]
    unnamed x26 -> x14, local copies, waits for them, and re-layouts: 8.15 us -> 3.3 us
    pallas_call x1, Pallas kernels: 0.76 us -> 3.61 us  [split_tail(): pl.pallas_call(tail_kernel, grid=(n // halo - 1,), in_specs=[pl.BlockSpec...]
    pallas_call x2 -> x3, Pallas kernels: 8.57 us -> 9.03 us  [the longest x2 4.53 us: gather_halo(): pl.pallas_call(kernel, grid_spec=pltpu.PrefetchScalarGridSpec(num_scalar_...]
  transfers between devices with their start and end apart: 18 -> 18, of which waited for: 9 -> 9; matrix products, arithmetic and copies ran while one was open for 0% -> 0% of each run, Pallas kernels for 8% -> 14%
where the time goes in v2:
time: 114 us; the launch traced here: 112 us
  waiting for transfers between devices  47 us (41%)
  starting transfers between devices  38 us (33%)
  Pallas kernels  23.8 us (21%)
  local copies, waits for them, and re-layouts  3.3 us (3%)
    ppermute x7, waiting for transfers between devices, shards(): landed.append(lax.ppermute(head[dz], 'feat', feat_shift(dz, 0)))  32.9 us
    ppermute x7, starting transfers between devices, shards(): landed.append(lax.ppermute(head[dz], 'feat', feat_shift(dz, 0)))  15.3 us
    all_to_all x1, starting transfers between devices, shards(): rest = lax.all_to_all(rest, 'feat', split_axis=0, concat_axis=0, tiled=True)  11.6 us
    ppermute x3, waiting for transfers between devices, shards(): lax.ppermute(h_head, 'blk', blk_shift(dy, 0))  9.13 us
    pallas_call x1, Pallas kernels, mask_tiles(): pl.pallas_call(mask_kernel, grid_spec=pltpu.PrefetchScalarGridSpec(num_sc...  8.67 us
    ppermute x3, starting transfers between devices, shards(): lax.ppermute(h_head, 'blk', blk_shift(dy, 0))  5.82 us
    ppermute x3, waiting for transfers between devices, shards(): parts.append(lax.ppermute(rows[j], 'feat', feat_shift(0, j)))  4.96 us
    ppermute x3, starting transfers between devices, shards(): parts.append(lax.ppermute(rows[j], 'feat', feat_shift(0, j)))  4.76 us
  transfers between devices with their start and end apart: 18, of which 9 were waited for; matrix products, arithmetic and copies ran while one was open for 0% of the time, Pallas kernels for 14%

profile of v2, /device:TPU:2, one launch (start us, length us, event | category | flops | bytes accessed | tf_op | source)
XLA Modules:
  0.0 112.4 jit_solution(4322819686630405324)
XLA Ops:
  0.0 3.6 %split_tail.1 = bf16[32,32,768]{2,1,0:T(8,128)(2,1)} custom-call(bf16[32,32,1024]{2,1,0:T(8,128)(2,1)} %x_ref.3), custom_call_target="tpu_custom_call" | custom-call | tf_op jit(solution)/shard_map/split_tail/pallas_call | solution.py:78
  3.6 11.6 %all-to-all-start = ((bf16[32,32,768]{2,1,0:T(8,128)(2,1)}), bf16[32,32,768]{2,1,0:T(8,128)(2,1)S(1)}, u32[]{:S(2)}, u32[]{:S(2)}) async-start(bf16[32,32,768]{2,1,0:T(8,128)(2,1)} %split_tail.1), calls=%async_computation | async-start | bytes 3145728 | tf_op jit(solution)/shard_map/all_to_all | solution.py:299
  15.2 0.0 copy-start.2
  15.2 0.0 copy-start.3
  15.3 0.0 copy-start.5
  15.3 1.3 %split_head.1 = (bf16[4,32,256]{2,1,0:T(8,128)(2,1)S(1)}, bf16[4,32,256]{2,1,0:T(8,128)(2,1)S(1)}, bf16[4,32,256]{2,1,0:T(8,128)(2,1)S(1)}, bf16[4,32,256]{2,1,0...) custom-call(s32[1]{0:T(128)} %bitcast.1.me_ref, ...), custom_call_target="tpu_custom_call" | custom-call | tf_op jit(solution)/shard_map/split_head/pallas_call | solution.py:57
  16.6 1.5 %collective-permute-start = (bf16[4,32,256]{2,1,0:T(8,128)(2,1)S(1)}, bf16[4,32,256]{2,1,0:T(8,128)(2,1)S(1)}, u32[]{:S(2)}, u32[]{:S(2)}) collective-permute-start(bf16[4,32,256]{2,1,0:T(8,128)(2,1)S(1)} %get-tuple-element.27), channel_id=1, source_target_pairs={{0,32},{8,40},{16,48},{24,56},{32,64},{40,72},{48,80},{56,88},{64,... | collective-permute-start | bytes 196616 | tf_op jit(solution)/shard_map/ppermute | solution.py:297
  18.1 2.4 %collective-permute-start.1 = (bf16[4,32,256]{2,1,0:T(8,128)(2,1)S(1)}, bf16[4,32,256]{2,1,0:T(8,128)(2,1)S(1)}, u32[]{:S(2)}, u32[]{:S(2)}) collective-permute-start(bf16[4,32,256]{2,1,0:T(8,128)(2,1)S(1)} %get-tuple-element.28), channel_id=1, source_target_pairs={{0,64},{8,72},{16,80},{24,88},{32,96},{40,104},{48,112},{56,120},{... | collective-permute-start | bytes 196616 | tf_op jit(solution)/shard_map/ppermute | solution.py:297
  20.5 2.7 %collective-permute-start.2 = (bf16[4,32,256]{2,1,0:T(8,128)(2,1)S(1)}, bf16[4,32,256]{2,1,0:T(8,128)(2,1)S(1)}, u32[]{:S(2)}, u32[]{:S(2)}) collective-permute-start(bf16[4,32,256]{2,1,0:T(8,128)(2,1)S(1)} %get-tuple-element.29), channel_id=1, source_target_pairs={{0,96},{8,104},{16,112},{24,120},{32,128},{40,136},{48,144},{56,15... | collective-permute-start | bytes 196616 | tf_op jit(solution)/shard_map/ppermute | solution.py:297
  23.2 2.3 %collective-permute-start.3 = (bf16[4,32,256]{2,1,0:T(8,128)(2,1)S(1)}, bf16[4,32,256]{2,1,0:T(8,128)(2,1)S(1)}, u32[]{:S(2)}, u32[]{:S(2)}) collective-permute-start(bf16[4,32,256]{2,1,0:T(8,128)(2,1)S(1)} %get-tuple-element.30), channel_id=1, source_target_pairs={{0,128},{8,136},{16,144},{24,152},{32,160},{40,168},{48,176},{56,1... | collective-permute-start | bytes 196616 | tf_op jit(solution)/shard_map/ppermute | solution.py:297
  25.5 2.8 %collective-permute-start.4 = (bf16[4,32,256]{2,1,0:T(8,128)(2,1)S(1)}, bf16[4,32,256]{2,1,0:T(8,128)(2,1)S(1)}, u32[]{:S(2)}, u32[]{:S(2)}) collective-permute-start(bf16[4,32,256]{2,1,0:T(8,128)(2,1)S(1)} %get-tuple-element.31), channel_id=1, source_target_pairs={{0,160},{8,168},{16,176},{24,184},{32,192},{40,200},{48,208},{56,2... | collective-permute-start | bytes 196616 | tf_op jit(solution)/shard_map/ppermute | solution.py:297
  28.3 26.2 %collective-permute-done.refs_1_ = bf16[4,32,256]{2,1,0:T(8,128)(2,1)S(1)} collective-permute-done((bf16[4,32,256]{2,1,0:T(8,128)(2,1)S(1)}, bf16[4,32,256]{2,1,0:T(8,128)(2,1)S(1)}, u32[]{:S(2)}, u32[]{:S(2)}) %collective-permute-start) | collective-permute-done | bytes 65568 | tf_op jit(solution)/shard_map/ppermute | solution.py:297
  54.5 2.4 %collective-permute-start.5 = (bf16[4,32,256]{2,1,0:T(8,128)(2,1)S(1)}, bf16[4,32,256]{2,1,0:T(8,128)(2,1)S(1)}, u32[]{:S(2)}, u32[]{:S(2)}) collective-permute-start(bf16[4,32,256]{2,1,0:T(8,128)(2,1)S(1)} %get-tuple-element.32), channel_id=1, source_target_pairs={{0,192},{8,200},{16,208},{24,216},{32,224},{40,232},{48,240},{56,2... | collective-permute-start | bytes 196616 | tf_op jit(solution)/shard_map/ppermute | solution.py:297
  56.9 2.0 %collective-permute-done.1.refs_2_ = bf16[4,32,256]{2,1,0:T(8,128)(2,1)S(1)} collective-permute-done((bf16[4,32,256]{2,1,0:T(8,128)(2,1)S(1)}, bf16[4,32,256]{2,1,0:T(8,128)(2,1)S(1)}, u32[]{:S(2)}, u32[]{:S(2)}) %collective-permute-start.1) | collective-permute-done | bytes 65568 | tf_op jit(solution)/shard_map/ppermute | solution.py:297
  58.9 1.2 %collective-permute-start.6 = (bf16[4,32,256]{2,1,0:T(8,128)(2,1)S(1)}, bf16[4,32,256]{2,1,0:T(8,128)(2,1)S(1)}, u32[]{:S(2)}, u32[]{:S(2)}) collective-permute-start(bf16[4,32,256]{2,1,0:T(8,128)(2,1)S(1)} %get-tuple-element.33), channel_id=1, source_target_pairs={{0,224},{8,232},{16,240},{24,248},{32,0},{40,8},{48,16},{56,24},{6... | collective-permute-start | bytes 196616 | tf_op jit(solution)/shard_map/ppermute | solution.py:297
  60.2 0.8 collective-permute-done.2.refs_3_
  61.0 3.8 %collective-permute-done.3.refs_4_ = bf16[4,32,256]{2,1,0:T(8,128)(2,1)S(1)} collective-permute-done((bf16[4,32,256]{2,1,0:T(8,128)(2,1)S(1)}, bf16[4,32,256]{2,1,0:T(8,128)(2,1)S(1)}, u32[]{:S(2)}, u32[]{:S(2)}) %collective-permute-start.3) | collective-permute-done | bytes 65568 | tf_op jit(solution)/shard_map/ppermute | solution.py:297
  64.8 0.0 collective-permute-done.4.refs_5_
  64.8 0.0 collective-permute-done.5.refs_6_
  64.8 0.0 collective-permute-done.6.refs_7_
  64.8 1.5 %collective-permute-start.7 = (bf16[256,256]{1,0:T(8,128)(2,1)S(1)}, bf16[256,256]{1,0:T(8,128)(2,1)S(1)}, u32[]{:S(2)}, u32[]{:S(2)}) collective-permute-start(bf16[256,256]{1,0:T(8,128)(2,1)S(1)} %get-tuple-element.35), channel_id=1, source_target_pairs={{0,8},{8,16},{16,24},{24,0},{32,40},{40,48},{48,56},{56,32},{64,72... | collective-permute-start | bytes 393224 | tf_op jit(solution)/shard_map/ppermute | solution.py:306
  66.3 0.9 collective-permute-start.8
  67.2 2.3 %collective-permute-start.9 = (bf16[256,256]{1,0:T(8,128)(2,1)S(1)}, bf16[256,256]{1,0:T(8,128)(2,1)S(1)}, u32[]{:S(2)}, u32[]{:S(2)}) collective-permute-start(bf16[256,256]{1,0:T(8,128)(2,1)S(1)} %get-tuple-element.37), channel_id=1, source_target_pairs={{0,24},{8,0},{16,8},{24,16},{32,56},{40,32},{48,40},{56,48},{64,88... | collective-permute-start | bytes 393224 | tf_op jit(solution)/shard_map/ppermute | solution.py:306
  69.6 0.7 collective-permute-done.7.b
  70.3 3.7 %collective-permute-done.8.c = bf16[256,256]{1,0:T(8,128)(2,1)S(1)} collective-permute-done((bf16[256,256]{1,0:T(8,128)(2,1)S(1)}, bf16[256,256]{1,0:T(8,128)(2,1)S(1)}, u32[]{:S(2)}, u32[]{:S(2)}) %collective-permute-start.8) | collective-permute-done | bytes 131104 | tf_op jit(solution)/shard_map/ppermute | solution.py:306
  74.0 0.6 collective-permute-done.9.d
  74.6 1.2 %halo_hidden.1 = (f32[256,256]{1,0:T(8,128)}, bf16[256,512]{1,0:T(8,128)(2,1)S(1)}) custom-call(s32[1]{0:T(128)} %bitcast.1.me_ref, bf16[256,256]{1,0:T(8,128)(2,1)S(1)} %get-tuple-element.34.a, bf16[256,256]{1,0:T(8,128)(2,1)S(1)} %collective-permute-done.7.b, bf16[256,256]{1,0:T(8,128)(2,1)S(1)} %collective-permute-done.8.c, ...), custom_call_target="tpu_custom_call" | custom-call | tf_op jit(solution)/shard_map/halo_hidden/pallas_call | solution.py:135
  75.7 1.6 %collective-permute-start.10 = (bf16[256,512]{1,0:T(8,128)(2,1)S(1)}, bf16[256,512]{1,0:T(8,128)(2,1)S(1)}, u32[]{:S(2)}, u32[]{:S(2)}) collective-permute-start(bf16[256,512]{1,0:T(8,128)(2,1)S(1)} %get-tuple-element.38.a), channel_id=1, source_target_pairs={{0,2},{1,3},{2,4},{3,5},{4,6},{5,7},{6,0},{7,1},{8,10},{9,11},{10,... | collective-permute-start | bytes 786440 | tf_op jit(solution)/shard_map/ppermute | solution.py:308
  77.3 2.9 %collective-permute-start.11 = (bf16[256,512]{1,0:T(8,128)(2,1)S(1)}, bf16[256,512]{1,0:T(8,128)(2,1)S(1)}, u32[]{:S(2)}, u32[]{:S(2)}) collective-permute-start(bf16[256,512]{1,0:T(8,128)(2,1)S(1)} %get-tuple-element.38.a), channel_id=1, source_target_pairs={{0,4},{1,5},{2,6},{3,7},{4,0},{5,1},{6,2},{7,3},{8,12},{9,13},{10,... | collective-permute-start | bytes 786440 | tf_op jit(solution)/shard_map/ppermute | solution.py:308
  80.2 1.3 %collective-permute-start.12 = (bf16[256,512]{1,0:T(8,128)(2,1)S(1)}, bf16[256,512]{1,0:T(8,128)(2,1)S(1)}, u32[]{:S(2)}, u32[]{:S(2)}) collective-permute-start(bf16[256,512]{1,0:T(8,128)(2,1)S(1)} %get-tuple-element.38.a), channel_id=1, source_target_pairs={{0,6},{1,7},{2,0},{3,1},{4,2},{5,3},{6,4},{7,5},{8,14},{9,15},{10,... | collective-permute-start | bytes 786440 | tf_op jit(solution)/shard_map/ppermute | solution.py:308
  81.6 0.0 collective-permute-start.13
  81.6 3.4 %collective-permute-done.10.b = bf16[256,512]{1,0:T(8,128)(2,1)S(1)} collective-permute-done((bf16[256,512]{1,0:T(8,128)(2,1)S(1)}, bf16[256,512]{1,0:T(8,128)(2,1)S(1)}, u32[]{:S(2)}, u32[]{:S(2)}) %collective-permute-start.10) | collective-permute-done | bytes 262176 | tf_op jit(solution)/shard_map/ppermute | solution.py:308
  85.0 0.0 collective-permute-start.14
  85.0 5.7 %collective-permute-done.11.c = bf16[256,512]{1,0:T(8,128)(2,1)S(1)} collective-permute-done((bf16[256,512]{1,0:T(8,128)(2,1)S(1)}, bf16[256,512]{1,0:T(8,128)(2,1)S(1)}, u32[]{:S(2)}, u32[]{:S(2)}) %collective-permute-start.11) | collective-permute-done | bytes 262176 | tf_op jit(solution)/shard_map/ppermute | solution.py:308
  90.7 0.0 collective-permute-start.15
  90.7 0.0 collective-permute-done.12.d
  90.7 0.5 collective-permute-start.16
  91.2 8.7 %mask_tiles.1 = (bf16[1024,256]{1,0:T(8,128)(2,1)}, bf16[1024,768]{1,0:T(8,128)(2,1)}, bf16[1024,1792]{1,0:T(8,128)(2,1)}, f32[1024,128]{1,0:T(8,128)}) custom-call(s32[8,22]{1,0:T(8,128)S(1)} %copy-done.5, bf16[1024,1024]{1,0:T(8,128)(2,1)} %al_ref.1, bf16[1024,1792]{1,0:T(8,128)(2,1)} %ar_ref.1), custom_call_target="tpu_custom_call" | custom-call | tf_op jit(solution)/shard_map/mask_tiles/pallas_call | solution.py:179
  99.9 2.0 %copy-done = bf16[1024,1792]{1,0:T(8,128)(2,1)S(1)} copy-done((bf16[1024,1792]{1,0:T(8,128)(2,1)S(1)}, bf16[1024,1792]{1,0:T(8,128)(2,1)}, u32[]{:S(2)}) %copy-start) | copy-done | bytes 3670040
  101.9 1.0 copy-done.4
  103.0 1.8 %shard_map.73.acc_ref = f32[1024,256]{1,0:T(8,128)S(1)} custom-call(bf16[1024,256]{1,0:T(8,128)(2,1)S(1)} %copy-done.4, bf16[1024,1792]{1,0:T(8,128)(2,1)S(1)} %copy-done, bf16[256,512]{1,0:T(8,128)(2,1)S(1)} %get-tuple-element.38.a, bf16[256,512]{1,0:T(8,128)(2,1)S(1)} %collective-permute-done.10.b, bf16[256,512]{1,0:T(8,128)(2,1)S(1)} %collective-permute-done.11.c, ...), custom_call_target="tpu_custom_call" | custom-call | tf_op jit(solution)/shard_map/pallas_call | solution.py:226
  104.8 0.0 copy-start.6
  104.8 0.0 collective-permute-done.13.a
  104.8 0.0 collective-permute-done.15.c
  104.8 0.0 collective-permute-done.16.d
  104.8 0.2 copy-done.1
  105.0 2.8 %shard_map.74.acc_hbm = f32[1024,256]{1,0:T(8,128)} custom-call(s32[1]{0:T(128)} %bitcast.1.me_ref, f32[1024,256]{1,0:T(8,128)S(1)} %shard_map.73.acc_ref, bf16[1024,1792]{1,0:T(8,128)(2,1)S(1)} %copy-done.1, bf16[256,512]{1,0:T(8,128)(2,1)S(1)} %collective-permute-done.13.a, bf16[256,512]{1,0:T(8,128)(2,1)S(1)} %collective-permute-done.14.b, ...), custom_call_target="tpu_custom_call" | custom-call | tf_op jit(solution)/shard_map/pallas_call | solution.py:226
  107.8 4.5 %last_step.1 = bf16[1024,256]{1,0:T(8,128)(2,1)} custom-call(bf16[1024,768]{1,0:T(8,128)(2,1)S(1)} %bitcast.3, bf16[1024,256]{1,0:T(8,128)(2,1)S(1)} %copy-done.2, bf16[1024,256]{1,0:T(8,128)(2,1)S(1)} %copy-done.3, bf16[1024,768]{1,0:T(8,128)(2,1)} %get-tuple-element.23.tail_hbm, f32[1024,256]{1,0:T(8,128)} %shard_map.74.acc_hbm, ...), custom_call_target="tpu_custom_call" | custom-call | tf_op jit(solution)/shard_map/last_step/pallas_call | solution.py:270
  (10 shorter events, 0.1 us)
Async XLA Ops:
  3.6 104.2 %all-to-all-start = ((bf16[32,32,768]{2,1,0:T(8,128)(2,1)}), bf16[32,32,768]{2,1,0:T(8,128)(2,1)S(1)}, u32[]{:S(2)}, u32[]{:S(2)}) async-start(bf16[32,32,768]{2,1,0:T(8,128)(2,1)} %split_tail.1), calls=%async_computation | async-start | bytes 3145728 | tf_op jit(solution)/shard_map/all_to_all | solution.py:299
  15.2 59.3 %copy-start.2 = (bf16[1024,256]{1,0:T(8,128)(2,1)S(1)}, bf16[1024,256]{1,0:T(8,128)(2,1)}, u32[]{:S(2)}) copy-start(bf16[1024,256]{1,0:T(8,128)(2,1)} %ws_ref.3) | copy-start | bytes 1572868
  15.2 59.3 %copy-start.3 = (bf16[1024,256]{1,0:T(8,128)(2,1)S(1)}, bf16[1024,256]{1,0:T(8,128)(2,1)}, u32[]{:S(2)}) copy-start(bf16[1024,256]{1,0:T(8,128)(2,1)} %wn_ref.3) | copy-start | bytes 1572868
  15.3 76.0 %copy-start.5 = (s32[8,22]{1,0:T(8,128)S(1)}, s32[8,22]{1,0:T(8,128)}, u32[]{:S(2)}) copy-start(s32[8,22]{1,0:T(8,128)} %mask_ref.1) | copy-start | bytes 2116
  16.6 37.9 %collective-permute-start = (bf16[4,32,256]{2,1,0:T(8,128)(2,1)S(1)}, bf16[4,32,256]{2,1,0:T(8,128)(2,1)S(1)}, u32[]{:S(2)}, u32[]{:S(2)}) collective-permute-start(bf16[4,32,256]{2,1,0:T(8,128)(2,1)S(1)} %get-tuple-element.27), channel_id=1, source_target_pairs={{0,32},{8,40},{16,48},{24,56},{32,64},{40,72},{48,80},{56,88},{64,... | collective-permute-start | bytes 196616 | tf_op jit(solution)/shard_map/ppermute | solution.py:297
  18.1 40.8 %collective-permute-start.1 = (bf16[4,32,256]{2,1,0:T(8,128)(2,1)S(1)}, bf16[4,32,256]{2,1,0:T(8,128)(2,1)S(1)}, u32[]{:S(2)}, u32[]{:S(2)}) collective-permute-start(bf16[4,32,256]{2,1,0:T(8,128)(2,1)S(1)} %get-tuple-element.28), channel_id=1, source_target_pairs={{0,64},{8,72},{16,80},{24,88},{32,96},{40,104},{48,112},{56,120},{... | collective-permute-start | bytes 196616 | tf_op jit(solution)/shard_map/ppermute | solution.py:297
  20.5 40.5 %collective-permute-start.2 = (bf16[4,32,256]{2,1,0:T(8,128)(2,1)S(1)}, bf16[4,32,256]{2,1,0:T(8,128)(2,1)S(1)}, u32[]{:S(2)}, u32[]{:S(2)}) collective-permute-start(bf16[4,32,256]{2,1,0:T(8,128)(2,1)S(1)} %get-tuple-element.29), channel_id=1, source_target_pairs={{0,96},{8,104},{16,112},{24,120},{32,128},{40,136},{48,144},{56,15... | collective-permute-start | bytes 196616 | tf_op jit(solution)/shard_map/ppermute | solution.py:297
  23.2 41.5 %collective-permute-start.3 = (bf16[4,32,256]{2,1,0:T(8,128)(2,1)S(1)}, bf16[4,32,256]{2,1,0:T(8,128)(2,1)S(1)}, u32[]{:S(2)}, u32[]{:S(2)}) collective-permute-start(bf16[4,32,256]{2,1,0:T(8,128)(2,1)S(1)} %get-tuple-element.30), channel_id=1, source_target_pairs={{0,128},{8,136},{16,144},{24,152},{32,160},{40,168},{48,176},{56,1... | collective-permute-start | bytes 196616 | tf_op jit(solution)/shard_map/ppermute | solution.py:297
  25.5 39.2 %collective-permute-start.4 = (bf16[4,32,256]{2,1,0:T(8,128)(2,1)S(1)}, bf16[4,32,256]{2,1,0:T(8,128)(2,1)S(1)}, u32[]{:S(2)}, u32[]{:S(2)}) collective-permute-start(bf16[4,32,256]{2,1,0:T(8,128)(2,1)S(1)} %get-tuple-element.31), channel_id=1, source_target_pairs={{0,160},{8,168},{16,176},{24,184},{32,192},{40,200},{48,208},{56,2... | collective-permute-start | bytes 196616 | tf_op jit(solution)/shard_map/ppermute | solution.py:297
  54.5 10.3 %collective-permute-start.5 = (bf16[4,32,256]{2,1,0:T(8,128)(2,1)S(1)}, bf16[4,32,256]{2,1,0:T(8,128)(2,1)S(1)}, u32[]{:S(2)}, u32[]{:S(2)}) collective-permute-start(bf16[4,32,256]{2,1,0:T(8,128)(2,1)S(1)} %get-tuple-element.32), channel_id=1, source_target_pairs={{0,192},{8,200},{16,208},{24,216},{32,224},{40,232},{48,240},{56,2... | collective-permute-start | bytes 196616 | tf_op jit(solution)/shard_map/ppermute | solution.py:297
  58.9 5.9 %collective-permute-start.6 = (bf16[4,32,256]{2,1,0:T(8,128)(2,1)S(1)}, bf16[4,32,256]{2,1,0:T(8,128)(2,1)S(1)}, u32[]{:S(2)}, u32[]{:S(2)}) collective-permute-start(bf16[4,32,256]{2,1,0:T(8,128)(2,1)S(1)} %get-tuple-element.33), channel_id=1, source_target_pairs={{0,224},{8,232},{16,240},{24,248},{32,0},{40,8},{48,16},{56,24},{6... | collective-permute-start | bytes 196616 | tf_op jit(solution)/shard_map/ppermute | solution.py:297
  64.8 5.5 %collective-permute-start.7 = (bf16[256,256]{1,0:T(8,128)(2,1)S(1)}, bf16[256,256]{1,0:T(8,128)(2,1)S(1)}, u32[]{:S(2)}, u32[]{:S(2)}) collective-permute-start(bf16[256,256]{1,0:T(8,128)(2,1)S(1)} %get-tuple-element.35), channel_id=1, source_target_pairs={{0,8},{8,16},{16,24},{24,0},{32,40},{40,48},{48,56},{56,32},{64,72... | collective-permute-start | bytes 393224 | tf_op jit(solution)/shard_map/ppermute | solution.py:306
  66.3 7.7 %collective-permute-start.8 = (bf16[256,256]{1,0:T(8,128)(2,1)S(1)}, bf16[256,256]{1,0:T(8,128)(2,1)S(1)}, u32[]{:S(2)}, u32[]{:S(2)}) collective-permute-start(bf16[256,256]{1,0:T(8,128)(2,1)S(1)} %get-tuple-element.36), channel_id=1, source_target_pairs={{0,16},{8,24},{16,0},{24,8},{32,48},{40,56},{48,32},{56,40},{64,80... | collective-permute-start | bytes 393224 | tf_op jit(solution)/shard_map/ppermute | solution.py:306
  67.2 7.3 %collective-permute-start.9 = (bf16[256,256]{1,0:T(8,128)(2,1)S(1)}, bf16[256,256]{1,0:T(8,128)(2,1)S(1)}, u32[]{:S(2)}, u32[]{:S(2)}) collective-permute-start(bf16[256,256]{1,0:T(8,128)(2,1)S(1)} %get-tuple-element.37), channel_id=1, source_target_pairs={{0,24},{8,0},{16,8},{24,16},{32,56},{40,32},{48,40},{56,48},{64,88... | collective-permute-start | bytes 393224 | tf_op jit(solution)/shard_map/ppermute | solution.py:306
  75.7 9.3 %collective-permute-start.10 = (bf16[256,512]{1,0:T(8,128)(2,1)S(1)}, bf16[256,512]{1,0:T(8,128)(2,1)S(1)}, u32[]{:S(2)}, u32[]{:S(2)}) collective-permute-start(bf16[256,512]{1,0:T(8,128)(2,1)S(1)} %get-tuple-element.38.a), channel_id=1, source_target_pairs={{0,2},{1,3},{2,4},{3,5},{4,6},{5,7},{6,0},{7,1},{8,10},{9,11},{10,... | collective-permute-start | bytes 786440 | tf_op jit(solution)/shard_map/ppermute | solution.py:308
  77.3 13.4 %collective-permute-start.11 = (bf16[256,512]{1,0:T(8,128)(2,1)S(1)}, bf16[256,512]{1,0:T(8,128)(2,1)S(1)}, u32[]{:S(2)}, u32[]{:S(2)}) collective-permute-start(bf16[256,512]{1,0:T(8,128)(2,1)S(1)} %get-tuple-element.38.a), channel_id=1, source_target_pairs={{0,4},{1,5},{2,6},{3,7},{4,0},{5,1},{6,2},{7,3},{8,12},{9,13},{10,... | collective-permute-start | bytes 786440 | tf_op jit(solution)/shard_map/ppermute | solution.py:308
  80.2 10.5 %collective-permute-start.12 = (bf16[256,512]{1,0:T(8,128)(2,1)S(1)}, bf16[256,512]{1,0:T(8,128)(2,1)S(1)}, u32[]{:S(2)}, u32[]{:S(2)}) collective-permute-start(bf16[256,512]{1,0:T(8,128)(2,1)S(1)} %get-tuple-element.38.a), channel_id=1, source_target_pairs={{0,6},{1,7},{2,0},{3,1},{4,2},{5,3},{6,4},{7,5},{8,14},{9,15},{10,... | collective-permute-start | bytes 786440 | tf_op jit(solution)/shard_map/ppermute | solution.py:308
  81.6 23.2 %collective-permute-start.13 = (bf16[256,512]{1,0:T(8,128)(2,1)S(1)}, bf16[256,512]{1,0:T(8,128)(2,1)S(1)}, u32[]{:S(2)}, u32[]{:S(2)}) collective-permute-start(bf16[256,512]{1,0:T(8,128)(2,1)S(1)} %get-tuple-element.38.a), channel_id=1, source_target_pairs={{0,1},{1,0},{2,3},{3,2},{4,5},{5,4},{6,7},{7,6},{8,9},{9,8},{10,11... | collective-permute-start | bytes 786440 | tf_op jit(solution)/shard_map/ppermute | solution.py:309
  85.0 19.8 %collective-permute-start.14 = (bf16[256,512]{1,0:T(8,128)(2,1)S(1)}, bf16[256,512]{1,0:T(8,128)(2,1)S(1)}, u32[]{:S(2)}, u32[]{:S(2)}) collective-permute-start(bf16[256,512]{1,0:T(8,128)(2,1)S(1)} %collective-permute-done.10.b), channel_id=1, source_target_pairs={{0,1},{1,0},{2,3},{3,2},{4,5},{5,4},{6,7},{7,6},{8,9},{9,8},{10,11... | collective-permute-start | bytes 786440 | tf_op jit(solution)/shard_map/ppermute | solution.py:309
  90.7 14.1 %collective-permute-start.15 = (bf16[256,512]{1,0:T(8,128)(2,1)S(1)}, bf16[256,512]{1,0:T(8,128)(2,1)S(1)}, u32[]{:S(2)}, u32[]{:S(2)}) collective-permute-start(bf16[256,512]{1,0:T(8,128)(2,1)S(1)} %collective-permute-done.11.c), channel_id=1, source_target_pairs={{0,1},{1,0},{2,3},{3,2},{4,5},{5,4},{6,7},{7,6},{8,9},{9,8},{10,11... | collective-permute-start | bytes 786440 | tf_op jit(solution)/shard_map/ppermute | solution.py:309
  90.7 14.1 %collective-permute-start.16 = (bf16[256,512]{1,0:T(8,128)(2,1)S(1)}, bf16[256,512]{1,0:T(8,128)(2,1)S(1)}, u32[]{:S(2)}, u32[]{:S(2)}) collective-permute-start(bf16[256,512]{1,0:T(8,128)(2,1)S(1)} %collective-permute-done.12.d), channel_id=1, source_target_pairs={{0,1},{1,0},{2,3},{3,2},{4,5},{5,4},{6,7},{7,6},{8,9},{9,8},{10,11... | collective-permute-start | bytes 786440 | tf_op jit(solution)/shard_map/ppermute | solution.py:309
  99.9 2.0 %copy-start = (bf16[1024,1792]{1,0:T(8,128)(2,1)S(1)}, bf16[1024,1792]{1,0:T(8,128)(2,1)}, u32[]{:S(2)}) copy-start(bf16[1024,1792]{1,0:T(8,128)(2,1)} %get-tuple-element.25.remote_ref) | copy-start | bytes 11010052
  101.9 1.0 copy-start.4
  103.0 2.0 %copy-start.1 = (bf16[1024,1792]{1,0:T(8,128)(2,1)S(1)}, bf16[1024,1792]{1,0:T(8,128)(2,1)}, u32[]{:S(2)}) copy-start(bf16[1024,1792]{1,0:T(8,128)(2,1)} %get-tuple-element.25.remote_ref) | copy-start | bytes 11010052
  104.8 3.0 %copy-start.6 = (f32[256]{0:T(256)S(1)}, f32[256]{0:T(256)}, u32[]{:S(2)}) copy-start(f32[256]{0:T(256)} %param.13) | copy-start | bytes 3076

commit v3 on v2

v3 whole, which is shorter than its diff:
```python
import jax
import jax.numpy as jnp
from jax import lax
from jax.experimental import pallas as pl
from jax.experimental.pallas import tpu as pltpu
from jax.sharding import PartitionSpec as P

TILE = 128
NZ = 8
NX = 4
NB = 8
EARLY = 512
BF = jnp.bfloat16
F32 = jnp.float32


VM = pltpu.CompilerParams(vmem_limit_bytes=16 << 20)


def full(shape):
    return pl.BlockSpec(shape, lambda *_: (0,) * len(shape))


def feat_shift(dz, dx):
    return [
        (z * NX + x, (z + dz) % NZ * NX + (x + dx) % NX) for z in range(NZ) for x in range(NX)
    ]


def blk_shift(dy, dc):
    return [(y * 2 + c, (y + dy) % 4 * 2 + (c + dc) % 2) for y in range(4) for c in range(2)]


def place(me_ref):
    feat = me_ref[0] // NB
    return feat // NX, feat % NX


def in_hbm(x):
    return pltpu.with_memory_space_constraint(x, pltpu.HBM)


def hbm(shape, dtype):
    return pltpu.HBM(shape, dtype)


def swap_matrix():
    r = lax.broadcasted_iota(jnp.int32, (256, 256), 0)
    c = lax.broadcasted_iota(jnp.int32, (256, 256), 1)
    hit = ((r & 15) == (c >> 4)) & ((r >> 4) == (c & 15))
    return jnp.where(hit, 1.0, 0.0).astype(BF)


def swapped(swap, block):
    n = block.shape[-1]
    out = jnp.dot(swap, block.reshape(256, n), preferred_element_type=F32)
    return out.astype(BF).reshape(16, 16, n)


def head_kernel(me_ref, x_ref, *rest):
    outs, turned = rest[:-1], rest[-1]
    swap = swap_matrix()
    f, g, _ = x_ref.shape
    for f0 in range(0, f, 16):
        for g0 in range(0, g, 16):
            turned[g0 : g0 + 16, f0 : f0 + 16, :] = swapped(swap, x_ref[f0 : f0 + 16, g0 : g0 + 16, :])
    z, x = place(me_ref)
    for dz in range(NZ):
        for j in range(NX):
            outs[dz][j] = turned[(z + dz) % NZ * NX + (x + j) % NX]


def split_head(me, features, halo):
    f, g, _ = features.shape
    return pl.pallas_call(
        head_kernel,
        grid_spec=pltpu.PrefetchScalarGridSpec(
            num_scalar_prefetch=1,
            grid=(1,),
            in_specs=[full((f, g, halo))],
            out_specs=[full((NX, f, halo))] * NZ,
            scratch_shapes=[pltpu.VMEM((g, f, halo), BF)],
        ),
        out_shape=[jax.ShapeDtypeStruct((NX, f, halo), BF)] * NZ,
        compiler_params=VM,
        name="split_head",
    )(me, features)


def tail_kernel(x_hbm, o_hbm, x_ref, o_ref, sem):
    f, g, n = x_ref.shape
    halo = x_hbm.shape[2] - n
    chunks = range(0, f, 16)
    ins = [
        pltpu.make_async_copy(
            x_hbm.at[pl.ds(f0, 16), :, pl.ds(halo, n)], x_ref.at[pl.ds(f0, 16)], sem.at[0, i]
        )
        for i, f0 in enumerate(chunks)
    ]
    for copy in ins:
        copy.start()
    swap = swap_matrix()
    outs = []
    for i, f0 in enumerate(chunks):
        ins[i].wait()
        for g0 in range(0, g, 16):
            o_ref[g0 : g0 + 16, f0 : f0 + 16, :] = swapped(swap, x_ref[f0 : f0 + 16, g0 : g0 + 16, :])
        copy = pltpu.make_async_copy(
            o_ref.at[:, pl.ds(f0, 16), :], o_hbm.at[:, pl.ds(f0, 16), :], sem.at[1, i]
        )
        copy.start()
        outs.append(copy)
    for copy in outs:
        copy.wait()


def split_tail(features, halo):
    f, g, n = features.shape
    return pl.pallas_call(
        tail_kernel,
        in_specs=[pl.BlockSpec(memory_space=pltpu.HBM)],
        out_specs=pl.BlockSpec(memory_space=pltpu.HBM),
        out_shape=hbm((g, f, n - halo), BF),
        scratch_shapes=[
            pltpu.VMEM((f, g, n - halo), BF),
            pltpu.VMEM((g, f, n - halo), BF),
            pltpu.SemaphoreType.DMA((2, f // 16)),
        ],
        compiler_params=VM,
        name="split_tail",
    )(features)


def regroup_kernel(*refs):
    ins, outs = refs[:NZ], refs[NZ:]
    f, halo = ins[0].shape[1], outs[0].shape[1]
    for j in range(NX):
        for dz in range(NZ):
            at = slice(dz * f, (dz + 1) * f)
            outs[j][at, :] = ins[dz][j, :, :halo]
            outs[NX + j][at, :] = ins[dz][j, :, halo:]


def regroup(parts, halo):
    _, f, early = parts[0].shape
    shapes = [(NZ * f, halo)] * NX + [(NZ * f, early - halo)] * NX
    return pl.pallas_call(
        regroup_kernel,
        grid=(1,),
        in_specs=[full((NX, f, early))] * NZ,
        out_specs=[full(shape) for shape in shapes],
        out_shape=[jax.ShapeDtypeStruct(shape, BF) for shape in shapes],
        compiler_params=VM,
        name="regroup",
    )(*parts)


def weights_kernel(me_ref, ws_hbm, wn_hbm, rot_ref, turned_ref, ws_ref, wn_ref, sem):
    copies = [
        pltpu.make_async_copy(ws_hbm, ws_ref, sem.at[0]),
        pltpu.make_async_copy(wn_hbm, wn_ref, sem.at[1]),
    ]
    for copy in copies:
        copy.start()
    z, x = place(me_ref)
    total, hid = ws_ref.shape
    f = total // (NZ * NX)
    for half, w_ref in enumerate((ws_ref, wn_ref)):
        copies[half].wait()
        at = slice(half * hid, (half + 1) * hid)
        turned_ref[at, :] = w_ref[...].T
        for j in range(NX):
            for dz in range(NZ):
                src = ((z + (NZ - dz)) % NZ * NX + (x + (NX - j)) % NX) * f
                to = (j * NZ + dz) * f
                rot_ref[to : to + f, at] = w_ref[pl.ds(pl.multiple_of(src, f), f), :]


def weights(me, w_self, w_neigh):
    f, hid = w_self.shape
    away = pl.BlockSpec(memory_space=pltpu.HBM)
    return pl.pallas_call(
        weights_kernel,
        grid_spec=pltpu.PrefetchScalarGridSpec(
            num_scalar_prefetch=1,
            grid=(1,),
            in_specs=[away, away],
            out_specs=[full((f, 2 * hid)), full((2 * hid, f))],
            scratch_shapes=[
                pltpu.VMEM((f, hid), BF),
                pltpu.VMEM((f, hid), BF),
                pltpu.SemaphoreType.DMA((2,)),
            ],
        ),
        out_shape=[
            jax.ShapeDtypeStruct((f, 2 * hid), BF),
            jax.ShapeDtypeStruct((2 * hid, f), BF),
        ],
        compiler_params=VM,
        name="weights",
    )(me, in_hbm(w_self), in_hbm(w_neigh))


def project(parts, rot_ref, columns):
    rows = parts[0].shape[0]
    total = None
    for j, part in enumerate(parts):
        one = lax.dot_general(
            part[...],
            rot_ref[j * rows : (j + 1) * rows, columns],
            (((0,), (0,)), ((), ())),
            preferred_element_type=F32,
        )
        total = one if total is None else total + one
    return total


def halo_kernel(a, b, c, d, rot_ref, h_ref):
    hid = h_ref.shape[1]
    h_ref[...] = project((a, b, c, d), rot_ref, slice(hid, None)).astype(BF)


def halo_hidden(parts, rot):
    rows, halo = parts[0].shape
    hid = rot.shape[1] // 2
    return pl.pallas_call(
        halo_kernel,
        grid=(1,),
        in_specs=[full((rows, halo))] * NX + [full(rot.shape)],
        out_specs=full((halo, hid)),
        out_shape=jax.ShapeDtypeStruct((halo, hid), BF),
        compiler_params=VM,
        name="halo_hidden",
    )(*parts, rot)


def mid_kernel(*refs):
    heads, mids, (rot_ref, mid_ref, acc_ref, self_ref, o_ref) = refs[:NX], refs[NX : 2 * NX], refs[2 * NX :]
    halo, hid = heads[0].shape[1], o_ref.shape[1]
    h = project(mids, rot_ref, slice(hid, None)).astype(BF)
    o_ref[...] = acc_ref[...] + jnp.dot(mid_ref[...], h, preferred_element_type=F32)
    self_ref[:halo, :] = project(heads, rot_ref, slice(0, hid))
    self_ref[halo:, :] = project(mids, rot_ref, slice(0, hid))


def mid_hidden(heads, mids, rot, live_mid, acc):
    early = heads[0].shape[1] + mids[0].shape[1]
    hid = rot.shape[1] // 2
    args = (*heads, *mids, rot, live_mid, acc)
    return pl.pallas_call(
        mid_kernel,
        grid=(1,),
        in_specs=[full(a.shape) for a in args],
        out_specs=[full((early, hid)), full(acc.shape)],
        out_shape=[hbm((early, hid), F32), jax.ShapeDtypeStruct(acc.shape, F32)],
        compiler_params=VM,
        name="mid_hidden",
    )(*args)


def mask_kernel(me_ref, mask_ref, al_hbm, ar_hbm, head_ref, mid_ref, tail_hbm, near_ref, far_ref, scale_hbm,
                al_ref, ar_ref, tail_ref, scale_ref, sem):
    block = 2 * TILE
    count = al_ref.shape[0] // block
    ins, outs = [], []
    for i in range(count):
        at = pl.ds(i * block, block)
        ins.append(
            (
                pltpu.make_async_copy(al_hbm.at[at], al_ref.at[at], sem.at[0, i]),
                pltpu.make_async_copy(ar_hbm.at[at], ar_ref.at[at], sem.at[1, i]),
            )
        )
        for copy in ins[-1]:
            copy.start()
    local, halo, mid = al_ref.shape[1] // TILE, head_ref.shape[1], mid_ref.shape[1]
    core = me_ref[0] % 2
    for i in range(count):
        for copy in ins[i]:
            copy.wait()
        for row in range(i * 2, i * 2 + 2):
            rows = slice(row * TILE, (row + 1) * TILE)
            degree = jnp.zeros((TILE, TILE), F32)
            for t in range(local + ar_ref.shape[1] // TILE):
                flag = mask_ref[row, t].astype(F32)
                at = t * TILE if t < local else (t - local) * TILE
                tile = (al_ref if t < local else ar_ref)[rows, at : at + TILE].astype(F32) * flag
                if t >= local:
                    back, inside = at // halo + 1, at % halo
                    if back % 2 == 0:
                        to, at = near_ref, (back // 2 - 1) * halo + inside
                    else:
                        slot = ((back + 1) // 2 + 4 - core) % 4
                        to, at = far_ref, pl.multiple_of(slot * halo + inside, TILE)
                elif at < halo:
                    to = head_ref
                elif at < halo + mid:
                    to, at = mid_ref, at - halo
                else:
                    to, at = tail_ref, at - halo - mid
                to[rows, pl.ds(at, TILE)] = tile.astype(BF)
                degree = degree + tile
            whole = jnp.sum(degree, axis=1, keepdims=True)
            scale_ref[rows, :] = jnp.broadcast_to(1.0 / jnp.sqrt(whole), (TILE, TILE))
        at = pl.ds(i * block, block)
        outs += [
            pltpu.make_async_copy(tail_ref.at[at], tail_hbm.at[at], sem.at[2, i]),
            pltpu.make_async_copy(scale_ref.at[at], scale_hbm.at[at], sem.at[3, i]),
        ]
        outs[-2].start()
        outs[-1].start()
    for copy in outs:
        copy.wait()


def mask_tiles(me, tile_mask, adj_local, adj_remote, halo, early):
    rows, n = adj_local.shape
    r = adj_remote.shape[1]
    away = pl.BlockSpec(memory_space=pltpu.HBM)
    return pl.pallas_call(
        mask_kernel,
        grid_spec=pltpu.PrefetchScalarGridSpec(
            num_scalar_prefetch=2,
            grid=(1,),
            in_specs=[away, away],
            out_specs=[
                full((rows, halo)),
                full((rows, early - halo)),
                away,
                full((rows, 3 * halo)),
                full((rows, 4 * halo)),
                away,
            ],
            scratch_shapes=[
                pltpu.VMEM((rows, n), BF),
                pltpu.VMEM((rows, r), BF),
                pltpu.VMEM((rows, n - early), BF),
                pltpu.VMEM((rows, TILE), F32),
                pltpu.SemaphoreType.DMA((4, rows // (2 * TILE))),
            ],
        ),
        out_shape=[
            jax.ShapeDtypeStruct((rows, halo), BF),
            jax.ShapeDtypeStruct((rows, early - halo), BF),
            hbm((rows, n - early), BF),
            jax.ShapeDtypeStruct((rows, 3 * halo), BF),
            jax.ShapeDtypeStruct((rows, 4 * halo), BF),
            hbm((rows, TILE), F32),
        ],
        compiler_params=pltpu.CompilerParams(vmem_limit_bytes=24 << 20),
        name="mask_tiles",
    )(me, tile_mask, in_hbm(adj_local), in_hbm(adj_remote))


def near_kernel(head_ref, near_ref, a, b, c, d, o_ref):
    halo = a.shape[0]
    total = jnp.dot(head_ref[...], a[...], preferred_element_type=F32)
    for i, part in enumerate((b, c, d)):
        at = slice(i * halo, (i + 1) * halo)
        total = total + jnp.dot(near_ref[:, at], part[...], preferred_element_type=F32)
    o_ref[...] = total


def far_kernel(acc_ref, far_ref, a, b, c, d, o_ref):
    halo = a.shape[0]
    total = acc_ref[...]
    for i, part in enumerate((a, b, c, d)):
        at = slice(i * halo, (i + 1) * halo)
        total = total + jnp.dot(far_ref[:, at], part[...], preferred_element_type=F32)
    o_ref[...] = total


def gather_halo(kernel, arrays, parts, out):
    rows = arrays[0].shape[0]
    hid = parts[0].shape[1]
    block = 256
    line = lambda w: pl.BlockSpec((block, w), lambda i: (i, 0))
    return pl.pallas_call(
        kernel,
        grid=(rows // block,),
        in_specs=[line(a.shape[1]) for a in arrays] + [full(p.shape) for p in parts],
        out_specs=line(hid),
        out_shape=out((rows, hid), F32),
        compiler_params=VM,
    )(*arrays, *parts)


def last_kernel(x_ref, wt_ref, tail_hbm, acc_hbm, scale_hbm, self_hbm, bias_ref, o_hbm,
                s_ref, tail_ref, acc_ref, scale_ref, o_ref, sem):
    rows, hid = acc_ref.shape
    early, block = self_hbm.shape[0], 256
    ins = []
    for i in range(rows // block):
        at = pl.ds(i * block, block)
        some = [
            pltpu.make_async_copy(tail_hbm.at[at], tail_ref.at[at], sem.at[0, i]),
            pltpu.make_async_copy(acc_hbm.at[at], acc_ref.at[at], sem.at[1, i]),
            pltpu.make_async_copy(scale_hbm.at[at], scale_ref.at[at], sem.at[2, i]),
        ]
        if i == 0:
            some.append(pltpu.make_async_copy(self_hbm, s_ref.at[pl.ds(0, early)], sem.at[3, 0]))
        for copy in some:
            copy.start()
        ins.append(some)
    ht = jnp.dot(wt_ref[hid:, :], x_ref[...], preferred_element_type=F32).astype(BF)
    s_ref[early:, :] = jnp.dot(wt_ref[:hid, :], x_ref[...], preferred_element_type=F32).T
    last = (((1,), (1,)), ((), ()))
    outs = []
    for i in range(rows // block):
        for copy in ins[i]:
            copy.wait()
        at = slice(i * block, (i + 1) * block)
        more = lax.dot_general(tail_ref[at, :], ht, last, preferred_element_type=F32)
        scale = jnp.concatenate([scale_ref[at, :]] * (hid // TILE), axis=1)
        o_ref[at, :] = jnp.maximum(
            s_ref[at, :] + (acc_ref[at, :] + more) * scale + bias_ref[...], 0.0
        ).astype(BF)
        at = pl.ds(i * block, block)
        outs.append(pltpu.make_async_copy(o_ref.at[at], o_hbm.at[at], sem.at[4, i]))
        outs[-1].start()
    for copy in outs:
        copy.wait()


def last_step(x, turned, tail, acc, scale, self_early, bias):
    rows, hid = acc.shape
    away = pl.BlockSpec(memory_space=pltpu.HBM)
    return pl.pallas_call(
        last_kernel,
        grid=(1,),
        in_specs=[full(x.shape), full(turned.shape)] + [away] * 4 + [full(bias.shape)],
        out_specs=away,
        scratch_shapes=[
            pltpu.VMEM((rows, hid), F32),
            pltpu.VMEM(tail.shape, BF),
            pltpu.VMEM(acc.shape, F32),
            pltpu.VMEM(scale.shape, F32),
            pltpu.VMEM((rows, hid), BF),
            pltpu.SemaphoreType.DMA((5, rows // 256)),
        ],
        out_shape=jax.ShapeDtypeStruct((rows, hid), BF),
        compiler_params=VM,
        name="last_step",
    )(x, turned, *(in_hbm(a) for a in (tail, acc, scale, self_early)), bias)


def shards(features, adj_local, adj_remote, tile_mask, w_self, w_neigh, out_bias):
    halo = adj_remote.shape[1] // (lax.axis_size("blk") - 1)
    me = lax.axis_index(("feat", "blk")).reshape(1)
    features = in_hbm(features)

    head = split_head(me, features, EARLY)
    landed = [head[0]]
    for dz in range(1, NZ):
        landed.append(lax.ppermute(head[dz], "feat", feat_shift(dz, 0)))
    rest = split_tail(features, EARLY)
    rest = lax.all_to_all(rest, "feat", split_axis=0, concat_axis=0, tiled=True)
    rest = rest.reshape(-1, rest.shape[-1])

    rot, turned = weights(me, w_self, w_neigh)
    live_head, live_mid, live_tail, live_near, live_far, scale = mask_tiles(
        me, tile_mask, adj_local, adj_remote, halo, EARLY
    )
    rows = regroup(landed, halo)
    parts, mids = [rows[0]], [rows[NX]]
    for j in range(1, NX):
        parts.append(lax.ppermute(rows[j], "feat", feat_shift(0, j)))
        mids.append(lax.ppermute(rows[NX + j], "feat", feat_shift(0, j)))
    h_head = halo_hidden(parts, rot)
    same = [h_head]
    for dy in (1, 2, 3):
        same.append(lax.ppermute(h_head, "blk", blk_shift(dy, 0)))
    other = [lax.ppermute(h, "blk", blk_shift(0, 1)) for h in same]
    acc = gather_halo(near_kernel, (live_head, live_near), same, jax.ShapeDtypeStruct)
    self_early, acc = mid_hidden(parts, mids, rot, live_mid, acc)
    acc = gather_halo(far_kernel, (acc, live_far), other, hbm)
    return last_step(rest, turned, live_tail, acc, scale, self_early, out_bias[None, :])


def solution(mesh):
    placed = (
        P("feat", None, "blk"),
        P(("feat", "blk"), None),
        P(("feat", "blk"), None),
        P(("feat", "blk"), None),
        P(),
        P(),
        P(),
    )

    return jax.shard_map(
        shards, mesh=mesh, in_specs=placed, out_specs=P(("feat", "blk"), None), check_vma=False
    )
```

time: 114 us -> 99.9 us (0.88)
  the two profiles are of different devices: /device:TPU:2 before, /device:TPU:1 now
where the time goes in v3:
time: 99.9 us; the launch traced here: 99.6 us
  starting transfers between devices  45.6 us (46%)
  waiting for transfers between devices  33.7 us (34%)
  Pallas kernels  20 us (20%)
    ppermute x7, waiting for transfers between devices, shards(): landed.append(lax.ppermute(head[dz], 'feat', feat_shift(dz, 0)))  32.4 us
    ppermute x7, starting transfers between devices, shards(): landed.append(lax.ppermute(head[dz], 'feat', feat_shift(dz, 0)))  14.1 us
    all_to_all x1, starting transfers between devices, shards(): rest = lax.all_to_all(rest, 'feat', split_axis=0, concat_axis=0, tiled=True)  11.9 us
    ppermute x3, starting transfers between devices, shards(): parts.append(lax.ppermute(rows[j], 'feat', feat_shift(0, j)))  5.21 us
    ppermute x4, starting transfers between devices, shards(): other = [lax.ppermute(h, 'blk', blk_shift(0, 1)) for h in same]  5.09 us
    ppermute x3, starting transfers between devices, shards(): same.append(lax.ppermute(h_head, 'blk', blk_shift(dy, 0)))  5.06 us
    pallas_call x1, Pallas kernels, mask_tiles(): pl.pallas_call(mask_kernel, grid_spec=pltpu.PrefetchScalarGridSpec(num_sc...  4.95 us
    ppermute x3, starting transfers between devices, shards(): mids.append(lax.ppermute(rows[NX + j], 'feat', feat_shift(0, j)))  4.25 us
  transfers between devices with their start and end apart: 21, of which 7 were waited for; matrix products, arithmetic and copies ran while one was open for 0% of the time, Pallas kernels for 14%

profile of v3, /device:TPU:1, one launch (start us, length us, event | category | flops | bytes accessed | tf_op | source)
XLA Modules:
  0.0 99.6 jit_solution(1530033949491149600)
XLA Ops:
  0.0 2.5 %split_tail.1 = bf16[32,32,512]{2,1,0:T(8,128)(2,1)} custom-call(bf16[32,32,1024]{2,1,0:T(8,128)(2,1)} %x_ref.1), custom_call_target="tpu_custom_call" | custom-call | tf_op jit(solution)/shard_map/split_tail/pallas_call | solution.py:119
  2.5 11.9 %all-to-all-start = ((bf16[32,32,512]{2,1,0:T(8,128)(2,1)}), bf16[32,32,512]{2,1,0:T(8,128)(2,1)S(1)}, u32[]{:S(2)}, u32[]{:S(2)}) async-start(bf16[32,32,512]{2,1,0:T(8,128)(2,1)} %split_tail.1), calls=%async_computation | async-start | bytes 2097152 | tf_op jit(solution)/shard_map/all_to_all | solution.py:457
  14.4 1.7 %split_head.1 = (bf16[4,32,512]{2,1,0:T(8,128)(2,1)S(1)}, bf16[4,32,512]{2,1,0:T(8,128)(2,1)S(1)}, bf16[4,32,512]{2,1,0:T(8,128)(2,1)S(1)}, bf16[4,32,512]{2,1,0...) custom-call(s32[1]{0:T(128)} %bitcast.1.me_ref, ...), custom_call_target="tpu_custom_call" | custom-call | tf_op jit(solution)/shard_map/split_head/pallas_call | solution.py:75
  16.1 0.0 copy-start
  16.1 1.3 %collective-permute-start = (bf16[4,32,512]{2,1,0:T(8,128)(2,1)S(1)}, bf16[4,32,512]{2,1,0:T(8,128)(2,1)S(1)}, u32[]{:S(2)}, u32[]{:S(2)}) collective-permute-start(bf16[4,32,512]{2,1,0:T(8,128)(2,1)S(1)} %get-tuple-element.34), channel_id=1, source_target_pairs={{0,32},{8,40},{16,48},{24,56},{32,64},{40,72},{48,80},{56,88},{64,... | collective-permute-start | bytes 393224 | tf_op jit(solution)/shard_map/ppermute | solution.py:455
  17.5 2.1 %collective-permute-start.1 = (bf16[4,32,512]{2,1,0:T(8,128)(2,1)S(1)}, bf16[4,32,512]{2,1,0:T(8,128)(2,1)S(1)}, u32[]{:S(2)}, u32[]{:S(2)}) collective-permute-start(bf16[4,32,512]{2,1,0:T(8,128)(2,1)S(1)} %get-tuple-element.35), channel_id=1, source_target_pairs={{0,64},{8,72},{16,80},{24,88},{32,96},{40,104},{48,112},{56,120},{... | collective-permute-start | bytes 393224 | tf_op jit(solution)/shard_map/ppermute | solution.py:455
  19.6 2.4 %collective-permute-start.2 = (bf16[4,32,512]{2,1,0:T(8,128)(2,1)S(1)}, bf16[4,32,512]{2,1,0:T(8,128)(2,1)S(1)}, u32[]{:S(2)}, u32[]{:S(2)}) collective-permute-start(bf16[4,32,512]{2,1,0:T(8,128)(2,1)S(1)} %get-tuple-element.36), channel_id=1, source_target_pairs={{0,96},{8,104},{16,112},{24,120},{32,128},{40,136},{48,144},{56,15... | collective-permute-start | bytes 393224 | tf_op jit(solution)/shard_map/ppermute | solution.py:455
  22.0 2.0 %collective-permute-start.3 = (bf16[4,32,512]{2,1,0:T(8,128)(2,1)S(1)}, bf16[4,32,512]{2,1,0:T(8,128)(2,1)S(1)}, u32[]{:S(2)}, u32[]{:S(2)}) collective-permute-start(bf16[4,32,512]{2,1,0:T(8,128)(2,1)S(1)} %get-tuple-element.37), channel_id=1, source_target_pairs={{0,128},{8,136},{16,144},{24,152},{32,160},{40,168},{48,176},{56,1... | collective-permute-start | bytes 393224 | tf_op jit(solution)/shard_map/ppermute | solution.py:455
  24.0 2.5 %collective-permute-start.4 = (bf16[4,32,512]{2,1,0:T(8,128)(2,1)S(1)}, bf16[4,32,512]{2,1,0:T(8,128)(2,1)S(1)}, u32[]{:S(2)}, u32[]{:S(2)}) collective-permute-start(bf16[4,32,512]{2,1,0:T(8,128)(2,1)S(1)} %get-tuple-element.38), channel_id=1, source_target_pairs={{0,160},{8,168},{16,176},{24,184},{32,192},{40,200},{48,208},{56,2... | collective-permute-start | bytes 393224 | tf_op jit(solution)/shard_map/ppermute | solution.py:455
  26.5 15.5 %collective-permute-done.refs_1_ = bf16[4,32,512]{2,1,0:T(8,128)(2,1)S(1)} collective-permute-done((bf16[4,32,512]{2,1,0:T(8,128)(2,1)S(1)}, bf16[4,32,512]{2,1,0:T(8,128)(2,1)S(1)}, u32[]{:S(2)}, u32[]{:S(2)}) %collective-permute-start) | collective-permute-done | bytes 131104 | tf_op jit(solution)/shard_map/ppermute | solution.py:455
  42.0 2.2 %collective-permute-start.5 = (bf16[4,32,512]{2,1,0:T(8,128)(2,1)S(1)}, bf16[4,32,512]{2,1,0:T(8,128)(2,1)S(1)}, u32[]{:S(2)}, u32[]{:S(2)}) collective-permute-start(bf16[4,32,512]{2,1,0:T(8,128)(2,1)S(1)} %get-tuple-element.39), channel_id=1, source_target_pairs={{0,192},{8,200},{16,208},{24,216},{32,224},{40,232},{48,240},{56,2... | collective-permute-start | bytes 393224 | tf_op jit(solution)/shard_map/ppermute | solution.py:455
  44.2 3.1 %collective-permute-done.1.refs_2_ = bf16[4,32,512]{2,1,0:T(8,128)(2,1)S(1)} collective-permute-done((bf16[4,32,512]{2,1,0:T(8,128)(2,1)S(1)}, bf16[4,32,512]{2,1,0:T(8,128)(2,1)S(1)}, u32[]{:S(2)}, u32[]{:S(2)}) %collective-permute-start.1) | collective-permute-done | bytes 131104 | tf_op jit(solution)/shard_map/ppermute | solution.py:455
  47.3 1.6 %collective-permute-start.6 = (bf16[4,32,512]{2,1,0:T(8,128)(2,1)S(1)}, bf16[4,32,512]{2,1,0:T(8,128)(2,1)S(1)}, u32[]{:S(2)}, u32[]{:S(2)}) collective-permute-start(bf16[4,32,512]{2,1,0:T(8,128)(2,1)S(1)} %get-tuple-element.40), channel_id=1, source_target_pairs={{0,224},{8,232},{16,240},{24,248},{32,0},{40,8},{48,16},{56,24},{6... | collective-permute-start | bytes 393224 | tf_op jit(solution)/shard_map/ppermute | solution.py:455
  48.9 7.0 %collective-permute-done.2.refs_3_ = bf16[4,32,512]{2,1,0:T(8,128)(2,1)S(1)} collective-permute-done((bf16[4,32,512]{2,1,0:T(8,128)(2,1)S(1)}, bf16[4,32,512]{2,1,0:T(8,128)(2,1)S(1)}, u32[]{:S(2)}, u32[]{:S(2)}) %collective-permute-start.2) | collective-permute-done | bytes 131104 | tf_op jit(solution)/shard_map/ppermute | solution.py:455
  56.0 6.7 %collective-permute-done.3.refs_4_ = bf16[4,32,512]{2,1,0:T(8,128)(2,1)S(1)} collective-permute-done((bf16[4,32,512]{2,1,0:T(8,128)(2,1)S(1)}, bf16[4,32,512]{2,1,0:T(8,128)(2,1)S(1)}, u32[]{:S(2)}, u32[]{:S(2)}) %collective-permute-start.3) | collective-permute-done | bytes 131104 | tf_op jit(solution)/shard_map/ppermute | solution.py:455
  62.6 0.0 collective-permute-done.4.refs_5_
  62.6 0.0 collective-permute-done.5.refs_6_
  62.7 0.0 collective-permute-done.6.refs_7_
  62.7 0.1 regroup.1
  62.7 1.7 %collective-permute-start.7 = (bf16[256,256]{1,0:T(8,128)(2,1)S(1)}, bf16[256,256]{1,0:T(8,128)(2,1)S(1)}, u32[]{:S(2)}, u32[]{:S(2)}) collective-permute-start(bf16[256,256]{1,0:T(8,128)(2,1)S(1)} %get-tuple-element.42), channel_id=1, source_target_pairs={{0,8},{8,16},{16,24},{24,0},{32,40},{40,48},{48,56},{56,32},{64,72... | collective-permute-start | bytes 393224 | tf_op jit(solution)/shard_map/ppermute | solution.py:467
  64.5 2.3 %collective-permute-start.8 = (bf16[256,256]{1,0:T(8,128)(2,1)S(1)}, bf16[256,256]{1,0:T(8,128)(2,1)S(1)}, u32[]{:S(2)}, u32[]{:S(2)}) collective-permute-start(bf16[256,256]{1,0:T(8,128)(2,1)S(1)} %get-tuple-element.43), channel_id=1, source_target_pairs={{0,16},{8,24},{16,0},{24,8},{32,48},{40,56},{48,32},{56,40},{64,80... | collective-permute-start | bytes 393224 | tf_op jit(solution)/shard_map/ppermute | solution.py:467
  66.8 1.2 %collective-permute-start.9 = (bf16[256,256]{1,0:T(8,128)(2,1)S(1)}, bf16[256,256]{1,0:T(8,128)(2,1)S(1)}, u32[]{:S(2)}, u32[]{:S(2)}) collective-permute-start(bf16[256,256]{1,0:T(8,128)(2,1)S(1)} %get-tuple-element.44), channel_id=1, source_target_pairs={{0,24},{8,0},{16,8},{24,16},{32,56},{40,32},{48,40},{56,48},{64,88... | collective-permute-start | bytes 393224 | tf_op jit(solution)/shard_map/ppermute | solution.py:467
  67.9 1.5 %weights.1 = (bf16[1024,512]{1,0:T(8,128)(2,1)S(1)}, bf16[512,1024]{1,0:T(8,128)(2,1)S(1)}) custom-call(s32[1]{0:T(128)} %bitcast.1.me_ref, bf16[1024,256]{1,0:T(8,128)(2,1)} %ws_hbm.1, bf16[1024,256]{1,0:T(8,128)(2,1)} %wn_hbm.1), custom_call_target="tpu_custom_call" | custom-call | tf_op jit(solution)/shard_map/weights/pallas_call | solution.py:182
  69.4 0.4 collective-permute-start.10
  69.8 0.9 collective-permute-start.11
  70.7 0.0 collective-permute-done.7.b.refs_1_
  70.7 1.0 %collective-permute-done.8.c.refs_2_ = bf16[256,256]{1,0:T(8,128)(2,1)S(1)} collective-permute-done((bf16[256,256]{1,0:T(8,128)(2,1)S(1)}, bf16[256,256]{1,0:T(8,128)(2,1)S(1)}, u32[]{:S(2)}, u32[]{:S(2)}) %collective-permute-start.8) | collective-permute-done | bytes 131104 | tf_op jit(solution)/shard_map/ppermute | solution.py:467
  71.7 0.2 collective-permute-done.9.d.refs_3_
  71.9 0.3 halo_hidden.1.a
  72.3 1.4 %collective-permute-start.13 = (bf16[256,256]{1,0:T(8,128)(2,1)S(1)}, bf16[256,256]{1,0:T(8,128)(2,1)S(1)}, u32[]{:S(2)}, u32[]{:S(2)}) collective-permute-start(bf16[256,256]{1,0:T(8,128)(2,1)S(1)} %halo_hidden.1.a), channel_id=1, source_target_pairs={{0,2},{1,3},{2,4},{3,5},{4,6},{5,7},{6,0},{7,1},{8,10},{9,11},{10,... | collective-permute-start | bytes 393224 | tf_op jit(solution)/shard_map/ppermute | solution.py:472
  73.6 2.6 %collective-permute-start.14 = (bf16[256,256]{1,0:T(8,128)(2,1)S(1)}, bf16[256,256]{1,0:T(8,128)(2,1)S(1)}, u32[]{:S(2)}, u32[]{:S(2)}) collective-permute-start(bf16[256,256]{1,0:T(8,128)(2,1)S(1)} %halo_hidden.1.a), channel_id=1, source_target_pairs={{0,4},{1,5},{2,6},{3,7},{4,0},{5,1},{6,2},{7,3},{8,12},{9,13},{10,... | collective-permute-start | bytes 393224 | tf_op jit(solution)/shard_map/ppermute | solution.py:472
  76.3 1.1 %collective-permute-start.15 = (bf16[256,256]{1,0:T(8,128)(2,1)S(1)}, bf16[256,256]{1,0:T(8,128)(2,1)S(1)}, u32[]{:S(2)}, u32[]{:S(2)}) collective-permute-start(bf16[256,256]{1,0:T(8,128)(2,1)S(1)} %halo_hidden.1.a), channel_id=1, source_target_pairs={{0,6},{1,7},{2,0},{3,1},{4,2},{5,3},{6,4},{7,5},{8,14},{9,15},{10,... | collective-permute-start | bytes 393224 | tf_op jit(solution)/shard_map/ppermute | solution.py:472
  77.3 0.1 collective-permute-done.10.refs_5_
  77.4 3.0 %collective-permute-start.12 = (bf16[256,256]{1,0:T(8,128)(2,1)S(1)}, bf16[256,256]{1,0:T(8,128)(2,1)S(1)}, u32[]{:S(2)}, u32[]{:S(2)}) collective-permute-start(bf16[256,256]{1,0:T(8,128)(2,1)S(1)} %get-tuple-element.48), channel_id=1, source_target_pairs={{0,24},{8,0},{16,8},{24,16},{32,56},{40,32},{48,40},{56,48},{64,88... | collective-permute-start | bytes 393224 | tf_op jit(solution)/shard_map/ppermute | solution.py:468
  80.4 0.0 collective-permute-done.11.refs_6_
  80.4 2.6 %collective-permute-start.16 = (bf16[256,256]{1,0:T(8,128)(2,1)S(1)}, bf16[256,256]{1,0:T(8,128)(2,1)S(1)}, u32[]{:S(2)}, u32[]{:S(2)}) collective-permute-start(bf16[256,256]{1,0:T(8,128)(2,1)S(1)} %halo_hidden.1.a), channel_id=1, source_target_pairs={{0,1},{1,0},{2,3},{3,2},{4,5},{5,4},{6,7},{7,6},{8,9},{9,8},{10,11... | collective-permute-start | bytes 393224 | tf_op jit(solution)/shard_map/ppermute | solution.py:473
  83.0 0.0 collective-permute-done.13.b
  83.0 0.1 collective-permute-start.17
  83.1 1.8 %collective-permute-start.18 = (bf16[256,256]{1,0:T(8,128)(2,1)S(1)}, bf16[256,256]{1,0:T(8,128)(2,1)S(1)}, u32[]{:S(2)}, u32[]{:S(2)}) collective-permute-start(bf16[256,256]{1,0:T(8,128)(2,1)S(1)} %collective-permute-done.14.c), channel_id=1, source_target_pairs={{0,1},{1,0},{2,3},{3,2},{4,5},{5,4},{6,7},{7,6},{8,9},{9,8},{10,11... | collective-permute-start | bytes 393224 | tf_op jit(solution)/shard_map/ppermute | solution.py:473
  84.9 0.0 collective-permute-done.15.d
  84.9 0.6 collective-permute-start.19
  85.5 4.9 %mask_tiles.1 = (bf16[1024,256]{1,0:T(8,128)(2,1)S(1)}, bf16[1024,256]{1,0:T(8,128)(2,1)S(1)}, bf16[1024,512]{1,0:T(8,128)(2,1)}, bf16[1024,768]{1,0:T(8,128)(2,...) custom-call(s32[1]{0:T(128)} %bitcast.1.me_ref, s32[8,22]{1,0:T(8,128)S(1)} %copy-done, ...), custom_call_target="tpu_custom_call" | custom-call | tf_op jit(solution)/shard_map/mask_tiles/pallas_call | solution.py:320
  90.4 1.3 %shard_map.73.refs_10_ = f32[1024,256]{1,0:T(8,128)S(1)} custom-call(bf16[1024,256]{1,0:T(8,128)(2,1)S(1)} %get-tuple-element.51.head_ref, bf16[1024,768]{1,0:T(8,128)(2,1)S(1)} %get-tuple-element.52.near_ref, bf16[256,256]{1,0:T(8,128)(2,1)S(1)} %halo_hidden.1.a, bf16[256,256]{1,0:T(8,128)(2,1)S(1)} %collective-permute-done.13.b, ...), custom_call_target="tpu_custom_call" | custom-call | tf_op jit(solution)/shard_map/pallas_call | solution.py:378
  91.7 1.9 %mid_hidden.1 = (f32[512,256]{1,0:T(8,128)}, f32[1024,256]{1,0:T(8,128)S(1)}) custom-call(bf16[256,256]{1,0:T(8,128)(2,1)S(1)} %get-tuple-element.41.a.refs_0_, bf16[256,256]{1,0:T(8,128)(2,1)S(1)} %collective-permute-done.7.b.refs_1_, bf16[256,256]{1,0:T(8,128)(2,1)S(1)} %collective-permute-done.8.c.refs_2_, ...), custom_call_target="tpu_custom_call" | custom-call | tf_op jit(solution)/shard_map/mid_hidden/pallas_call | solution.py:250
  93.6 0.0 collective-permute-done.18.c
  93.6 0.0 copy-start.1
  93.6 2.4 %shard_map.74.acc_hbm = f32[1024,256]{1,0:T(8,128)} custom-call(f32[1024,256]{1,0:T(8,128)S(1)} %get-tuple-element.53.acc_ref, bf16[1024,1024]{1,0:T(8,128)(2,1)S(1)} %get-tuple-element.54.far_ref, bf16[256,256]{1,0:T(8,128)(2,1)S(1)} %collective-permute-done.16.a, bf16[256,256]{1,0:T(8,128)(2,1)S(1)} %collective-permute-done.17.b, ...), custom_call_target="tpu_custom_call" | custom-call | tf_op jit(solution)/shard_map/pallas_call | solution.py:378
  96.0 3.4 %last_step.1 = bf16[1024,256]{1,0:T(8,128)(2,1)} custom-call(bf16[1024,512]{1,0:T(8,128)(2,1)S(1)} %bitcast.3, bf16[512,1024]{1,0:T(8,128)(2,1)S(1)} %get-tuple-element.31.wt_ref, bf16[1024,512]{1,0:T(8,128)(2,1)} %get-tuple-element.32.tail_hbm, f32[1024,256]{1,0:T(8,128)} %shard_map.74.acc_hbm, f32[1024,128]{1,0:T(8,128)} %get-tuple-element.55.scale_hbm, ...), custom_call_target="tpu_custom_call" | custom-call | tf_op jit(solution)/shard_map/last_step/pallas_call | solution.py:428
  (8 shorter events, 0.0 us)
Async XLA Ops:
  2.5 93.5 %all-to-all-start = ((bf16[32,32,512]{2,1,0:T(8,128)(2,1)}), bf16[32,32,512]{2,1,0:T(8,128)(2,1)S(1)}, u32[]{:S(2)}, u32[]{:S(2)}) async-start(bf16[32,32,512]{2,1,0:T(8,128)(2,1)} %split_tail.1), calls=%async_computation | async-start | bytes 2097152 | tf_op jit(solution)/shard_map/all_to_all | solution.py:457
  16.1 69.4 %copy-start = (s32[8,22]{1,0:T(8,128)S(1)}, s32[8,22]{1,0:T(8,128)}, u32[]{:S(2)}) copy-start(s32[8,22]{1,0:T(8,128)} %mask_ref.1) | copy-start | bytes 2116
  16.1 25.9 %collective-permute-start = (bf16[4,32,512]{2,1,0:T(8,128)(2,1)S(1)}, bf16[4,32,512]{2,1,0:T(8,128)(2,1)S(1)}, u32[]{:S(2)}, u32[]{:S(2)}) collective-permute-start(bf16[4,32,512]{2,1,0:T(8,128)(2,1)S(1)} %get-tuple-element.34), channel_id=1, source_target_pairs={{0,32},{8,40},{16,48},{24,56},{32,64},{40,72},{48,80},{56,88},{64,... | collective-permute-start | bytes 393224 | tf_op jit(solution)/shard_map/ppermute | solution.py:455
  17.5 29.9 %collective-permute-start.1 = (bf16[4,32,512]{2,1,0:T(8,128)(2,1)S(1)}, bf16[4,32,512]{2,1,0:T(8,128)(2,1)S(1)}, u32[]{:S(2)}, u32[]{:S(2)}) collective-permute-start(bf16[4,32,512]{2,1,0:T(8,128)(2,1)S(1)} %get-tuple-element.35), channel_id=1, source_target_pairs={{0,64},{8,72},{16,80},{24,88},{32,96},{40,104},{48,112},{56,120},{... | collective-permute-start | bytes 393224 | tf_op jit(solution)/shard_map/ppermute | solution.py:455
  19.6 36.4 %collective-permute-start.2 = (bf16[4,32,512]{2,1,0:T(8,128)(2,1)S(1)}, bf16[4,32,512]{2,1,0:T(8,128)(2,1)S(1)}, u32[]{:S(2)}, u32[]{:S(2)}) collective-permute-start(bf16[4,32,512]{2,1,0:T(8,128)(2,1)S(1)} %get-tuple-element.36), channel_id=1, source_target_pairs={{0,96},{8,104},{16,112},{24,120},{32,128},{40,136},{48,144},{56,15... | collective-permute-start | bytes 393224 | tf_op jit(solution)/shard_map/ppermute | solution.py:455
  22.0 40.7 %collective-permute-start.3 = (bf16[4,32,512]{2,1,0:T(8,128)(2,1)S(1)}, bf16[4,32,512]{2,1,0:T(8,128)(2,1)S(1)}, u32[]{:S(2)}, u32[]{:S(2)}) collective-permute-start(bf16[4,32,512]{2,1,0:T(8,128)(2,1)S(1)} %get-tuple-element.37), channel_id=1, source_target_pairs={{0,128},{8,136},{16,144},{24,152},{32,160},{40,168},{48,176},{56,1... | collective-permute-start | bytes 393224 | tf_op jit(solution)/shard_map/ppermute | solution.py:455
  24.0 38.6 %collective-permute-start.4 = (bf16[4,32,512]{2,1,0:T(8,128)(2,1)S(1)}, bf16[4,32,512]{2,1,0:T(8,128)(2,1)S(1)}, u32[]{:S(2)}, u32[]{:S(2)}) collective-permute-start(bf16[4,32,512]{2,1,0:T(8,128)(2,1)S(1)} %get-tuple-element.38), channel_id=1, source_target_pairs={{0,160},{8,168},{16,176},{24,184},{32,192},{40,200},{48,208},{56,2... | collective-permute-start | bytes 393224 | tf_op jit(solution)/shard_map/ppermute | solution.py:455
  42.0 20.6 %collective-permute-start.5 = (bf16[4,32,512]{2,1,0:T(8,128)(2,1)S(1)}, bf16[4,32,512]{2,1,0:T(8,128)(2,1)S(1)}, u32[]{:S(2)}, u32[]{:S(2)}) collective-permute-start(bf16[4,32,512]{2,1,0:T(8,128)(2,1)S(1)} %get-tuple-element.39), channel_id=1, source_target_pairs={{0,192},{8,200},{16,208},{24,216},{32,224},{40,232},{48,240},{56,2... | collective-permute-start | bytes 393224 | tf_op jit(solution)/shard_map/ppermute | solution.py:455
  47.3 15.3 %collective-permute-start.6 = (bf16[4,32,512]{2,1,0:T(8,128)(2,1)S(1)}, bf16[4,32,512]{2,1,0:T(8,128)(2,1)S(1)}, u32[]{:S(2)}, u32[]{:S(2)}) collective-permute-start(bf16[4,32,512]{2,1,0:T(8,128)(2,1)S(1)} %get-tuple-element.40), channel_id=1, source_target_pairs={{0,224},{8,232},{16,240},{24,248},{32,0},{40,8},{48,16},{56,24},{6... | collective-permute-start | bytes 393224 | tf_op jit(solution)/shard_map/ppermute | solution.py:455
  62.7 8.0 %collective-permute-start.7 = (bf16[256,256]{1,0:T(8,128)(2,1)S(1)}, bf16[256,256]{1,0:T(8,128)(2,1)S(1)}, u32[]{:S(2)}, u32[]{:S(2)}) collective-permute-start(bf16[256,256]{1,0:T(8,128)(2,1)S(1)} %get-tuple-element.42), channel_id=1, source_target_pairs={{0,8},{8,16},{16,24},{24,0},{32,40},{40,48},{48,56},{56,32},{64,72... | collective-permute-start | bytes 393224 | tf_op jit(solution)/shard_map/ppermute | solution.py:467
  64.5 7.2 %collective-permute-start.8 = (bf16[256,256]{1,0:T(8,128)(2,1)S(1)}, bf16[256,256]{1,0:T(8,128)(2,1)S(1)}, u32[]{:S(2)}, u32[]{:S(2)}) collective-permute-start(bf16[256,256]{1,0:T(8,128)(2,1)S(1)} %get-tuple-element.43), channel_id=1, source_target_pairs={{0,16},{8,24},{16,0},{24,8},{32,48},{40,56},{48,32},{56,40},{64,80... | collective-permute-start | bytes 393224 | tf_op jit(solution)/shard_map/ppermute | solution.py:467
  66.8 5.2 %collective-permute-start.9 = (bf16[256,256]{1,0:T(8,128)(2,1)S(1)}, bf16[256,256]{1,0:T(8,128)(2,1)S(1)}, u32[]{:S(2)}, u32[]{:S(2)}) collective-permute-start(bf16[256,256]{1,0:T(8,128)(2,1)S(1)} %get-tuple-element.44), channel_id=1, source_target_pairs={{0,24},{8,0},{16,8},{24,16},{32,56},{40,32},{48,40},{56,48},{64,88... | collective-permute-start | bytes 393224 | tf_op jit(solution)/shard_map/ppermute | solution.py:467
  69.4 8.0 %collective-permute-start.10 = (bf16[256,256]{1,0:T(8,128)(2,1)S(1)}, bf16[256,256]{1,0:T(8,128)(2,1)S(1)}, u32[]{:S(2)}, u32[]{:S(2)}) collective-permute-start(bf16[256,256]{1,0:T(8,128)(2,1)S(1)} %get-tuple-element.46), channel_id=1, source_target_pairs={{0,8},{8,16},{16,24},{24,0},{32,40},{40,48},{48,56},{56,32},{64,72... | collective-permute-start | bytes 393224 | tf_op jit(solution)/shard_map/ppermute | solution.py:468
  69.8 10.6 %collective-permute-start.11 = (bf16[256,256]{1,0:T(8,128)(2,1)S(1)}, bf16[256,256]{1,0:T(8,128)(2,1)S(1)}, u32[]{:S(2)}, u32[]{:S(2)}) collective-permute-start(bf16[256,256]{1,0:T(8,128)(2,1)S(1)} %get-tuple-element.47), channel_id=1, source_target_pairs={{0,16},{8,24},{16,0},{24,8},{32,48},{40,56},{48,32},{56,40},{64,80... | collective-permute-start | bytes 393224 | tf_op jit(solution)/shard_map/ppermute | solution.py:468
  72.3 10.8 %collective-permute-start.13 = (bf16[256,256]{1,0:T(8,128)(2,1)S(1)}, bf16[256,256]{1,0:T(8,128)(2,1)S(1)}, u32[]{:S(2)}, u32[]{:S(2)}) collective-permute-start(bf16[256,256]{1,0:T(8,128)(2,1)S(1)} %halo_hidden.1.a), channel_id=1, source_target_pairs={{0,2},{1,3},{2,4},{3,5},{4,6},{5,7},{6,0},{7,1},{8,10},{9,11},{10,... | collective-permute-start | bytes 393224 | tf_op jit(solution)/shard_map/ppermute | solution.py:472
  73.6 9.5 %collective-permute-start.14 = (bf16[256,256]{1,0:T(8,128)(2,1)S(1)}, bf16[256,256]{1,0:T(8,128)(2,1)S(1)}, u32[]{:S(2)}, u32[]{:S(2)}) collective-permute-start(bf16[256,256]{1,0:T(8,128)(2,1)S(1)} %halo_hidden.1.a), channel_id=1, source_target_pairs={{0,4},{1,5},{2,6},{3,7},{4,0},{5,1},{6,2},{7,3},{8,12},{9,13},{10,... | collective-permute-start | bytes 393224 | tf_op jit(solution)/shard_map/ppermute | solution.py:472
  76.3 8.6 %collective-permute-start.15 = (bf16[256,256]{1,0:T(8,128)(2,1)S(1)}, bf16[256,256]{1,0:T(8,128)(2,1)S(1)}, u32[]{:S(2)}, u32[]{:S(2)}) collective-permute-start(bf16[256,256]{1,0:T(8,128)(2,1)S(1)} %halo_hidden.1.a), channel_id=1, source_target_pairs={{0,6},{1,7},{2,0},{3,1},{4,2},{5,3},{6,4},{7,5},{8,14},{9,15},{10,... | collective-permute-start | bytes 393224 | tf_op jit(solution)/shard_map/ppermute | solution.py:472
  77.4 14.3 %collective-permute-start.12 = (bf16[256,256]{1,0:T(8,128)(2,1)S(1)}, bf16[256,256]{1,0:T(8,128)(2,1)S(1)}, u32[]{:S(2)}, u32[]{:S(2)}) collective-permute-start(bf16[256,256]{1,0:T(8,128)(2,1)S(1)} %get-tuple-element.48), channel_id=1, source_target_pairs={{0,24},{8,0},{16,8},{24,16},{32,56},{40,32},{48,40},{56,48},{64,88... | collective-permute-start | bytes 393224 | tf_op jit(solution)/shard_map/ppermute | solution.py:468
  80.4 13.2 %collective-permute-start.16 = (bf16[256,256]{1,0:T(8,128)(2,1)S(1)}, bf16[256,256]{1,0:T(8,128)(2,1)S(1)}, u32[]{:S(2)}, u32[]{:S(2)}) collective-permute-start(bf16[256,256]{1,0:T(8,128)(2,1)S(1)} %halo_hidden.1.a), channel_id=1, source_target_pairs={{0,1},{1,0},{2,3},{3,2},{4,5},{5,4},{6,7},{7,6},{8,9},{9,8},{10,11... | collective-permute-start | bytes 393224 | tf_op jit(solution)/shard_map/ppermute | solution.py:473
  83.0 10.6 %collective-permute-start.17 = (bf16[256,256]{1,0:T(8,128)(2,1)S(1)}, bf16[256,256]{1,0:T(8,128)(2,1)S(1)}, u32[]{:S(2)}, u32[]{:S(2)}) collective-permute-start(bf16[256,256]{1,0:T(8,128)(2,1)S(1)} %collective-permute-done.13.b), channel_id=1, source_target_pairs={{0,1},{1,0},{2,3},{3,2},{4,5},{5,4},{6,7},{7,6},{8,9},{9,8},{10,11... | collective-permute-start | bytes 393224 | tf_op jit(solution)/shard_map/ppermute | solution.py:473
  83.1 10.5 %collective-permute-start.18 = (bf16[256,256]{1,0:T(8,128)(2,1)S(1)}, bf16[256,256]{1,0:T(8,128)(2,1)S(1)}, u32[]{:S(2)}, u32[]{:S(2)}) collective-permute-start(bf16[256,256]{1,0:T(8,128)(2,1)S(1)} %collective-permute-done.14.c), channel_id=1, source_target_pairs={{0,1},{1,0},{2,3},{3,2},{4,5},{5,4},{6,7},{7,6},{8,9},{9,8},{10,11... | collective-permute-start | bytes 393224 | tf_op jit(solution)/shard_map/ppermute | solution.py:473
  84.9 8.8 %collective-permute-start.19 = (bf16[256,256]{1,0:T(8,128)(2,1)S(1)}, bf16[256,256]{1,0:T(8,128)(2,1)S(1)}, u32[]{:S(2)}, u32[]{:S(2)}) collective-permute-start(bf16[256,256]{1,0:T(8,128)(2,1)S(1)} %collective-permute-done.15.d), channel_id=1, source_target_pairs={{0,1},{1,0},{2,3},{3,2},{4,5},{5,4},{6,7},{7,6},{8,9},{9,8},{10,11... | collective-permute-start | bytes 393224 | tf_op jit(solution)/shard_map/ppermute | solution.py:473
  93.6 2.4 %copy-start.1 = (f32[256]{0:T(256)S(1)}, f32[256]{0:T(256)}, u32[]{:S(2)}) copy-start(f32[256]{0:T(256)} %param.13) | copy-start | bytes 3076

commit v4 on v3

--- a/solution.py
+++ b/solution.py
@@ -9,7 +9,7 @@
 NZ = 8
 NX = 4
 NB = 8
-EARLY = 512
+EARLY = 384
 BF = jnp.bfloat16
 F32 = jnp.float32
 
@@ -44,91 +44,84 @@
     return pltpu.HBM(shape, dtype)
 
 
-def swap_matrix():
-    r = lax.broadcasted_iota(jnp.int32, (256, 256), 0)
-    c = lax.broadcasted_iota(jnp.int32, (256, 256), 1)
-    hit = ((r & 15) == (c >> 4)) & ((r >> 4) == (c & 15))
-    return jnp.where(hit, 1.0, 0.0).astype(BF)
-
-
-def swapped(swap, block):
-    n = block.shape[-1]
-    out = jnp.dot(swap, block.reshape(256, n), preferred_element_type=F32)
-    return out.astype(BF).reshape(16, 16, n)
-
-
-def head_kernel(me_ref, x_ref, *rest):
-    outs, turned = rest[:-1], rest[-1]
-    swap = swap_matrix()
-    f, g, _ = x_ref.shape
-    for f0 in range(0, f, 16):
-        for g0 in range(0, g, 16):
-            turned[g0 : g0 + 16, f0 : f0 + 16, :] = swapped(swap, x_ref[f0 : f0 + 16, g0 : g0 + 16, :])
-    z, x = place(me_ref)
-    for dz in range(NZ):
-        for j in range(NX):
-            outs[dz][j] = turned[(z + dz) % NZ * NX + (x + j) % NX]
-
-
-def split_head(me, features, halo):
-    f, g, _ = features.shape
-    return pl.pallas_call(
-        head_kernel,
+def swap_matrix(g, z, x):
+    rows = 8 * g
+    r = lax.broadcasted_iota(jnp.int32, (rows, rows), 0)
+    c = lax.broadcasted_iota(jnp.int32, (rows, rows), 1)
+    slot = r // 8
+    place_of = (slot // NX + z) % NZ * NX + (slot % NX + x) % NX
+    return jnp.where(c == (r % 8) * g + place_of, 1.0, 0.0).astype(BF)
+
+
+def swapped(swap, x_ref, f0, at):
+    g, n = x_ref.shape[1], at.stop - at.start
+    halves = [
+        jnp.dot(swap, x_ref[f : f + 8, :, at].reshape(8 * g, n), preferred_element_type=F32)
+        .reshape(g, 8, n)
+        for f in (f0, f0 + 8)
+    ]
+    return jnp.concatenate(halves, axis=1).astype(BF)
+
+
+def split_kernel(me_ref, x_hbm, *rest):
+    heads, (tail_hbm, x_ref, tail_ref, sem) = rest[:NZ], rest[NZ:]
+    f, g, n = x_ref.shape
+    early = heads[0].shape[2]
+    chunks = range(0, f, 16)
+
+    def load(i, f0, start, size, which):
+        at = (pl.ds(f0, 16), slice(None), pl.ds(start, size))
+        return pltpu.make_async_copy(x_hbm.at[at], x_ref.at[at], sem.at[which, i])
+
+    late = [load(i, f0, early, n - early, 0) for i, f0 in enumerate(chunks)]
+    soon = [load(i, f0, 0, early, 1) for i, f0 in enumerate(chunks)]
+    for copy in late + soon:
+        copy.start()
+    zero = jnp.int32(0)
+    plain = swap_matrix(g, zero, zero)
+    turned = swap_matrix(g, *place(me_ref))
+    outs = []
+    for i, f0 in enumerate(chunks):
+        late[i].wait()
+        for n0 in range(early, n, 2 * TILE):
+            at = slice(n0, min(n0 + 2 * TILE, n))
+            to = slice(at.start - early, at.stop - early)
+            tail_ref[:, f0 : f0 + 16, to] = swapped(plain, x_ref, f0, at)
+        at = (slice(None), pl.ds(f0, 16), slice(None))
+        outs.append(pltpu.make_async_copy(tail_ref.at[at], tail_hbm.at[at], sem.at[2, i]))
+        outs[-1].start()
+    for i, f0 in enumerate(chunks):
+        soon[i].wait()
+        for n0 in range(0, early, 2 * TILE):
+            at = slice(n0, min(n0 + 2 * TILE, early))
+            block = swapped(turned, x_ref, f0, at)
+            for dz in range(NZ):
+                heads[dz][:, f0 : f0 + 16, at] = block[dz * NX : (dz + 1) * NX]
+    for copy in outs:
+        copy.wait()
+
+
+def split(me, features, early):
+    f, g, n = features.shape
+    away = pl.BlockSpec(memory_space=pltpu.HBM)
+    *heads, tail = pl.pallas_call(
+        split_kernel,
         grid_spec=pltpu.PrefetchScalarGridSpec(
             num_scalar_prefetch=1,
             grid=(1,),
-            in_specs=[full((f, g, halo))],
-            out_specs=[full((NX, f, halo))] * NZ,
-            scratch_shapes=[pltpu.VMEM((g, f, halo), BF)],
+            in_specs=[away],
+            out_specs=[full((NX, f, early))] * NZ + [away],
+            scratch_shapes=[
+                pltpu.VMEM((f, g, n), BF),
+                pltpu.VMEM((g, f, n - early), BF),
+                pltpu.SemaphoreType.DMA((3, f // 16)),
+            ],
         ),
-        out_shape=[jax.ShapeDtypeStruct((NX, f, halo), BF)] * NZ,
-        compiler_params=VM,
-        name="split_head",
+        out_shape=[jax.ShapeDtypeStruct((NX, f, early), BF)] * NZ + [hbm((g, f, n - early), BF)],
+        compiler_params=VM,
+        name="split",
     )(me, features)
-
-
-def tail_kernel(x_hbm, o_hbm, x_ref, o_ref, sem):
-    f, g, n = x_ref.shape
-    halo = x_hbm.shape[2] - n
-    chunks = range(0, f, 16)
-    ins = [
-        pltpu.make_async_copy(
-            x_hbm.at[pl.ds(f0, 16), :, pl.ds(halo, n)], x_ref.at[pl.ds(f0, 16)], sem.at[0, i]
-        )
-        for i, f0 in enumerate(chunks)
-    ]
-    for copy in ins:
-        copy.start()
-    swap = swap_matrix()
-    outs = []
-    for i, f0 in enumerate(chunks):
-        ins[i].wait()
-        for g0 in range(0, g, 16):
-            o_ref[g0 : g0 + 16, f0 : f0 + 16, :] = swapped(swap, x_ref[f0 : f0 + 16, g0 : g0 + 16, :])
-        copy = pltpu.make_async_copy(
-            o_ref.at[:, pl.ds(f0, 16), :], o_hbm.at[:, pl.ds(f0, 16), :], sem.at[1, i]
-        )
-        copy.start()
-        outs.append(copy)
-    for copy in outs:
-        copy.wait()
-
-
-def split_tail(features, halo):
-    f, g, n = features.shape
-    return pl.pallas_call(
-        tail_kernel,
-        in_specs=[pl.BlockSpec(memory_space=pltpu.HBM)],
-        out_specs=pl.BlockSpec(memory_space=pltpu.HBM),
-        out_shape=hbm((g, f, n - halo), BF),
-        scratch_shapes=[
-            pltpu.VMEM((f, g, n - halo), BF),
-            pltpu.VMEM((g, f, n - halo), BF),
-            pltpu.SemaphoreType.DMA((2, f // 16)),
-        ],
-        compiler_params=VM,
-        name="split_tail",
-    )(features)
+    return heads, tail
 
 
 def regroup_kernel(*refs):
@@ -201,32 +194,26 @@
     )(me, in_hbm(w_self), in_hbm(w_neigh))
 
 
-def project(parts, rot_ref, columns):
-    rows = parts[0].shape[0]
+def halo_kernel(a, b, c, d, rot_ref, h_ref):
+    rows, (halo, hid) = a.shape[0], h_ref.shape
     total = None
-    for j, part in enumerate(parts):
+    for j, part in enumerate((a, b, c, d)):
         one = lax.dot_general(
             part[...],
-            rot_ref[j * rows : (j + 1) * rows, columns],
+            rot_ref[j * rows : (j + 1) * rows, hid:],
             (((0,), (0,)), ((), ())),
             preferred_element_type=F32,
         )
         total = one if total is None else total + one
-    return total
-
-
-def halo_kernel(a, b, c, d, rot_ref, h_ref):
-    hid = h_ref.shape[1]
-    h_ref[...] = project((a, b, c, d), rot_ref, slice(hid, None)).astype(BF)
-
-
-def halo_hidden(parts, rot):
-    rows, halo = parts[0].shape
+    h_ref[...] = total.astype(BF)
+
+
+def halo_hidden(parts, rot, halo):
     hid = rot.shape[1] // 2
     return pl.pallas_call(
         halo_kernel,
         grid=(1,),
-        in_specs=[full((rows, halo))] * NX + [full(rot.shape)],
+        in_specs=[full(parts[0].shape)] * NX + [full(rot.shape)],
         out_specs=full((halo, hid)),
         out_shape=jax.ShapeDtypeStruct((halo, hid), BF),
         compiler_params=VM,
@@ -235,24 +222,36 @@
 
 
 def mid_kernel(*refs):
-    heads, mids, (rot_ref, mid_ref, acc_ref, self_ref, o_ref) = refs[:NX], refs[NX : 2 * NX], refs[2 * NX :]
-    halo, hid = heads[0].shape[1], o_ref.shape[1]
-    h = project(mids, rot_ref, slice(hid, None)).astype(BF)
-    o_ref[...] = acc_ref[...] + jnp.dot(mid_ref[...], h, preferred_element_type=F32)
-    self_ref[:halo, :] = project(heads, rot_ref, slice(0, hid))
-    self_ref[halo:, :] = project(mids, rot_ref, slice(0, hid))
-
-
-def mid_hidden(heads, mids, rot, live_mid, acc):
-    early = heads[0].shape[1] + mids[0].shape[1]
-    hid = rot.shape[1] // 2
-    args = (*heads, *mids, rot, live_mid, acc)
+    halves, (rot_ref, own_ref, head_ref, mid_ref, self_ref, o_ref) = refs[: 2 * NX], refs[2 * NX :]
+    halo, hid = own_ref.shape
+    rows = halves[0].shape[0]
+    total = [None, None]
+    for k, part in enumerate(halves):
+        j, which = k % NX, k // NX
+        one = lax.dot_general(
+            part[...],
+            rot_ref[j * rows : (j + 1) * rows, : hid * (1 + which)],
+            (((0,), (0,)), ((), ())),
+            preferred_element_type=F32,
+        )
+        total[which] = one if j == 0 else total[which] + one
+    self_ref[:halo, :] = total[0]
+    self_ref[halo:, :] = total[1][:, :hid]
+    h = total[1][:, hid:].astype(BF)
+    o_ref[...] = jnp.dot(head_ref[...], own_ref[...], preferred_element_type=F32) + jnp.dot(
+        mid_ref[...], h, preferred_element_type=F32
+    )
+
+
+def mid_hidden(parts, mids, rot, own, live_head, live_mid):
+    early, rows, hid = parts[0].shape[1] + mids[0].shape[1], live_mid.shape[0], own.shape[1]
+    args = (*parts, *mids, rot, own, live_head, live_mid)
     return pl.pallas_call(
         mid_kernel,
         grid=(1,),
         in_specs=[full(a.shape) for a in args],
-        out_specs=[full((early, hid)), full(acc.shape)],
-        out_shape=[hbm((early, hid), F32), jax.ShapeDtypeStruct(acc.shape, F32)],
+        out_specs=[full((early, hid)), full((rows, hid))],
+        out_shape=[hbm((early, hid), F32), jax.ShapeDtypeStruct((rows, hid), F32)],
         compiler_params=VM,
         name="mid_hidden",
     )(*args)
@@ -352,41 +351,33 @@
     )(me, tile_mask, in_hbm(adj_local), in_hbm(adj_remote))
 
 
-def near_kernel(head_ref, near_ref, a, b, c, d, o_ref):
-    halo = a.shape[0]
-    total = jnp.dot(head_ref[...], a[...], preferred_element_type=F32)
-    for i, part in enumerate((b, c, d)):
+def gather_kernel(acc_ref, live_ref, *rest):
+    parts, o_ref = rest[:-1], rest[-1]
+    halo = parts[0].shape[0]
+    total = acc_ref[...]
+    for i, part in enumerate(parts):
         at = slice(i * halo, (i + 1) * halo)
-        total = total + jnp.dot(near_ref[:, at], part[...], preferred_element_type=F32)
+        total = total + jnp.dot(live_ref[:, at], part[...], preferred_element_type=F32)
     o_ref[...] = total
 
 
-def far_kernel(acc_ref, far_ref, a, b, c, d, o_ref):
-    halo = a.shape[0]
-    total = acc_ref[...]
-    for i, part in enumerate((a, b, c, d)):
-        at = slice(i * halo, (i + 1) * halo)
-        total = total + jnp.dot(far_ref[:, at], part[...], preferred_element_type=F32)
-    o_ref[...] = total
-
-
-def gather_halo(kernel, arrays, parts, out):
+def gather_halo(arrays, parts):
     rows = arrays[0].shape[0]
     hid = parts[0].shape[1]
     block = 256
     line = lambda w: pl.BlockSpec((block, w), lambda i: (i, 0))
     return pl.pallas_call(
-        kernel,
+        gather_kernel,
         grid=(rows // block,),
         in_specs=[line(a.shape[1]) for a in arrays] + [full(p.shape) for p in parts],
         out_specs=line(hid),
-        out_shape=out((rows, hid), F32),
+        out_shape=jax.ShapeDtypeStruct((rows, hid), F32),
         compiler_params=VM,
     )(*arrays, *parts)
 
 
-def last_kernel(x_ref, wt_ref, tail_hbm, acc_hbm, scale_hbm, self_hbm, bias_ref, o_hbm,
-                s_ref, tail_ref, acc_ref, scale_ref, o_ref, sem):
+def last_kernel(x_ref, wt_ref, acc_ref, tail_hbm, scale_hbm, self_hbm, bias_ref, o_hbm,
+                s_ref, tail_ref, scale_ref, o_ref, sem):
     rows, hid = acc_ref.shape
     early, block = self_hbm.shape[0], 256
     ins = []
@@ -394,7 +385,6 @@
         at = pl.ds(i * block, block)
         some = [
             pltpu.make_async_copy(tail_hbm.at[at], tail_ref.at[at], sem.at[0, i]),
-            pltpu.make_async_copy(acc_hbm.at[at], acc_ref.at[at], sem.at[1, i]),
             pltpu.make_async_copy(scale_hbm.at[at], scale_ref.at[at], sem.at[2, i]),
         ]
         if i == 0:
@@ -422,18 +412,17 @@
         copy.wait()
 
 
-def last_step(x, turned, tail, acc, scale, self_early, bias):
+def last_step(x, turned, acc, tail, scale, self_early, bias):
     rows, hid = acc.shape
     away = pl.BlockSpec(memory_space=pltpu.HBM)
     return pl.pallas_call(
         last_kernel,
         grid=(1,),
-        in_specs=[full(x.shape), full(turned.shape)] + [away] * 4 + [full(bias.shape)],
+        in_specs=[full(x.shape), full(turned.shape), full(acc.shape)] + [away] * 3 + [full(bias.shape)],
         out_specs=away,
         scratch_shapes=[
             pltpu.VMEM((rows, hid), F32),
             pltpu.VMEM(tail.shape, BF),
-            pltpu.VMEM(acc.shape, F32),
             pltpu.VMEM(scale.shape, F32),
             pltpu.VMEM((rows, hid), BF),
             pltpu.SemaphoreType.DMA((5, rows // 256)),
@@ -441,7 +430,7 @@
         out_shape=jax.ShapeDtypeStruct((rows, hid), BF),
         compiler_params=VM,
         name="last_step",
-    )(x, turned, *(in_hbm(a) for a in (tail, acc, scale, self_early)), bias)
+    )(x, turned, acc, *(in_hbm(a) for a in (tail, scale, self_early)), bias)
 
 
 def shards(features, adj_local, adj_remote, tile_mask, w_self, w_neigh, out_bias):
@@ -449,11 +438,10 @@
     me = lax.axis_index(("feat", "blk")).reshape(1)
     features = in_hbm(features)
 
-    head = split_head(me, features, EARLY)
+    head, rest = split(me, features, EARLY)
     landed = [head[0]]
     for dz in range(1, NZ):
         landed.append(lax.ppermute(head[dz], "feat", feat_shift(dz, 0)))
-    rest = split_tail(features, EARLY)
     rest = lax.all_to_all(rest, "feat", split_axis=0, concat_axis=0, tiled=True)
     rest = rest.reshape(-1, rest.shape[-1])
 
@@ -466,15 +454,15 @@
     for j in range(1, NX):
         parts.append(lax.ppermute(rows[j], "feat", feat_shift(0, j)))
         mids.append(lax.ppermute(rows[NX + j], "feat", feat_shift(0, j)))
-    h_head = halo_hidden(parts, rot)
-    same = [h_head]
+    h_head = halo_hidden(parts, rot, halo)
+    same = []
     for dy in (1, 2, 3):
         same.append(lax.ppermute(h_head, "blk", blk_shift(dy, 0)))
-    other = [lax.ppermute(h, "blk", blk_shift(0, 1)) for h in same]
-    acc = gather_halo(near_kernel, (live_head, live_near), same, jax.ShapeDtypeStruct)
-    self_early, acc = mid_hidden(parts, mids, rot, live_mid, acc)
-    acc = gather_halo(far_kernel, (acc, live_far), other, hbm)
-    return last_step(rest, turned, live_tail, acc, scale, self_early, out_bias[None, :])
+    other = [lax.ppermute(h, "blk", blk_shift(0, 1)) for h in [h_head] + same]
+    self_early, acc = mid_hidden(parts, mids, rot, h_head, live_head, live_mid)
+    acc = gather_halo((acc, live_near), same)
+    acc = gather_halo((acc, live_far), other)
+    return last_step(rest, turned, acc, live_tail, scale, self_early, out_bias[None, :])
 
 
 def solution(mesh):

time: 99.9 us -> 102 us (1.021)
  the two profiles are of different devices: /device:TPU:1 before, /device:TPU:2 now
where the time goes in v4:
time: 102 us; the launch traced here: 101 us
  starting transfers between devices  42.1 us (41%)
  waiting for transfers between devices  40.6 us (40%)
  Pallas kernels  17.8 us (17%)
    ppermute x7, waiting for transfers between devices, shards(): landed.append(lax.ppermute(head[dz], 'feat', feat_shift(dz, 0)))  33.9 us
    ppermute x7, starting transfers between devices, shards(): landed.append(lax.ppermute(head[dz], 'feat', feat_shift(dz, 0)))  15.2 us
    all_to_all x1, starting transfers between devices, shards(): rest = lax.all_to_all(rest, 'feat', split_axis=0, concat_axis=0, tiled=True)  11.6 us
    ppermute x3, starting transfers between devices, shards(): same.append(lax.ppermute(h_head, 'blk', blk_shift(dy, 0)))  5.89 us
    pallas_call x1, Pallas kernels, mask_tiles(): pl.pallas_call(mask_kernel, grid_spec=pltpu.PrefetchScalarGridSpec(num_sc...  4.97 us
    ppermute x3, starting transfers between devices, shards(): parts.append(lax.ppermute(rows[j], 'feat', feat_shift(0, j)))  4.81 us
    pallas_call x1, Pallas kernels, last_step(): pl.pallas_call(last_kernel, grid=(1,), in_specs=[full(x.shape), full(turn...  4.35 us
    ppermute x3, starting transfers between devices, shards(): mids.append(lax.ppermute(rows[NX + j], 'feat', feat_shift(0, j)))  3.55 us
  transfers between devices with their start and end apart: 21, of which 8 were waited for; matrix products, arithmetic and copies ran while one was open for 0% of the time, Pallas kernels for 11%

profile of v4, /device:TPU:2, one launch (start us, length us, event | category | flops | bytes accessed | tf_op | source)
XLA Modules:
  0.0 100.8 jit_solution(10558320467927674567)
XLA Ops:
  0.0 2.8 %split.1 = (bf16[4,32,384]{2,1,0:T(8,128)(2,1)S(1)}, bf16[4,32,384]{2,1,0:T(8,128)(2,1)S(1)}, bf16[4,32,384]{2,1,0:T(8,128)(2,1)S(1)}, bf16[4,32,384]{2,1,0:T(8,...) custom-call(s32[1]{0:T(128)} %bitcast.me_ref, ...), custom_call_target="tpu_custom_call" | custom-call | tf_op jit(solution)/shard_map/split/pallas_call | solution.py:107
  2.8 11.6 %all-to-all-start = ((bf16[32,32,640]{2,1,0:T(8,128)(2,1)}), bf16[32,32,640]{2,1,0:T(8,128)(2,1)S(1)}, u32[]{:S(2)}, u32[]{:S(2)}) async-start(bf16[32,32,640]{2,1,0:T(8,128)(2,1)} %get-tuple-element.32), calls=%async_computation | async-start | bytes 2621440 | tf_op jit(solution)/shard_map/all_to_all | solution.py:445
  14.4 0.0 copy-start
  14.4 1.5 %collective-permute-start = (bf16[4,32,384]{2,1,0:T(8,128)(2,1)S(1)}, bf16[4,32,384]{2,1,0:T(8,128)(2,1)S(1)}, u32[]{:S(2)}, u32[]{:S(2)}) collective-permute-start(bf16[4,32,384]{2,1,0:T(8,128)(2,1)S(1)} %get-tuple-element.35), channel_id=1, source_target_pairs={{0,32},{8,40},{16,48},{24,56},{32,64},{40,72},{48,80},{56,88},{64,... | collective-permute-start | bytes 294920 | tf_op jit(solution)/shard_map/ppermute | solution.py:444
  16.0 2.4 %collective-permute-start.1 = (bf16[4,32,384]{2,1,0:T(8,128)(2,1)S(1)}, bf16[4,32,384]{2,1,0:T(8,128)(2,1)S(1)}, u32[]{:S(2)}, u32[]{:S(2)}) collective-permute-start(bf16[4,32,384]{2,1,0:T(8,128)(2,1)S(1)} %get-tuple-element.36), channel_id=1, source_target_pairs={{0,64},{8,72},{16,80},{24,88},{32,96},{40,104},{48,112},{56,120},{... | collective-permute-start | bytes 294920 | tf_op jit(solution)/shard_map/ppermute | solution.py:444
  18.3 2.7 %collective-permute-start.2 = (bf16[4,32,384]{2,1,0:T(8,128)(2,1)S(1)}, bf16[4,32,384]{2,1,0:T(8,128)(2,1)S(1)}, u32[]{:S(2)}, u32[]{:S(2)}) collective-permute-start(bf16[4,32,384]{2,1,0:T(8,128)(2,1)S(1)} %get-tuple-element.37), channel_id=1, source_target_pairs={{0,96},{8,104},{16,112},{24,120},{32,128},{40,136},{48,144},{56,15... | collective-permute-start | bytes 294920 | tf_op jit(solution)/shard_map/ppermute | solution.py:444
  21.1 2.3 %collective-permute-start.3 = (bf16[4,32,384]{2,1,0:T(8,128)(2,1)S(1)}, bf16[4,32,384]{2,1,0:T(8,128)(2,1)S(1)}, u32[]{:S(2)}, u32[]{:S(2)}) collective-permute-start(bf16[4,32,384]{2,1,0:T(8,128)(2,1)S(1)} %get-tuple-element.38), channel_id=1, source_target_pairs={{0,128},{8,136},{16,144},{24,152},{32,160},{40,168},{48,176},{56,1... | collective-permute-start | bytes 294920 | tf_op jit(solution)/shard_map/ppermute | solution.py:444
  23.4 2.7 %collective-permute-start.4 = (bf16[4,32,384]{2,1,0:T(8,128)(2,1)S(1)}, bf16[4,32,384]{2,1,0:T(8,128)(2,1)S(1)}, u32[]{:S(2)}, u32[]{:S(2)}) collective-permute-start(bf16[4,32,384]{2,1,0:T(8,128)(2,1)S(1)} %get-tuple-element.39), channel_id=1, source_target_pairs={{0,160},{8,168},{16,176},{24,184},{32,192},{40,200},{48,208},{56,2... | collective-permute-start | bytes 294920 | tf_op jit(solution)/shard_map/ppermute | solution.py:444
  26.1 23.1 %collective-permute-done.refs_1_ = bf16[4,32,384]{2,1,0:T(8,128)(2,1)S(1)} collective-permute-done((bf16[4,32,384]{2,1,0:T(8,128)(2,1)S(1)}, bf16[4,32,384]{2,1,0:T(8,128)(2,1)S(1)}, u32[]{:S(2)}, u32[]{:S(2)}) %collective-permute-start) | collective-permute-done | bytes 98336 | tf_op jit(solution)/shard_map/ppermute | solution.py:444
  49.2 2.1 %collective-permute-start.5 = (bf16[4,32,384]{2,1,0:T(8,128)(2,1)S(1)}, bf16[4,32,384]{2,1,0:T(8,128)(2,1)S(1)}, u32[]{:S(2)}, u32[]{:S(2)}) collective-permute-start(bf16[4,32,384]{2,1,0:T(8,128)(2,1)S(1)} %get-tuple-element.40), channel_id=1, source_target_pairs={{0,192},{8,200},{16,208},{24,216},{32,224},{40,232},{48,240},{56,2... | collective-permute-start | bytes 294920 | tf_op jit(solution)/shard_map/ppermute | solution.py:444
  51.3 3.3 %collective-permute-done.1.refs_2_ = bf16[4,32,384]{2,1,0:T(8,128)(2,1)S(1)} collective-permute-done((bf16[4,32,384]{2,1,0:T(8,128)(2,1)S(1)}, bf16[4,32,384]{2,1,0:T(8,128)(2,1)S(1)}, u32[]{:S(2)}, u32[]{:S(2)}) %collective-permute-start.1) | collective-permute-done | bytes 98336 | tf_op jit(solution)/shard_map/ppermute | solution.py:444
  54.6 1.4 %collective-permute-start.6 = (bf16[4,32,384]{2,1,0:T(8,128)(2,1)S(1)}, bf16[4,32,384]{2,1,0:T(8,128)(2,1)S(1)}, u32[]{:S(2)}, u32[]{:S(2)}) collective-permute-start(bf16[4,32,384]{2,1,0:T(8,128)(2,1)S(1)} %get-tuple-element.41), channel_id=1, source_target_pairs={{0,224},{8,232},{16,240},{24,248},{32,0},{40,8},{48,16},{56,24},{6... | collective-permute-start | bytes 294920 | tf_op jit(solution)/shard_map/ppermute | solution.py:444
  56.1 3.7 %collective-permute-done.2.refs_3_ = bf16[4,32,384]{2,1,0:T(8,128)(2,1)S(1)} collective-permute-done((bf16[4,32,384]{2,1,0:T(8,128)(2,1)S(1)}, bf16[4,32,384]{2,1,0:T(8,128)(2,1)S(1)}, u32[]{:S(2)}, u32[]{:S(2)}) %collective-permute-start.2) | collective-permute-done | bytes 98336 | tf_op jit(solution)/shard_map/ppermute | solution.py:444
  59.8 3.8 %collective-permute-done.3.refs_4_ = bf16[4,32,384]{2,1,0:T(8,128)(2,1)S(1)} collective-permute-done((bf16[4,32,384]{2,1,0:T(8,128)(2,1)S(1)}, bf16[4,32,384]{2,1,0:T(8,128)(2,1)S(1)}, u32[]{:S(2)}, u32[]{:S(2)}) %collective-permute-start.3) | collective-permute-done | bytes 98336 | tf_op jit(solution)/shard_map/ppermute | solution.py:444
  63.6 0.0 collective-permute-done.4.refs_5_
  63.6 0.0 collective-permute-done.5.refs_6_
  63.6 0.0 collective-permute-done.6.refs_7_
  63.6 0.1 regroup.1
  63.7 1.5 %collective-permute-start.7 = (bf16[256,256]{1,0:T(8,128)(2,1)S(1)}, bf16[256,256]{1,0:T(8,128)(2,1)S(1)}, u32[]{:S(2)}, u32[]{:S(2)}) collective-permute-start(bf16[256,256]{1,0:T(8,128)(2,1)S(1)} %get-tuple-element.43), channel_id=1, source_target_pairs={{0,8},{8,16},{16,24},{24,0},{32,40},{40,48},{48,56},{56,32},{64,72... | collective-permute-start | bytes 393224 | tf_op jit(solution)/shard_map/ppermute | solution.py:455
  65.2 1.1 %collective-permute-start.8 = (bf16[256,256]{1,0:T(8,128)(2,1)S(1)}, bf16[256,256]{1,0:T(8,128)(2,1)S(1)}, u32[]{:S(2)}, u32[]{:S(2)}) collective-permute-start(bf16[256,256]{1,0:T(8,128)(2,1)S(1)} %get-tuple-element.44), channel_id=1, source_target_pairs={{0,16},{8,24},{16,0},{24,8},{32,48},{40,56},{48,32},{56,40},{64,80... | collective-permute-start | bytes 393224 | tf_op jit(solution)/shard_map/ppermute | solution.py:455
  66.3 2.1 %collective-permute-start.9 = (bf16[256,256]{1,0:T(8,128)(2,1)S(1)}, bf16[256,256]{1,0:T(8,128)(2,1)S(1)}, u32[]{:S(2)}, u32[]{:S(2)}) collective-permute-start(bf16[256,256]{1,0:T(8,128)(2,1)S(1)} %get-tuple-element.45), channel_id=1, source_target_pairs={{0,24},{8,0},{16,8},{24,16},{32,56},{40,32},{48,40},{56,48},{64,88... | collective-permute-start | bytes 393224 | tf_op jit(solution)/shard_map/ppermute | solution.py:455
  68.5 1.5 %weights.1 = (bf16[1024,512]{1,0:T(8,128)(2,1)S(1)}, bf16[512,1024]{1,0:T(8,128)(2,1)S(1)}) custom-call(s32[1]{0:T(128)} %bitcast.me_ref, bf16[1024,256]{1,0:T(8,128)(2,1)} %ws_hbm.1, bf16[1024,256]{1,0:T(8,128)(2,1)} %wn_hbm.1), custom_call_target="tpu_custom_call" | custom-call | tf_op jit(solution)/shard_map/weights/pallas_call | solution.py:175
  70.0 0.0 collective-permute-done.7.b.refs_1_
  70.0 2.8 %collective-permute-done.8.c.refs_2_ = bf16[256,256]{1,0:T(8,128)(2,1)S(1)} collective-permute-done((bf16[256,256]{1,0:T(8,128)(2,1)S(1)}, bf16[256,256]{1,0:T(8,128)(2,1)S(1)}, u32[]{:S(2)}, u32[]{:S(2)}) %collective-permute-start.8) | collective-permute-done | bytes 131104 | tf_op jit(solution)/shard_map/ppermute | solution.py:455
  72.8 0.6 collective-permute-done.9.d.refs_3_
  73.4 0.3 halo_hidden.1.refs_9_
  73.7 1.7 %collective-permute-start.13 = (bf16[256,256]{1,0:T(8,128)(2,1)S(1)}, bf16[256,256]{1,0:T(8,128)(2,1)S(1)}, u32[]{:S(2)}, u32[]{:S(2)}) collective-permute-start(bf16[256,256]{1,0:T(8,128)(2,1)S(1)} %halo_hidden.1.refs_9_), channel_id=1, source_target_pairs={{0,2},{1,3},{2,4},{3,5},{4,6},{5,7},{6,0},{7,1},{8,10},{9,11},{10,... | collective-permute-start | bytes 393224 | tf_op jit(solution)/shard_map/ppermute | solution.py:460
  75.4 2.9 %collective-permute-start.14 = (bf16[256,256]{1,0:T(8,128)(2,1)S(1)}, bf16[256,256]{1,0:T(8,128)(2,1)S(1)}, u32[]{:S(2)}, u32[]{:S(2)}) collective-permute-start(bf16[256,256]{1,0:T(8,128)(2,1)S(1)} %halo_hidden.1.refs_9_), channel_id=1, source_target_pairs={{0,4},{1,5},{2,6},{3,7},{4,0},{5,1},{6,2},{7,3},{8,12},{9,13},{10,... | collective-permute-start | bytes 393224 | tf_op jit(solution)/shard_map/ppermute | solution.py:460
  78.3 1.3 %collective-permute-start.15 = (bf16[256,256]{1,0:T(8,128)(2,1)S(1)}, bf16[256,256]{1,0:T(8,128)(2,1)S(1)}, u32[]{:S(2)}, u32[]{:S(2)}) collective-permute-start(bf16[256,256]{1,0:T(8,128)(2,1)S(1)} %halo_hidden.1.refs_9_), channel_id=1, source_target_pairs={{0,6},{1,7},{2,0},{3,1},{4,2},{5,3},{6,4},{7,5},{8,14},{9,15},{10,... | collective-permute-start | bytes 393224 | tf_op jit(solution)/shard_map/ppermute | solution.py:460
  79.6 1.4 %collective-permute-start.10 = (bf16[256,128]{1,0:T(8,128)(2,1)S(1)}, bf16[256,128]{1,0:T(8,128)(2,1)S(1)}, u32[]{:S(2)}, u32[]{:S(2)}) collective-permute-start(bf16[256,128]{1,0:T(8,128)(2,1)S(1)} %get-tuple-element.47), channel_id=1, source_target_pairs={{0,8},{8,16},{16,24},{24,0},{32,40},{40,48},{48,56},{56,32},{64,72... | collective-permute-start | bytes 196616 | tf_op jit(solution)/shard_map/ppermute | solution.py:456
  81.0 1.5 %collective-permute-start.11 = (bf16[256,128]{1,0:T(8,128)(2,1)S(1)}, bf16[256,128]{1,0:T(8,128)(2,1)S(1)}, u32[]{:S(2)}, u32[]{:S(2)}) collective-permute-start(bf16[256,128]{1,0:T(8,128)(2,1)S(1)} %get-tuple-element.48), channel_id=1, source_target_pairs={{0,16},{8,24},{16,0},{24,8},{32,48},{40,56},{48,32},{56,40},{64,80... | collective-permute-start | bytes 196616 | tf_op jit(solution)/shard_map/ppermute | solution.py:456
  82.5 2.0 %collective-permute-done.10.refs_5_ = bf16[256,128]{1,0:T(8,128)(2,1)S(1)} collective-permute-done((bf16[256,128]{1,0:T(8,128)(2,1)S(1)}, bf16[256,128]{1,0:T(8,128)(2,1)S(1)}, u32[]{:S(2)}, u32[]{:S(2)}) %collective-permute-start.10) | collective-permute-done | bytes 65568 | tf_op jit(solution)/shard_map/ppermute | solution.py:456
  84.5 0.0 collective-permute-start.16
  84.5 0.0 collective-permute-done.13.rest_0_
  84.5 0.5 collective-permute-start.17
  85.0 0.1 collective-permute-start.18
  85.1 0.4 collective-permute-start.19
  85.5 1.2 %collective-permute-done.11.refs_6_ = bf16[256,128]{1,0:T(8,128)(2,1)S(1)} collective-permute-done((bf16[256,128]{1,0:T(8,128)(2,1)S(1)}, bf16[256,128]{1,0:T(8,128)(2,1)S(1)}, u32[]{:S(2)}, u32[]{:S(2)}) %collective-permute-start.11) | collective-permute-done | bytes 65568 | tf_op jit(solution)/shard_map/ppermute | solution.py:456
  86.7 0.7 collective-permute-start.12
  87.4 5.0 %mask_tiles.1 = (bf16[1024,256]{1,0:T(8,128)(2,1)S(1)}, bf16[1024,128]{1,0:T(8,128)(2,1)S(1)}, bf16[1024,640]{1,0:T(8,128)(2,1)}, bf16[1024,768]{1,0:T(8,128)(2,...) custom-call(s32[1]{0:T(128)} %bitcast.me_ref, s32[8,22]{1,0:T(8,128)S(1)} %copy-done, ...), custom_call_target="tpu_custom_call" | custom-call | tf_op jit(solution)/shard_map/mask_tiles/pallas_call | solution.py:319
  92.4 0.0 collective-permute-done.12.refs_7_
  92.4 1.5 %mid_hidden.1 = (f32[384,256]{1,0:T(8,128)}, f32[1024,256]{1,0:T(8,128)S(1)}) custom-call(bf16[256,256]{1,0:T(8,128)(2,1)S(1)} %get-tuple-element.42.a.refs_0_, bf16[256,256]{1,0:T(8,128)(2,1)S(1)} %collective-permute-done.7.b.refs_1_, bf16[256,256]{1,0:T(8,128)(2,1)S(1)} %collective-permute-done.8.c.refs_2_, ...), custom_call_target="tpu_custom_call" | custom-call | tf_op jit(solution)/shard_map/mid_hidden/pallas_call | solution.py:249
  93.9 1.1 %shard_map.73.acc_ref = f32[1024,256]{1,0:T(8,128)S(1)} custom-call(f32[1024,256]{1,0:T(8,128)S(1)} %get-tuple-element.53.acc_ref, bf16[1024,768]{1,0:T(8,128)(2,1)S(1)} %get-tuple-element.54.live_ref, bf16[256,256]{1,0:T(8,128)(2,1)S(1)} %collective-permute-done.13.rest_0_, bf16[256,256]{1,0:T(8,128)(2,1)S(1)} %collective-permute-done.14.rest_1_, ...), custom_call_target="tpu_custom_call" | custom-call | tf_op jit(solution)/shard_map/pallas_call | solution.py:369
  95.0 0.0 collective-permute-done.18.rest_2_
  95.0 0.0 collective-permute-done.19.rest_3_
  95.0 0.0 copy-start.1
  95.1 1.3 %shard_map.74.acc_ref = f32[1024,256]{1,0:T(8,128)S(1)} custom-call(f32[1024,256]{1,0:T(8,128)S(1)} %shard_map.73.acc_ref, bf16[1024,1024]{1,0:T(8,128)(2,1)S(1)} %get-tuple-element.55.live_ref, bf16[256,256]{1,0:T(8,128)(2,1)S(1)} %collective-permute-done.16.rest_0_, bf16[256,256]{1,0:T(8,128)(2,1)S(1)} %collective-permute-done.17.rest_1_, ...), custom_call_target="tpu_custom_call" | custom-call | tf_op jit(solution)/shard_map/pallas_call | solution.py:369
  96.3 4.3 %last_step.1 = bf16[1024,256]{1,0:T(8,128)(2,1)} custom-call(bf16[1024,640]{1,0:T(8,128)(2,1)S(1)} %bitcast.3, bf16[512,1024]{1,0:T(8,128)(2,1)S(1)} %get-tuple-element.33.wt_ref, f32[1024,256]{1,0:T(8,128)S(1)} %shard_map.74.acc_ref, bf16[1024,640]{1,0:T(8,128)(2,1)} %get-tuple-element.56.tail_hbm, f32[1024,128]{1,0:T(8,128)} %get-tuple-element.57.scale_hbm, ...), custom_call_target="tpu_custom_call" | custom-call | tf_op jit(solution)/shard_map/last_step/pallas_call | solution.py:418
  (7 shorter events, 0.0 us)
Async XLA Ops:
  2.8 93.5 %all-to-all-start = ((bf16[32,32,640]{2,1,0:T(8,128)(2,1)}), bf16[32,32,640]{2,1,0:T(8,128)(2,1)S(1)}, u32[]{:S(2)}, u32[]{:S(2)}) async-start(bf16[32,32,640]{2,1,0:T(8,128)(2,1)} %get-tuple-element.32), calls=%async_computation | async-start | bytes 2621440 | tf_op jit(solution)/shard_map/all_to_all | solution.py:445
  14.4 73.0 %copy-start = (s32[8,22]{1,0:T(8,128)S(1)}, s32[8,22]{1,0:T(8,128)}, u32[]{:S(2)}) copy-start(s32[8,22]{1,0:T(8,128)} %mask_ref.1) | copy-start | bytes 2116
  14.4 34.8 %collective-permute-start = (bf16[4,32,384]{2,1,0:T(8,128)(2,1)S(1)}, bf16[4,32,384]{2,1,0:T(8,128)(2,1)S(1)}, u32[]{:S(2)}, u32[]{:S(2)}) collective-permute-start(bf16[4,32,384]{2,1,0:T(8,128)(2,1)S(1)} %get-tuple-element.35), channel_id=1, source_target_pairs={{0,32},{8,40},{16,48},{24,56},{32,64},{40,72},{48,80},{56,88},{64,... | collective-permute-start | bytes 294920 | tf_op jit(solution)/shard_map/ppermute | solution.py:444
  16.0 38.7 %collective-permute-start.1 = (bf16[4,32,384]{2,1,0:T(8,128)(2,1)S(1)}, bf16[4,32,384]{2,1,0:T(8,128)(2,1)S(1)}, u32[]{:S(2)}, u32[]{:S(2)}) collective-permute-start(bf16[4,32,384]{2,1,0:T(8,128)(2,1)S(1)} %get-tuple-element.36), channel_id=1, source_target_pairs={{0,64},{8,72},{16,80},{24,88},{32,96},{40,104},{48,112},{56,120},{... | collective-permute-start | bytes 294920 | tf_op jit(solution)/shard_map/ppermute | solution.py:444
  18.3 41.4 %collective-permute-start.2 = (bf16[4,32,384]{2,1,0:T(8,128)(2,1)S(1)}, bf16[4,32,384]{2,1,0:T(8,128)(2,1)S(1)}, u32[]{:S(2)}, u32[]{:S(2)}) collective-permute-start(bf16[4,32,384]{2,1,0:T(8,128)(2,1)S(1)} %get-tuple-element.37), channel_id=1, source_target_pairs={{0,96},{8,104},{16,112},{24,120},{32,128},{40,136},{48,144},{56,15... | collective-permute-start | bytes 294920 | tf_op jit(solution)/shard_map/ppermute | solution.py:444
  21.1 42.5 %collective-permute-start.3 = (bf16[4,32,384]{2,1,0:T(8,128)(2,1)S(1)}, bf16[4,32,384]{2,1,0:T(8,128)(2,1)S(1)}, u32[]{:S(2)}, u32[]{:S(2)}) collective-permute-start(bf16[4,32,384]{2,1,0:T(8,128)(2,1)S(1)} %get-tuple-element.38), channel_id=1, source_target_pairs={{0,128},{8,136},{16,144},{24,152},{32,160},{40,168},{48,176},{56,1... | collective-permute-start | bytes 294920 | tf_op jit(solution)/shard_map/ppermute | solution.py:444
  23.4 40.2 %collective-permute-start.4 = (bf16[4,32,384]{2,1,0:T(8,128)(2,1)S(1)}, bf16[4,32,384]{2,1,0:T(8,128)(2,1)S(1)}, u32[]{:S(2)}, u32[]{:S(2)}) collective-permute-start(bf16[4,32,384]{2,1,0:T(8,128)(2,1)S(1)} %get-tuple-element.39), channel_id=1, source_target_pairs={{0,160},{8,168},{16,176},{24,184},{32,192},{40,200},{48,208},{56,2... | collective-permute-start | bytes 294920 | tf_op jit(solution)/shard_map/ppermute | solution.py:444
  49.2 14.4 %collective-permute-start.5 = (bf16[4,32,384]{2,1,0:T(8,128)(2,1)S(1)}, bf16[4,32,384]{2,1,0:T(8,128)(2,1)S(1)}, u32[]{:S(2)}, u32[]{:S(2)}) collective-permute-start(bf16[4,32,384]{2,1,0:T(8,128)(2,1)S(1)} %get-tuple-element.40), channel_id=1, source_target_pairs={{0,192},{8,200},{16,208},{24,216},{32,224},{40,232},{48,240},{56,2... | collective-permute-start | bytes 294920 | tf_op jit(solution)/shard_map/ppermute | solution.py:444
  54.6 8.9 %collective-permute-start.6 = (bf16[4,32,384]{2,1,0:T(8,128)(2,1)S(1)}, bf16[4,32,384]{2,1,0:T(8,128)(2,1)S(1)}, u32[]{:S(2)}, u32[]{:S(2)}) collective-permute-start(bf16[4,32,384]{2,1,0:T(8,128)(2,1)S(1)} %get-tuple-element.41), channel_id=1, source_target_pairs={{0,224},{8,232},{16,240},{24,248},{32,0},{40,8},{48,16},{56,24},{6... | collective-permute-start | bytes 294920 | tf_op jit(solution)/shard_map/ppermute | solution.py:444
  63.7 6.3 %collective-permute-start.7 = (bf16[256,256]{1,0:T(8,128)(2,1)S(1)}, bf16[256,256]{1,0:T(8,128)(2,1)S(1)}, u32[]{:S(2)}, u32[]{:S(2)}) collective-permute-start(bf16[256,256]{1,0:T(8,128)(2,1)S(1)} %get-tuple-element.43), channel_id=1, source_target_pairs={{0,8},{8,16},{16,24},{24,0},{32,40},{40,48},{48,56},{56,32},{64,72... | collective-permute-start | bytes 393224 | tf_op jit(solution)/shard_map/ppermute | solution.py:455
  65.2 7.6 %collective-permute-start.8 = (bf16[256,256]{1,0:T(8,128)(2,1)S(1)}, bf16[256,256]{1,0:T(8,128)(2,1)S(1)}, u32[]{:S(2)}, u32[]{:S(2)}) collective-permute-start(bf16[256,256]{1,0:T(8,128)(2,1)S(1)} %get-tuple-element.44), channel_id=1, source_target_pairs={{0,16},{8,24},{16,0},{24,8},{32,48},{40,56},{48,32},{56,40},{64,80... | collective-permute-start | bytes 393224 | tf_op jit(solution)/shard_map/ppermute | solution.py:455
  66.3 7.0 %collective-permute-start.9 = (bf16[256,256]{1,0:T(8,128)(2,1)S(1)}, bf16[256,256]{1,0:T(8,128)(2,1)S(1)}, u32[]{:S(2)}, u32[]{:S(2)}) collective-permute-start(bf16[256,256]{1,0:T(8,128)(2,1)S(1)} %get-tuple-element.45), channel_id=1, source_target_pairs={{0,24},{8,0},{16,8},{24,16},{32,56},{40,32},{48,40},{56,48},{64,88... | collective-permute-start | bytes 393224 | tf_op jit(solution)/shard_map/ppermute | solution.py:455
  73.7 10.7 %collective-permute-start.13 = (bf16[256,256]{1,0:T(8,128)(2,1)S(1)}, bf16[256,256]{1,0:T(8,128)(2,1)S(1)}, u32[]{:S(2)}, u32[]{:S(2)}) collective-permute-start(bf16[256,256]{1,0:T(8,128)(2,1)S(1)} %halo_hidden.1.refs_9_), channel_id=1, source_target_pairs={{0,2},{1,3},{2,4},{3,5},{4,6},{5,7},{6,0},{7,1},{8,10},{9,11},{10,... | collective-permute-start | bytes 393224 | tf_op jit(solution)/shard_map/ppermute | solution.py:460
  75.4 9.6 %collective-permute-start.14 = (bf16[256,256]{1,0:T(8,128)(2,1)S(1)}, bf16[256,256]{1,0:T(8,128)(2,1)S(1)}, u32[]{:S(2)}, u32[]{:S(2)}) collective-permute-start(bf16[256,256]{1,0:T(8,128)(2,1)S(1)} %halo_hidden.1.refs_9_), channel_id=1, source_target_pairs={{0,4},{1,5},{2,6},{3,7},{4,0},{5,1},{6,2},{7,3},{8,12},{9,13},{10,... | collective-permute-start | bytes 393224 | tf_op jit(solution)/shard_map/ppermute | solution.py:460
  78.3 6.8 %collective-permute-start.15 = (bf16[256,256]{1,0:T(8,128)(2,1)S(1)}, bf16[256,256]{1,0:T(8,128)(2,1)S(1)}, u32[]{:S(2)}, u32[]{:S(2)}) collective-permute-start(bf16[256,256]{1,0:T(8,128)(2,1)S(1)} %halo_hidden.1.refs_9_), channel_id=1, source_target_pairs={{0,6},{1,7},{2,0},{3,1},{4,2},{5,3},{6,4},{7,5},{8,14},{9,15},{10,... | collective-permute-start | bytes 393224 | tf_op jit(solution)/shard_map/ppermute | solution.py:460
  79.6 4.8 %collective-permute-start.10 = (bf16[256,128]{1,0:T(8,128)(2,1)S(1)}, bf16[256,128]{1,0:T(8,128)(2,1)S(1)}, u32[]{:S(2)}, u32[]{:S(2)}) collective-permute-start(bf16[256,128]{1,0:T(8,128)(2,1)S(1)} %get-tuple-element.47), channel_id=1, source_target_pairs={{0,8},{8,16},{16,24},{24,0},{32,40},{40,48},{48,56},{56,32},{64,72... | collective-permute-start | bytes 196616 | tf_op jit(solution)/shard_map/ppermute | solution.py:456
  81.0 5.8 %collective-permute-start.11 = (bf16[256,128]{1,0:T(8,128)(2,1)S(1)}, bf16[256,128]{1,0:T(8,128)(2,1)S(1)}, u32[]{:S(2)}, u32[]{:S(2)}) collective-permute-start(bf16[256,128]{1,0:T(8,128)(2,1)S(1)} %get-tuple-element.48), channel_id=1, source_target_pairs={{0,16},{8,24},{16,0},{24,8},{32,48},{40,56},{48,32},{56,40},{64,80... | collective-permute-start | bytes 196616 | tf_op jit(solution)/shard_map/ppermute | solution.py:456
  84.5 10.5 %collective-permute-start.16 = (bf16[256,256]{1,0:T(8,128)(2,1)S(1)}, bf16[256,256]{1,0:T(8,128)(2,1)S(1)}, u32[]{:S(2)}, u32[]{:S(2)}) collective-permute-start(bf16[256,256]{1,0:T(8,128)(2,1)S(1)} %halo_hidden.1.refs_9_), channel_id=1, source_target_pairs={{0,1},{1,0},{2,3},{3,2},{4,5},{5,4},{6,7},{7,6},{8,9},{9,8},{10,11... | collective-permute-start | bytes 393224 | tf_op jit(solution)/shard_map/ppermute | solution.py:461
  84.5 10.6 %collective-permute-start.17 = (bf16[256,256]{1,0:T(8,128)(2,1)S(1)}, bf16[256,256]{1,0:T(8,128)(2,1)S(1)}, u32[]{:S(2)}, u32[]{:S(2)}) collective-permute-start(bf16[256,256]{1,0:T(8,128)(2,1)S(1)} %collective-permute-done.13.rest_0_), channel_id=1, source_target_pairs={{0,1},{1,0},{2,3},{3,2},{4,5},{5,4},{6,7},{7,6},{8,9},{9,8},{10,11... | collective-permute-start | bytes 393224 | tf_op jit(solution)/shard_map/ppermute | solution.py:461
  85.0 10.1 %collective-permute-start.18 = (bf16[256,256]{1,0:T(8,128)(2,1)S(1)}, bf16[256,256]{1,0:T(8,128)(2,1)S(1)}, u32[]{:S(2)}, u32[]{:S(2)}) collective-permute-start(bf16[256,256]{1,0:T(8,128)(2,1)S(1)} %collective-permute-done.14.rest_1_), channel_id=1, source_target_pairs={{0,1},{1,0},{2,3},{3,2},{4,5},{5,4},{6,7},{7,6},{8,9},{9,8},{10,11... | collective-permute-start | bytes 393224 | tf_op jit(solution)/shard_map/ppermute | solution.py:461
  85.1 10.0 %collective-permute-start.19 = (bf16[256,256]{1,0:T(8,128)(2,1)S(1)}, bf16[256,256]{1,0:T(8,128)(2,1)S(1)}, u32[]{:S(2)}, u32[]{:S(2)}) collective-permute-start(bf16[256,256]{1,0:T(8,128)(2,1)S(1)} %collective-permute-done.15.rest_2_), channel_id=1, source_target_pairs={{0,1},{1,0},{2,3},{3,2},{4,5},{5,4},{6,7},{7,6},{8,9},{9,8},{10,11... | collective-permute-start | bytes 393224 | tf_op jit(solution)/shard_map/ppermute | solution.py:461
  86.7 5.7 %collective-permute-start.12 = (bf16[256,128]{1,0:T(8,128)(2,1)S(1)}, bf16[256,128]{1,0:T(8,128)(2,1)S(1)}, u32[]{:S(2)}, u32[]{:S(2)}) collective-permute-start(bf16[256,128]{1,0:T(8,128)(2,1)S(1)} %get-tuple-element.49), channel_id=1, source_target_pairs={{0,24},{8,0},{16,8},{24,16},{32,56},{40,32},{48,40},{56,48},{64,88... | collective-permute-start | bytes 196616 | tf_op jit(solution)/shard_map/ppermute | solution.py:456
  95.0 1.3 %copy-start.1 = (f32[256]{0:T(256)S(1)}, f32[256]{0:T(256)}, u32[]{:S(2)}) copy-start(f32[256]{0:T(256)} %param.13) | copy-start | bytes 3076

commit v5 on v4

--- a/solution.py
+++ b/solution.py
@@ -48,9 +48,8 @@
     rows = 8 * g
     r = lax.broadcasted_iota(jnp.int32, (rows, rows), 0)
     c = lax.broadcasted_iota(jnp.int32, (rows, rows), 1)
-    slot = r // 8
-    place_of = (slot // NX + z) % NZ * NX + (slot % NX + x) % NX
-    return jnp.where(c == (r % 8) * g + place_of, 1.0, 0.0).astype(BF)
+    place_of = (((r >> 5) + z) & (NZ - 1)) * NX + (((r >> 3) + x) & (NX - 1))
+    return jnp.where(c == (r & 7) * g + place_of, 1.0, 0.0).astype(BF)
 
 
 def swapped(swap, x_ref, f0, at):
@@ -161,7 +160,7 @@
     for half, w_ref in enumerate((ws_ref, wn_ref)):
         copies[half].wait()
         at = slice(half * hid, (half + 1) * hid)
-        turned_ref[at, :] = w_ref[...].T
+        turned_ref[:, at] = w_ref[...]
         for j in range(NX):
             for dz in range(NZ):
                 src = ((z + (NZ - dz)) % NZ * NX + (x + (NX - j)) % NX) * f
@@ -178,7 +177,7 @@
             num_scalar_prefetch=1,
             grid=(1,),
             in_specs=[away, away],
-            out_specs=[full((f, 2 * hid)), full((2 * hid, f))],
+            out_specs=[full((f, 2 * hid))] * 2,
             scratch_shapes=[
                 pltpu.VMEM((f, hid), BF),
                 pltpu.VMEM((f, hid), BF),
@@ -187,7 +186,7 @@
         ),
         out_shape=[
             jax.ShapeDtypeStruct((f, 2 * hid), BF),
-            jax.ShapeDtypeStruct((2 * hid, f), BF),
+            jax.ShapeDtypeStruct((f, 2 * hid), BF),
         ],
         compiler_params=VM,
         name="weights",
@@ -281,9 +280,9 @@
             rows = slice(row * TILE, (row + 1) * TILE)
             degree = jnp.zeros((TILE, TILE), F32)
             for t in range(local + ar_ref.shape[1] // TILE):
-                flag = mask_ref[row, t].astype(F32)
+                flag = jnp.full((TILE, TILE), mask_ref[row, t].astype(F32)).astype(BF)
                 at = t * TILE if t < local else (t - local) * TILE
-                tile = (al_ref if t < local else ar_ref)[rows, at : at + TILE].astype(F32) * flag
+                tile = (al_ref if t < local else ar_ref)[rows, at : at + TILE] * flag
                 if t >= local:
                     back, inside = at // halo + 1, at % halo
                     if back % 2 == 0:
@@ -297,8 +296,8 @@
                     to, at = mid_ref, at - halo
                 else:
                     to, at = tail_ref, at - halo - mid
-                to[rows, pl.ds(at, TILE)] = tile.astype(BF)
-                degree = degree + tile
+                to[rows, pl.ds(at, TILE)] = tile
+                degree = degree + tile.astype(F32)
             whole = jnp.sum(degree, axis=1, keepdims=True)
             scale_ref[rows, :] = jnp.broadcast_to(1.0 / jnp.sqrt(whole), (TILE, TILE))
         at = pl.ds(i * block, block)
@@ -376,8 +375,8 @@
     )(*arrays, *parts)
 
 
-def last_kernel(x_ref, wt_ref, acc_ref, tail_hbm, scale_hbm, self_hbm, bias_ref, o_hbm,
-                s_ref, tail_ref, scale_ref, o_ref, sem):
+def last_kernel(x_ref, w_ref, acc_ref, tail_hbm, scale_hbm, self_hbm, bias_ref, o_hbm,
+                s_ref, h_ref, tail_ref, scale_ref, o_ref, sem):
     rows, hid = acc_ref.shape
     early, block = self_hbm.shape[0], 256
     ins = []
@@ -392,15 +391,18 @@
         for copy in some:
             copy.start()
         ins.append(some)
-    ht = jnp.dot(wt_ref[hid:, :], x_ref[...], preferred_element_type=F32).astype(BF)
-    s_ref[early:, :] = jnp.dot(wt_ref[:hid, :], x_ref[...], preferred_element_type=F32).T
-    last = (((1,), (1,)), ((), ()))
+    first = (((0,), (0,)), ((), ()))
+    for n0 in range(0, x_ref.shape[1], x_ref.shape[1]):
+        at = slice(n0, n0 + x_ref.shape[1])
+        both = lax.dot_general(x_ref[:, at], w_ref[...], first, preferred_element_type=F32)
+        s_ref[pl.ds(early + at.start, at.stop - at.start), :] = both[:, :hid]
+        h_ref[at, :] = both[:, hid:].astype(BF)
     outs = []
     for i in range(rows // block):
         for copy in ins[i]:
             copy.wait()
         at = slice(i * block, (i + 1) * block)
-        more = lax.dot_general(tail_ref[at, :], ht, last, preferred_element_type=F32)
+        more = jnp.dot(tail_ref[at, :], h_ref[...], preferred_element_type=F32)
         scale = jnp.concatenate([scale_ref[at, :]] * (hid // TILE), axis=1)
         o_ref[at, :] = jnp.maximum(
             s_ref[at, :] + (acc_ref[at, :] + more) * scale + bias_ref[...], 0.0
@@ -422,6 +424,7 @@
         out_specs=away,
         scratch_shapes=[
             pltpu.VMEM((rows, hid), F32),
+            pltpu.VMEM((x.shape[1], hid), BF),
             pltpu.VMEM(tail.shape, BF),
             pltpu.VMEM(scale.shape, F32),
             pltpu.VMEM((rows, hid), BF),

time: 102 us -> 102 us (level)
  transfers between devices with their start and end apart: 21 -> 21, of which waited for: 8 -> 8; matrix products, arithmetic and copies ran while one was open for 0% -> 0% of each run, Pallas kernels for 11% -> 10%
where the time goes in v5:
time: 102 us; the launch traced here: 100 us
  starting transfers between devices  42.1 us (41%)
  waiting for transfers between devices  40.8 us (40%)
  Pallas kernels  17 us (17%)
    ppermute x7, waiting for transfers between devices, shards(): landed.append(lax.ppermute(head[dz], 'feat', feat_shift(dz, 0)))  33.9 us
    ppermute x7, starting transfers between devices, shards(): landed.append(lax.ppermute(head[dz], 'feat', feat_shift(dz, 0)))  15.2 us
    all_to_all x1, starting transfers between devices, shards(): rest = lax.all_to_all(rest, 'feat', split_axis=0, concat_axis=0, tiled=True)  11.6 us
    ppermute x3, starting transfers between devices, shards(): same.append(lax.ppermute(h_head, 'blk', blk_shift(dy, 0)))  5.9 us
    ppermute x3, starting transfers between devices, shards(): parts.append(lax.ppermute(rows[j], 'feat', feat_shift(0, j)))  4.81 us
    pallas_call x1, Pallas kernels, mask_tiles(): pl.pallas_call(mask_kernel, grid_spec=pltpu.PrefetchScalarGridSpec(num_sc...  4.76 us
    pallas_call x1, Pallas kernels, last_step(): pl.pallas_call(last_kernel, grid=(1,), in_specs=[full(x.shape), full(turn...  3.98 us
    ppermute x3, waiting for transfers between devices, shards(): parts.append(lax.ppermute(rows[j], 'feat', feat_shift(0, j)))  3.59 us
  transfers between devices with their start and end apart: 21, of which 8 were waited for; matrix products, arithmetic and copies ran while one was open for 0% of the time, Pallas kernels for 10%

profile of v5, /device:TPU:2, one launch (start us, length us, event | category | flops | bytes accessed | tf_op | source)
XLA Modules:
  0.0 100.3 jit_solution(16811826777773848098)
XLA Ops:
  0.0 2.8 %split.1 = (bf16[4,32,384]{2,1,0:T(8,128)(2,1)S(1)}, bf16[4,32,384]{2,1,0:T(8,128)(2,1)S(1)}, bf16[4,32,384]{2,1,0:T(8,128)(2,1)S(1)}, bf16[4,32,384]{2,1,0:T(8,...) custom-call(s32[1]{0:T(128)} %bitcast.me_ref, ...), custom_call_target="tpu_custom_call" | custom-call | tf_op jit(solution)/shard_map/split/pallas_call | solution.py:106
  2.8 11.6 %all-to-all-start = ((bf16[32,32,640]{2,1,0:T(8,128)(2,1)}), bf16[32,32,640]{2,1,0:T(8,128)(2,1)S(1)}, u32[]{:S(2)}, u32[]{:S(2)}) async-start(bf16[32,32,640]{2,1,0:T(8,128)(2,1)} %get-tuple-element.32), calls=%async_computation | async-start | bytes 2621440 | tf_op jit(solution)/shard_map/all_to_all | solution.py:448
  14.4 0.0 copy-start
  14.4 1.5 %collective-permute-start = (bf16[4,32,384]{2,1,0:T(8,128)(2,1)S(1)}, bf16[4,32,384]{2,1,0:T(8,128)(2,1)S(1)}, u32[]{:S(2)}, u32[]{:S(2)}) collective-permute-start(bf16[4,32,384]{2,1,0:T(8,128)(2,1)S(1)} %get-tuple-element.35), channel_id=1, source_target_pairs={{0,32},{8,40},{16,48},{24,56},{32,64},{40,72},{48,80},{56,88},{64,... | collective-permute-start | bytes 294920 | tf_op jit(solution)/shard_map/ppermute | solution.py:447
  16.0 2.4 %collective-permute-start.1 = (bf16[4,32,384]{2,1,0:T(8,128)(2,1)S(1)}, bf16[4,32,384]{2,1,0:T(8,128)(2,1)S(1)}, u32[]{:S(2)}, u32[]{:S(2)}) collective-permute-start(bf16[4,32,384]{2,1,0:T(8,128)(2,1)S(1)} %get-tuple-element.36), channel_id=1, source_target_pairs={{0,64},{8,72},{16,80},{24,88},{32,96},{40,104},{48,112},{56,120},{... | collective-permute-start | bytes 294920 | tf_op jit(solution)/shard_map/ppermute | solution.py:447
  18.3 2.7 %collective-permute-start.2 = (bf16[4,32,384]{2,1,0:T(8,128)(2,1)S(1)}, bf16[4,32,384]{2,1,0:T(8,128)(2,1)S(1)}, u32[]{:S(2)}, u32[]{:S(2)}) collective-permute-start(bf16[4,32,384]{2,1,0:T(8,128)(2,1)S(1)} %get-tuple-element.37), channel_id=1, source_target_pairs={{0,96},{8,104},{16,112},{24,120},{32,128},{40,136},{48,144},{56,15... | collective-permute-start | bytes 294920 | tf_op jit(solution)/shard_map/ppermute | solution.py:447
  21.0 2.3 %collective-permute-start.3 = (bf16[4,32,384]{2,1,0:T(8,128)(2,1)S(1)}, bf16[4,32,384]{2,1,0:T(8,128)(2,1)S(1)}, u32[]{:S(2)}, u32[]{:S(2)}) collective-permute-start(bf16[4,32,384]{2,1,0:T(8,128)(2,1)S(1)} %get-tuple-element.38), channel_id=1, source_target_pairs={{0,128},{8,136},{16,144},{24,152},{32,160},{40,168},{48,176},{56,1... | collective-permute-start | bytes 294920 | tf_op jit(solution)/shard_map/ppermute | solution.py:447
  23.4 2.7 %collective-permute-start.4 = (bf16[4,32,384]{2,1,0:T(8,128)(2,1)S(1)}, bf16[4,32,384]{2,1,0:T(8,128)(2,1)S(1)}, u32[]{:S(2)}, u32[]{:S(2)}) collective-permute-start(bf16[4,32,384]{2,1,0:T(8,128)(2,1)S(1)} %get-tuple-element.39), channel_id=1, source_target_pairs={{0,160},{8,168},{16,176},{24,184},{32,192},{40,200},{48,208},{56,2... | collective-permute-start | bytes 294920 | tf_op jit(solution)/shard_map/ppermute | solution.py:447
  26.1 23.1 %collective-permute-done.refs_1_ = bf16[4,32,384]{2,1,0:T(8,128)(2,1)S(1)} collective-permute-done((bf16[4,32,384]{2,1,0:T(8,128)(2,1)S(1)}, bf16[4,32,384]{2,1,0:T(8,128)(2,1)S(1)}, u32[]{:S(2)}, u32[]{:S(2)}) %collective-permute-start) | collective-permute-done | bytes 98336 | tf_op jit(solution)/shard_map/ppermute | solution.py:447
  49.2 2.1 %collective-permute-start.5 = (bf16[4,32,384]{2,1,0:T(8,128)(2,1)S(1)}, bf16[4,32,384]{2,1,0:T(8,128)(2,1)S(1)}, u32[]{:S(2)}, u32[]{:S(2)}) collective-permute-start(bf16[4,32,384]{2,1,0:T(8,128)(2,1)S(1)} %get-tuple-element.40), channel_id=1, source_target_pairs={{0,192},{8,200},{16,208},{24,216},{32,224},{40,232},{48,240},{56,2... | collective-permute-start | bytes 294920 | tf_op jit(solution)/shard_map/ppermute | solution.py:447
  51.3 3.3 %collective-permute-done.1.refs_2_ = bf16[4,32,384]{2,1,0:T(8,128)(2,1)S(1)} collective-permute-done((bf16[4,32,384]{2,1,0:T(8,128)(2,1)S(1)}, bf16[4,32,384]{2,1,0:T(8,128)(2,1)S(1)}, u32[]{:S(2)}, u32[]{:S(2)}) %collective-permute-start.1) | collective-permute-done | bytes 98336 | tf_op jit(solution)/shard_map/ppermute | solution.py:447
  54.6 1.4 %collective-permute-start.6 = (bf16[4,32,384]{2,1,0:T(8,128)(2,1)S(1)}, bf16[4,32,384]{2,1,0:T(8,128)(2,1)S(1)}, u32[]{:S(2)}, u32[]{:S(2)}) collective-permute-start(bf16[4,32,384]{2,1,0:T(8,128)(2,1)S(1)} %get-tuple-element.41), channel_id=1, source_target_pairs={{0,224},{8,232},{16,240},{24,248},{32,0},{40,8},{48,16},{56,24},{6... | collective-permute-start | bytes 294920 | tf_op jit(solution)/shard_map/ppermute | solution.py:447
  56.1 3.7 %collective-permute-done.2.refs_3_ = bf16[4,32,384]{2,1,0:T(8,128)(2,1)S(1)} collective-permute-done((bf16[4,32,384]{2,1,0:T(8,128)(2,1)S(1)}, bf16[4,32,384]{2,1,0:T(8,128)(2,1)S(1)}, u32[]{:S(2)}, u32[]{:S(2)}) %collective-permute-start.2) | collective-permute-done | bytes 98336 | tf_op jit(solution)/shard_map/ppermute | solution.py:447
  59.7 3.8 %collective-permute-done.3.refs_4_ = bf16[4,32,384]{2,1,0:T(8,128)(2,1)S(1)} collective-permute-done((bf16[4,32,384]{2,1,0:T(8,128)(2,1)S(1)}, bf16[4,32,384]{2,1,0:T(8,128)(2,1)S(1)}, u32[]{:S(2)}, u32[]{:S(2)}) %collective-permute-start.3) | collective-permute-done | bytes 98336 | tf_op jit(solution)/shard_map/ppermute | solution.py:447
  63.5 0.0 collective-permute-done.4.refs_5_
  63.6 0.0 collective-permute-done.5.refs_6_
  63.6 0.1 regroup.1
  63.6 1.5 %collective-permute-start.7 = (bf16[256,256]{1,0:T(8,128)(2,1)S(1)}, bf16[256,256]{1,0:T(8,128)(2,1)S(1)}, u32[]{:S(2)}, u32[]{:S(2)}) collective-permute-start(bf16[256,256]{1,0:T(8,128)(2,1)S(1)} %get-tuple-element.43), channel_id=1, source_target_pairs={{0,8},{8,16},{16,24},{24,0},{32,40},{40,48},{48,56},{56,32},{64,72... | collective-permute-start | bytes 393224 | tf_op jit(solution)/shard_map/ppermute | solution.py:458
  65.2 1.1 %collective-permute-start.8 = (bf16[256,256]{1,0:T(8,128)(2,1)S(1)}, bf16[256,256]{1,0:T(8,128)(2,1)S(1)}, u32[]{:S(2)}, u32[]{:S(2)}) collective-permute-start(bf16[256,256]{1,0:T(8,128)(2,1)S(1)} %get-tuple-element.44), channel_id=1, source_target_pairs={{0,16},{8,24},{16,0},{24,8},{32,48},{40,56},{48,32},{56,40},{64,80... | collective-permute-start | bytes 393224 | tf_op jit(solution)/shard_map/ppermute | solution.py:458
  66.3 2.1 %collective-permute-start.9 = (bf16[256,256]{1,0:T(8,128)(2,1)S(1)}, bf16[256,256]{1,0:T(8,128)(2,1)S(1)}, u32[]{:S(2)}, u32[]{:S(2)}) collective-permute-start(bf16[256,256]{1,0:T(8,128)(2,1)S(1)} %get-tuple-element.45), channel_id=1, source_target_pairs={{0,24},{8,0},{16,8},{24,16},{32,56},{40,32},{48,40},{56,48},{64,88... | collective-permute-start | bytes 393224 | tf_op jit(solution)/shard_map/ppermute | solution.py:458
  68.5 1.3 %weights.1 = (bf16[1024,512]{1,0:T(8,128)(2,1)S(1)}, bf16[1024,512]{1,0:T(8,128)(2,1)S(1)}) custom-call(s32[1]{0:T(128)} %bitcast.me_ref, bf16[1024,256]{1,0:T(8,128)(2,1)} %ws_hbm.1, bf16[1024,256]{1,0:T(8,128)(2,1)} %wn_hbm.1), custom_call_target="tpu_custom_call" | custom-call | tf_op jit(solution)/shard_map/weights/pallas_call | solution.py:174
  69.8 0.0 collective-permute-done.7.b.refs_1_
  69.8 3.0 %collective-permute-done.8.c.refs_2_ = bf16[256,256]{1,0:T(8,128)(2,1)S(1)} collective-permute-done((bf16[256,256]{1,0:T(8,128)(2,1)S(1)}, bf16[256,256]{1,0:T(8,128)(2,1)S(1)}, u32[]{:S(2)}, u32[]{:S(2)}) %collective-permute-start.8) | collective-permute-done | bytes 131104 | tf_op jit(solution)/shard_map/ppermute | solution.py:458
  72.7 0.6 collective-permute-done.9.d.refs_3_
  73.4 0.3 halo_hidden.1.refs_9_
  73.7 1.7 %collective-permute-start.13 = (bf16[256,256]{1,0:T(8,128)(2,1)S(1)}, bf16[256,256]{1,0:T(8,128)(2,1)S(1)}, u32[]{:S(2)}, u32[]{:S(2)}) collective-permute-start(bf16[256,256]{1,0:T(8,128)(2,1)S(1)} %halo_hidden.1.refs_9_), channel_id=1, source_target_pairs={{0,2},{1,3},{2,4},{3,5},{4,6},{5,7},{6,0},{7,1},{8,10},{9,11},{10,... | collective-permute-start | bytes 393224 | tf_op jit(solution)/shard_map/ppermute | solution.py:463
  75.4 2.9 %collective-permute-start.14 = (bf16[256,256]{1,0:T(8,128)(2,1)S(1)}, bf16[256,256]{1,0:T(8,128)(2,1)S(1)}, u32[]{:S(2)}, u32[]{:S(2)}) collective-permute-start(bf16[256,256]{1,0:T(8,128)(2,1)S(1)} %halo_hidden.1.refs_9_), channel_id=1, source_target_pairs={{0,4},{1,5},{2,6},{3,7},{4,0},{5,1},{6,2},{7,3},{8,12},{9,13},{10,... | collective-permute-start | bytes 393224 | tf_op jit(solution)/shard_map/ppermute | solution.py:463
  78.3 1.3 %collective-permute-start.15 = (bf16[256,256]{1,0:T(8,128)(2,1)S(1)}, bf16[256,256]{1,0:T(8,128)(2,1)S(1)}, u32[]{:S(2)}, u32[]{:S(2)}) collective-permute-start(bf16[256,256]{1,0:T(8,128)(2,1)S(1)} %halo_hidden.1.refs_9_), channel_id=1, source_target_pairs={{0,6},{1,7},{2,0},{3,1},{4,2},{5,3},{6,4},{7,5},{8,14},{9,15},{10,... | collective-permute-start | bytes 393224 | tf_op jit(solution)/shard_map/ppermute | solution.py:463
  79.6 1.4 %collective-permute-start.10 = (bf16[256,128]{1,0:T(8,128)(2,1)S(1)}, bf16[256,128]{1,0:T(8,128)(2,1)S(1)}, u32[]{:S(2)}, u32[]{:S(2)}) collective-permute-start(bf16[256,128]{1,0:T(8,128)(2,1)S(1)} %get-tuple-element.47), channel_id=1, source_target_pairs={{0,8},{8,16},{16,24},{24,0},{32,40},{40,48},{48,56},{56,32},{64,72... | collective-permute-start | bytes 196616 | tf_op jit(solution)/shard_map/ppermute | solution.py:459
  81.0 1.5 %collective-permute-start.11 = (bf16[256,128]{1,0:T(8,128)(2,1)S(1)}, bf16[256,128]{1,0:T(8,128)(2,1)S(1)}, u32[]{:S(2)}, u32[]{:S(2)}) collective-permute-start(bf16[256,128]{1,0:T(8,128)(2,1)S(1)} %get-tuple-element.48), channel_id=1, source_target_pairs={{0,16},{8,24},{16,0},{24,8},{32,48},{40,56},{48,32},{56,40},{64,80... | collective-permute-start | bytes 196616 | tf_op jit(solution)/shard_map/ppermute | solution.py:459
  82.5 2.0 %collective-permute-done.10.refs_5_ = bf16[256,128]{1,0:T(8,128)(2,1)S(1)} collective-permute-done((bf16[256,128]{1,0:T(8,128)(2,1)S(1)}, bf16[256,128]{1,0:T(8,128)(2,1)S(1)}, u32[]{:S(2)}, u32[]{:S(2)}) %collective-permute-start.10) | collective-permute-done | bytes 65568 | tf_op jit(solution)/shard_map/ppermute | solution.py:459
  84.4 0.0 collective-permute-start.16
  84.5 0.0 collective-permute-done.13.rest_0_
  84.5 0.5 collective-permute-start.17
  85.0 0.0 collective-permute-done.14.rest_1_
  85.0 0.1 collective-permute-start.18
  85.1 0.0 collective-permute-done.15.rest_2_
  85.1 0.4 collective-permute-start.19
  85.5 1.3 %collective-permute-done.11.refs_6_ = bf16[256,128]{1,0:T(8,128)(2,1)S(1)} collective-permute-done((bf16[256,128]{1,0:T(8,128)(2,1)S(1)}, bf16[256,128]{1,0:T(8,128)(2,1)S(1)}, u32[]{:S(2)}, u32[]{:S(2)}) %collective-permute-start.11) | collective-permute-done | bytes 65568 | tf_op jit(solution)/shard_map/ppermute | solution.py:459
  86.7 0.7 collective-permute-start.12
  87.4 4.8 %mask_tiles.1 = (bf16[1024,256]{1,0:T(8,128)(2,1)S(1)}, bf16[1024,128]{1,0:T(8,128)(2,1)S(1)}, bf16[1024,640]{1,0:T(8,128)(2,1)}, bf16[1024,768]{1,0:T(8,128)(2,...) custom-call(s32[1]{0:T(128)} %bitcast.me_ref, s32[8,22]{1,0:T(8,128)S(1)} %copy-done, ...), custom_call_target="tpu_custom_call" | custom-call | tf_op jit(solution)/shard_map/mask_tiles/pallas_call | solution.py:318
  92.2 1.5 %mid_hidden.1 = (f32[384,256]{1,0:T(8,128)}, f32[1024,256]{1,0:T(8,128)S(1)}) custom-call(bf16[256,256]{1,0:T(8,128)(2,1)S(1)} %get-tuple-element.42.a.refs_0_, bf16[256,256]{1,0:T(8,128)(2,1)S(1)} %collective-permute-done.7.b.refs_1_, bf16[256,256]{1,0:T(8,128)(2,1)S(1)} %collective-permute-done.8.c.refs_2_, ...), custom_call_target="tpu_custom_call" | custom-call | tf_op jit(solution)/shard_map/mid_hidden/pallas_call | solution.py:248
  93.7 1.1 %shard_map.73.acc_ref = f32[1024,256]{1,0:T(8,128)S(1)} custom-call(f32[1024,256]{1,0:T(8,128)S(1)} %get-tuple-element.53.acc_ref, bf16[1024,768]{1,0:T(8,128)(2,1)S(1)} %get-tuple-element.54.live_ref, bf16[256,256]{1,0:T(8,128)(2,1)S(1)} %collective-permute-done.13.rest_0_, bf16[256,256]{1,0:T(8,128)(2,1)S(1)} %collective-permute-done.14.rest_1_, ...), custom_call_target="tpu_custom_call" | custom-call | tf_op jit(solution)/shard_map/pallas_call | solution.py:368
  94.8 0.0 collective-permute-done.16.rest_0_
  94.8 0.0 collective-permute-done.19.rest_3_
  94.8 0.0 copy-start.1
  94.8 1.3 %shard_map.74.acc_ref = f32[1024,256]{1,0:T(8,128)S(1)} custom-call(f32[1024,256]{1,0:T(8,128)S(1)} %shard_map.73.acc_ref, bf16[1024,1024]{1,0:T(8,128)(2,1)S(1)} %get-tuple-element.55.live_ref, bf16[256,256]{1,0:T(8,128)(2,1)S(1)} %collective-permute-done.16.rest_0_, bf16[256,256]{1,0:T(8,128)(2,1)S(1)} %collective-permute-done.17.rest_1_, ...), custom_call_target="tpu_custom_call" | custom-call | tf_op jit(solution)/shard_map/pallas_call | solution.py:368
  96.1 4.0 %last_step.1 = bf16[1024,256]{1,0:T(8,128)(2,1)} custom-call(bf16[1024,640]{1,0:T(8,128)(2,1)S(1)} %bitcast.3, bf16[1024,512]{1,0:T(8,128)(2,1)S(1)} %get-tuple-element.33.w_ref, f32[1024,256]{1,0:T(8,128)S(1)} %shard_map.74.acc_ref, bf16[1024,640]{1,0:T(8,128)(2,1)} %get-tuple-element.56.tail_hbm, f32[1024,128]{1,0:T(8,128)} %get-tuple-element.57.scale_hbm, ...), custom_call_target="tpu_custom_call" | custom-call | tf_op jit(solution)/shard_map/last_step/pallas_call | solution.py:420
  (7 shorter events, 0.0 us)
Async XLA Ops:
  2.8 93.3 %all-to-all-start = ((bf16[32,32,640]{2,1,0:T(8,128)(2,1)}), bf16[32,32,640]{2,1,0:T(8,128)(2,1)S(1)}, u32[]{:S(2)}, u32[]{:S(2)}) async-start(bf16[32,32,640]{2,1,0:T(8,128)(2,1)} %get-tuple-element.32), calls=%async_computation | async-start | bytes 2621440 | tf_op jit(solution)/shard_map/all_to_all | solution.py:448
  14.4 73.0 %copy-start = (s32[8,22]{1,0:T(8,128)S(1)}, s32[8,22]{1,0:T(8,128)}, u32[]{:S(2)}) copy-start(s32[8,22]{1,0:T(8,128)} %mask_ref.1) | copy-start | bytes 2116
  14.4 34.8 %collective-permute-start = (bf16[4,32,384]{2,1,0:T(8,128)(2,1)S(1)}, bf16[4,32,384]{2,1,0:T(8,128)(2,1)S(1)}, u32[]{:S(2)}, u32[]{:S(2)}) collective-permute-start(bf16[4,32,384]{2,1,0:T(8,128)(2,1)S(1)} %get-tuple-element.35), channel_id=1, source_target_pairs={{0,32},{8,40},{16,48},{24,56},{32,64},{40,72},{48,80},{56,88},{64,... | collective-permute-start | bytes 294920 | tf_op jit(solution)/shard_map/ppermute | solution.py:447
  16.0 38.7 %collective-permute-start.1 = (bf16[4,32,384]{2,1,0:T(8,128)(2,1)S(1)}, bf16[4,32,384]{2,1,0:T(8,128)(2,1)S(1)}, u32[]{:S(2)}, u32[]{:S(2)}) collective-permute-start(bf16[4,32,384]{2,1,0:T(8,128)(2,1)S(1)} %get-tuple-element.36), channel_id=1, source_target_pairs={{0,64},{8,72},{16,80},{24,88},{32,96},{40,104},{48,112},{56,120},{... | collective-permute-start | bytes 294920 | tf_op jit(solution)/shard_map/ppermute | solution.py:447
  18.3 41.4 %collective-permute-start.2 = (bf16[4,32,384]{2,1,0:T(8,128)(2,1)S(1)}, bf16[4,32,384]{2,1,0:T(8,128)(2,1)S(1)}, u32[]{:S(2)}, u32[]{:S(2)}) collective-permute-start(bf16[4,32,384]{2,1,0:T(8,128)(2,1)S(1)} %get-tuple-element.37), channel_id=1, source_target_pairs={{0,96},{8,104},{16,112},{24,120},{32,128},{40,136},{48,144},{56,15... | collective-permute-start | bytes 294920 | tf_op jit(solution)/shard_map/ppermute | solution.py:447
  21.0 42.5 %collective-permute-start.3 = (bf16[4,32,384]{2,1,0:T(8,128)(2,1)S(1)}, bf16[4,32,384]{2,1,0:T(8,128)(2,1)S(1)}, u32[]{:S(2)}, u32[]{:S(2)}) collective-permute-start(bf16[4,32,384]{2,1,0:T(8,128)(2,1)S(1)} %get-tuple-element.38), channel_id=1, source_target_pairs={{0,128},{8,136},{16,144},{24,152},{32,160},{40,168},{48,176},{56,1... | collective-permute-start | bytes 294920 | tf_op jit(solution)/shard_map/ppermute | solution.py:447
  23.4 40.2 %collective-permute-start.4 = (bf16[4,32,384]{2,1,0:T(8,128)(2,1)S(1)}, bf16[4,32,384]{2,1,0:T(8,128)(2,1)S(1)}, u32[]{:S(2)}, u32[]{:S(2)}) collective-permute-start(bf16[4,32,384]{2,1,0:T(8,128)(2,1)S(1)} %get-tuple-element.39), channel_id=1, source_target_pairs={{0,160},{8,168},{16,176},{24,184},{32,192},{40,200},{48,208},{56,2... | collective-permute-start | bytes 294920 | tf_op jit(solution)/shard_map/ppermute | solution.py:447
  49.2 14.4 %collective-permute-start.5 = (bf16[4,32,384]{2,1,0:T(8,128)(2,1)S(1)}, bf16[4,32,384]{2,1,0:T(8,128)(2,1)S(1)}, u32[]{:S(2)}, u32[]{:S(2)}) collective-permute-start(bf16[4,32,384]{2,1,0:T(8,128)(2,1)S(1)} %get-tuple-element.40), channel_id=1, source_target_pairs={{0,192},{8,200},{16,208},{24,216},{32,224},{40,232},{48,240},{56,2... | collective-permute-start | bytes 294920 | tf_op jit(solution)/shard_map/ppermute | solution.py:447
  54.6 8.9 %collective-permute-start.6 = (bf16[4,32,384]{2,1,0:T(8,128)(2,1)S(1)}, bf16[4,32,384]{2,1,0:T(8,128)(2,1)S(1)}, u32[]{:S(2)}, u32[]{:S(2)}) collective-permute-start(bf16[4,32,384]{2,1,0:T(8,128)(2,1)S(1)} %get-tuple-element.41), channel_id=1, source_target_pairs={{0,224},{8,232},{16,240},{24,248},{32,0},{40,8},{48,16},{56,24},{6... | collective-permute-start | bytes 294920 | tf_op jit(solution)/shard_map/ppermute | solution.py:447
  63.6 6.1 %collective-permute-start.7 = (bf16[256,256]{1,0:T(8,128)(2,1)S(1)}, bf16[256,256]{1,0:T(8,128)(2,1)S(1)}, u32[]{:S(2)}, u32[]{:S(2)}) collective-permute-start(bf16[256,256]{1,0:T(8,128)(2,1)S(1)} %get-tuple-element.43), channel_id=1, source_target_pairs={{0,8},{8,16},{16,24},{24,0},{32,40},{40,48},{48,56},{56,32},{64,72... | collective-permute-start | bytes 393224 | tf_op jit(solution)/shard_map/ppermute | solution.py:458
  65.2 7.6 %collective-permute-start.8 = (bf16[256,256]{1,0:T(8,128)(2,1)S(1)}, bf16[256,256]{1,0:T(8,128)(2,1)S(1)}, u32[]{:S(2)}, u32[]{:S(2)}) collective-permute-start(bf16[256,256]{1,0:T(8,128)(2,1)S(1)} %get-tuple-element.44), channel_id=1, source_target_pairs={{0,16},{8,24},{16,0},{24,8},{32,48},{40,56},{48,32},{56,40},{64,80... | collective-permute-start | bytes 393224 | tf_op jit(solution)/shard_map/ppermute | solution.py:458
  66.3 7.0 %collective-permute-start.9 = (bf16[256,256]{1,0:T(8,128)(2,1)S(1)}, bf16[256,256]{1,0:T(8,128)(2,1)S(1)}, u32[]{:S(2)}, u32[]{:S(2)}) collective-permute-start(bf16[256,256]{1,0:T(8,128)(2,1)S(1)} %get-tuple-element.45), channel_id=1, source_target_pairs={{0,24},{8,0},{16,8},{24,16},{32,56},{40,32},{48,40},{56,48},{64,88... | collective-permute-start | bytes 393224 | tf_op jit(solution)/shard_map/ppermute | solution.py:458
  73.7 10.8 %collective-permute-start.13 = (bf16[256,256]{1,0:T(8,128)(2,1)S(1)}, bf16[256,256]{1,0:T(8,128)(2,1)S(1)}, u32[]{:S(2)}, u32[]{:S(2)}) collective-permute-start(bf16[256,256]{1,0:T(8,128)(2,1)S(1)} %halo_hidden.1.refs_9_), channel_id=1, source_target_pairs={{0,2},{1,3},{2,4},{3,5},{4,6},{5,7},{6,0},{7,1},{8,10},{9,11},{10,... | collective-permute-start | bytes 393224 | tf_op jit(solution)/shard_map/ppermute | solution.py:463
  75.4 9.6 %collective-permute-start.14 = (bf16[256,256]{1,0:T(8,128)(2,1)S(1)}, bf16[256,256]{1,0:T(8,128)(2,1)S(1)}, u32[]{:S(2)}, u32[]{:S(2)}) collective-permute-start(bf16[256,256]{1,0:T(8,128)(2,1)S(1)} %halo_hidden.1.refs_9_), channel_id=1, source_target_pairs={{0,4},{1,5},{2,6},{3,7},{4,0},{5,1},{6,2},{7,3},{8,12},{9,13},{10,... | collective-permute-start | bytes 393224 | tf_op jit(solution)/shard_map/ppermute | solution.py:463
  78.3 6.8 %collective-permute-start.15 = (bf16[256,256]{1,0:T(8,128)(2,1)S(1)}, bf16[256,256]{1,0:T(8,128)(2,1)S(1)}, u32[]{:S(2)}, u32[]{:S(2)}) collective-permute-start(bf16[256,256]{1,0:T(8,128)(2,1)S(1)} %halo_hidden.1.refs_9_), channel_id=1, source_target_pairs={{0,6},{1,7},{2,0},{3,1},{4,2},{5,3},{6,4},{7,5},{8,14},{9,15},{10,... | collective-permute-start | bytes 393224 | tf_op jit(solution)/shard_map/ppermute | solution.py:463
  79.6 4.8 %collective-permute-start.10 = (bf16[256,128]{1,0:T(8,128)(2,1)S(1)}, bf16[256,128]{1,0:T(8,128)(2,1)S(1)}, u32[]{:S(2)}, u32[]{:S(2)}) collective-permute-start(bf16[256,128]{1,0:T(8,128)(2,1)S(1)} %get-tuple-element.47), channel_id=1, source_target_pairs={{0,8},{8,16},{16,24},{24,0},{32,40},{40,48},{48,56},{56,32},{64,72... | collective-permute-start | bytes 196616 | tf_op jit(solution)/shard_map/ppermute | solution.py:459
  81.0 5.8 %collective-permute-start.11 = (bf16[256,128]{1,0:T(8,128)(2,1)S(1)}, bf16[256,128]{1,0:T(8,128)(2,1)S(1)}, u32[]{:S(2)}, u32[]{:S(2)}) collective-permute-start(bf16[256,128]{1,0:T(8,128)(2,1)S(1)} %get-tuple-element.48), channel_id=1, source_target_pairs={{0,16},{8,24},{16,0},{24,8},{32,48},{40,56},{48,32},{56,40},{64,80... | collective-permute-start | bytes 196616 | tf_op jit(solution)/shard_map/ppermute | solution.py:459
  84.4 10.3 %collective-permute-start.16 = (bf16[256,256]{1,0:T(8,128)(2,1)S(1)}, bf16[256,256]{1,0:T(8,128)(2,1)S(1)}, u32[]{:S(2)}, u32[]{:S(2)}) collective-permute-start(bf16[256,256]{1,0:T(8,128)(2,1)S(1)} %halo_hidden.1.refs_9_), channel_id=1, source_target_pairs={{0,1},{1,0},{2,3},{3,2},{4,5},{5,4},{6,7},{7,6},{8,9},{9,8},{10,11... | collective-permute-start | bytes 393224 | tf_op jit(solution)/shard_map/ppermute | solution.py:464
  84.5 10.3 %collective-permute-start.17 = (bf16[256,256]{1,0:T(8,128)(2,1)S(1)}, bf16[256,256]{1,0:T(8,128)(2,1)S(1)}, u32[]{:S(2)}, u32[]{:S(2)}) collective-permute-start(bf16[256,256]{1,0:T(8,128)(2,1)S(1)} %collective-permute-done.13.rest_0_), channel_id=1, source_target_pairs={{0,1},{1,0},{2,3},{3,2},{4,5},{5,4},{6,7},{7,6},{8,9},{9,8},{10,11... | collective-permute-start | bytes 393224 | tf_op jit(solution)/shard_map/ppermute | solution.py:464
  85.0 9.8 %collective-permute-start.18 = (bf16[256,256]{1,0:T(8,128)(2,1)S(1)}, bf16[256,256]{1,0:T(8,128)(2,1)S(1)}, u32[]{:S(2)}, u32[]{:S(2)}) collective-permute-start(bf16[256,256]{1,0:T(8,128)(2,1)S(1)} %collective-permute-done.14.rest_1_), channel_id=1, source_target_pairs={{0,1},{1,0},{2,3},{3,2},{4,5},{5,4},{6,7},{7,6},{8,9},{9,8},{10,11... | collective-permute-start | bytes 393224 | tf_op jit(solution)/shard_map/ppermute | solution.py:464
  85.1 9.8 %collective-permute-start.19 = (bf16[256,256]{1,0:T(8,128)(2,1)S(1)}, bf16[256,256]{1,0:T(8,128)(2,1)S(1)}, u32[]{:S(2)}, u32[]{:S(2)}) collective-permute-start(bf16[256,256]{1,0:T(8,128)(2,1)S(1)} %collective-permute-done.15.rest_2_), channel_id=1, source_target_pairs={{0,1},{1,0},{2,3},{3,2},{4,5},{5,4},{6,7},{7,6},{8,9},{9,8},{10,11... | collective-permute-start | bytes 393224 | tf_op jit(solution)/shard_map/ppermute | solution.py:464
  86.7 5.5 %collective-permute-start.12 = (bf16[256,128]{1,0:T(8,128)(2,1)S(1)}, bf16[256,128]{1,0:T(8,128)(2,1)S(1)}, u32[]{:S(2)}, u32[]{:S(2)}) collective-permute-start(bf16[256,128]{1,0:T(8,128)(2,1)S(1)} %get-tuple-element.49), channel_id=1, source_target_pairs={{0,24},{8,0},{16,8},{24,16},{32,56},{40,32},{48,40},{56,48},{64,88... | collective-permute-start | bytes 196616 | tf_op jit(solution)/shard_map/ppermute | solution.py:459
  94.8 1.3 %copy-start.1 = (f32[256]{0:T(256)S(1)}, f32[256]{0:T(256)}, u32[]{:S(2)}) copy-start(f32[256]{0:T(256)} %param.13) | copy-start | bytes 3076

commit v6 on v5

--- a/solution.py
+++ b/solution.py
@@ -27,6 +27,15 @@
     ]
 
 
+def way_shift(dz):
+    pairs = []
+    for feat in range(NZ * NX):
+        for b in range(NB):
+            z = (feat // NX + (1 - 2 * (b % 2)) * dz) % NZ
+            pairs.append((feat * NB + b, (z * NX + feat % NX) * NB + b))
+    return pairs
+
+
 def blk_shift(dy, dc):
     return [(y * 2 + c, (y + dy) % 4 * 2 + (c + dc) % 2) for y in range(4) for c in range(2)]
 
@@ -36,6 +45,10 @@
     return feat // NX, feat % NX
 
 
+def way_of(me_ref):
+    return 1 - 2 * (me_ref[0] % 2)
+
+
 def in_hbm(x):
     return pltpu.with_memory_space_constraint(x, pltpu.HBM)
 
@@ -44,11 +57,13 @@
     return pltpu.HBM(shape, dtype)
 
 
-def swap_matrix(g, z, x):
+def swap_matrix(g, z, x, way):
     rows = 8 * g
     r = lax.broadcasted_iota(jnp.int32, (rows, rows), 0)
     c = lax.broadcasted_iota(jnp.int32, (rows, rows), 1)
-    place_of = (((r >> 5) + z) & (NZ - 1)) * NX + (((r >> 3) + x) & (NX - 1))
+    slot = r >> 5
+    step = jnp.where(slot <= NZ // 2, slot, NZ // 2 - slot) * way
+    place_of = ((step + z) & (NZ - 1)) * NX + (((r >> 3) + x) & (NX - 1))
     return jnp.where(c == (r & 7) * g + place_of, 1.0, 0.0).astype(BF)
 
 
@@ -63,9 +78,9 @@
 
 
 def split_kernel(me_ref, x_hbm, *rest):
-    heads, (tail_hbm, x_ref, tail_ref, sem) = rest[:NZ], rest[NZ:]
+    own_ref, keep_ref, four_ref, give_ref, tail_hbm, x_ref, tail_ref, sem = rest
     f, g, n = x_ref.shape
-    early = heads[0].shape[2]
+    early = own_ref.shape[2]
     chunks = range(0, f, 16)
 
     def load(i, f0, start, size, which):
@@ -76,9 +91,10 @@
     soon = [load(i, f0, 0, early, 1) for i, f0 in enumerate(chunks)]
     for copy in late + soon:
         copy.start()
-    zero = jnp.int32(0)
-    plain = swap_matrix(g, zero, zero)
-    turned = swap_matrix(g, *place(me_ref))
+    r = lax.broadcasted_iota(jnp.int32, (8 * g, 8 * g), 0)
+    c = lax.broadcasted_iota(jnp.int32, (8 * g, 8 * g), 1)
+    plain = jnp.where(c == (r & 7) * g + (r >> 3), 1.0, 0.0).astype(BF)
+    turned = swap_matrix(g, *place(me_ref), way_of(me_ref))
     outs = []
     for i, f0 in enumerate(chunks):
         late[i].wait()
@@ -94,8 +110,11 @@
         for n0 in range(0, early, 2 * TILE):
             at = slice(n0, min(n0 + 2 * TILE, early))
             block = swapped(turned, x_ref, f0, at)
-            for dz in range(NZ):
-                heads[dz][:, f0 : f0 + 16, at] = block[dz * NX : (dz + 1) * NX]
+            own_ref[:, f0 : f0 + 16, at] = block[:NX]
+            four_ref[:, f0 : f0 + 16, at] = block[4 * NX : 5 * NX]
+            for k in range(3):
+                keep_ref[k, :, f0 : f0 + 16, at] = block[(k + 1) * NX : (k + 2) * NX]
+                give_ref[k, :, f0 : f0 + 16, at] = block[(k + 5) * NX : (k + 6) * NX]
     for copy in outs:
         copy.wait()
 
@@ -103,48 +122,87 @@
 def split(me, features, early):
     f, g, n = features.shape
     away = pl.BlockSpec(memory_space=pltpu.HBM)
-    *heads, tail = pl.pallas_call(
+    one, three = (NX, f, early), (3, NX, f, early)
+    return pl.pallas_call(
         split_kernel,
         grid_spec=pltpu.PrefetchScalarGridSpec(
             num_scalar_prefetch=1,
             grid=(1,),
             in_specs=[away],
-            out_specs=[full((NX, f, early))] * NZ + [away],
+            out_specs=[full(one), full(three), full(one), full(three), away],
             scratch_shapes=[
                 pltpu.VMEM((f, g, n), BF),
                 pltpu.VMEM((g, f, n - early), BF),
                 pltpu.SemaphoreType.DMA((3, f // 16)),
             ],
         ),
-        out_shape=[jax.ShapeDtypeStruct((NX, f, early), BF)] * NZ + [hbm((g, f, n - early), BF)],
+        out_shape=[jax.ShapeDtypeStruct(shape, BF) for shape in (one, three, one, three)]
+        + [hbm((g, f, n - early), BF)],
         compiler_params=VM,
         name="split",
     )(me, features)
-    return heads, tail
-
-
-def regroup_kernel(*refs):
-    ins, outs = refs[:NZ], refs[NZ:]
-    f, halo = ins[0].shape[1], outs[0].shape[1]
+
+
+def join_kernel(keep_ref, got_ref, *outs):
+    for k, out in enumerate(outs):
+        out[0] = keep_ref[k]
+        out[1] = got_ref[k]
+
+
+def join(keep, got):
+    _, nx, f, early = keep.shape
+    return pl.pallas_call(
+        join_kernel,
+        grid=(1,),
+        in_specs=[full(keep.shape)] * 2,
+        out_specs=[full((2, nx, f, early))] * 3,
+        out_shape=[jax.ShapeDtypeStruct((2, nx, f, early), BF)] * 3,
+        compiler_params=VM,
+        name="join",
+    )(keep, got)
+
+
+def pack_kernel(a, b, c, o_ref):
+    for k, part in enumerate((a, b, c)):
+        o_ref[k] = part[1]
+
+
+def pack(parts):
+    _, nx, f, early = parts[0].shape
+    return pl.pallas_call(
+        pack_kernel,
+        grid=(1,),
+        in_specs=[full(parts[0].shape)] * 3,
+        out_specs=full((3, nx, f, early)),
+        out_shape=jax.ShapeDtypeStruct((3, nx, f, early), BF),
+        compiler_params=VM,
+        name="pack",
+    )(*parts)
+
+
+def regroup_kernel(own, a, b, c, four, back, *outs):
+    f, halo = own.shape[1], outs[0].shape[1]
     for j in range(NX):
-        for dz in range(NZ):
-            at = slice(dz * f, (dz + 1) * f)
-            outs[j][at, :] = ins[dz][j, :, :halo]
-            outs[NX + j][at, :] = ins[dz][j, :, halo:]
-
-
-def regroup(parts, halo):
-    _, f, early = parts[0].shape
+        pieces = [own[j], a[0, j], b[0, j], c[0, j], four[j]] + [back[k, j] for k in range(3)]
+        for slot, piece in enumerate(pieces):
+            at = slice(slot * f, (slot + 1) * f)
+            outs[j][at, :] = piece[:, :halo]
+            outs[NX + j][at, :] = piece[:, halo:]
+
+
+def regroup(own, landed, four, back, halo):
+    _, f, early = own.shape
+    args = (own, *landed, four, back)
     shapes = [(NZ * f, halo)] * NX + [(NZ * f, early - halo)] * NX
     return pl.pallas_call(
         regroup_kernel,
         grid=(1,),
-        in_specs=[full((NX, f, early))] * NZ,
+        in_specs=[full(a.shape) for a in args],
         out_specs=[full(shape) for shape in shapes],
         out_shape=[jax.ShapeDtypeStruct(shape, BF) for shape in shapes],
         compiler_params=VM,
         name="regroup",
-    )(*parts)
+    )(*args)
 
 
 def weights_kernel(me_ref, ws_hbm, wn_hbm, rot_ref, turned_ref, ws_ref, wn_ref, sem):
@@ -154,7 +212,7 @@
     ]
     for copy in copies:
         copy.start()
-    z, x = place(me_ref)
+    (z, x), way = place(me_ref), way_of(me_ref)
     total, hid = ws_ref.shape
     f = total // (NZ * NX)
     for half, w_ref in enumerate((ws_ref, wn_ref)):
@@ -163,7 +221,8 @@
         turned_ref[:, at] = w_ref[...]
         for j in range(NX):
             for dz in range(NZ):
-                src = ((z + (NZ - dz)) % NZ * NX + (x + (NX - j)) % NX) * f
+                step = -dz if dz <= NZ // 2 else dz - NZ // 2
+                src = (((z + way * step + NZ) % NZ) * NX + (x + (NX - j)) % NX) * f
                 to = (j * NZ + dz) * f
                 rot_ref[to : to + f, at] = w_ref[pl.ds(pl.multiple_of(src, f), f), :]
 
@@ -441,10 +500,12 @@
     me = lax.axis_index(("feat", "blk")).reshape(1)
     features = in_hbm(features)
 
-    head, rest = split(me, features, EARLY)
-    landed = [head[0]]
-    for dz in range(1, NZ):
-        landed.append(lax.ppermute(head[dz], "feat", feat_shift(dz, 0)))
+    own, keep, four, give, rest = split(me, features, EARLY)
+    got = lax.ppermute(give, "blk", blk_shift(0, 1))
+    four = lax.ppermute(four, "feat", feat_shift(NZ // 2, 0))
+    landed = []
+    for k, part in enumerate(join(keep, got)):
+        landed.append(lax.ppermute(part, ("feat", "blk"), way_shift(k + 1)))
     rest = lax.all_to_all(rest, "feat", split_axis=0, concat_axis=0, tiled=True)
     rest = rest.reshape(-1, rest.shape[-1])
 
@@ -452,7 +513,8 @@
     live_head, live_mid, live_tail, live_near, live_far, scale = mask_tiles(
         me, tile_mask, adj_local, adj_remote, halo, EARLY
     )
-    rows = regroup(landed, halo)
+    back = lax.ppermute(pack(landed), "blk", blk_shift(0, 1))
+    rows = regroup(own, landed, four, back, halo)
     parts, mids = [rows[0]], [rows[NX]]
     for j in range(1, NX):
         parts.append(lax.ppermute(rows[j], "feat", feat_shift(0, j)))

time: 102 us -> 107 us (1.049)
  waiting for transfers between devices: 40.8 us -> 53.1 us
  starting transfers between devices: 42.1 us -> 35.7 us
    ppermute x7 -> x6, waiting for transfers between devices: 33.9 us -> 46.1 us  [the longest x3 36.3 us: shards(): landed.append(lax.ppermute(part, ('feat', 'blk'), way_shift(k + 1)))]
    ppermute x7 -> x6, starting transfers between devices: 15.2 us -> 8.33 us  [the longest x3 6.63 us: shards(): landed.append(lax.ppermute(part, ('feat', 'blk'), way_shift(k + 1)))]
  transfers between devices with their start and end apart: 21 -> 20, of which waited for: 8 -> 9; matrix products, arithmetic and copies ran while one was open for 0% -> 0% of each run, Pallas kernels for 10% -> 10%
where the time goes in v6:
time: 107 us; the launch traced here: 106 us
  waiting for transfers between devices  53.1 us (50%)
  starting transfers between devices  35.7 us (33%)
  Pallas kernels  17.1 us (16%)
    ppermute x3, waiting for transfers between devices, shards(): landed.append(lax.ppermute(part, ('feat', 'blk'), way_shift(k + 1)))  36.3 us
    all_to_all x1, starting transfers between devices, shards(): rest = lax.all_to_all(rest, 'feat', split_axis=0, concat_axis=0, tiled=True)  11.6 us
    ppermute x1, waiting for transfers between devices, shards(): four = lax.ppermute(four, 'feat', feat_shift(NZ // 2, 0))  8.33 us
    ppermute x3, starting transfers between devices, shards(): landed.append(lax.ppermute(part, ('feat', 'blk'), way_shift(k + 1)))  6.63 us
    ppermute x3, starting transfers between devices, shards(): same.append(lax.ppermute(h_head, 'blk', blk_shift(dy, 0)))  5.9 us
    ppermute x3, starting transfers between devices, shards(): parts.append(lax.ppermute(rows[j], 'feat', feat_shift(0, j)))  4.8 us
    pallas_call x1, Pallas kernels, mask_tiles(): pl.pallas_call(mask_kernel, grid_spec=pltpu.PrefetchScalarGridSpec(num_sc...  4.76 us
    ppermute x3, waiting for transfers between devices, shards(): parts.append(lax.ppermute(rows[j], 'feat', feat_shift(0, j)))  4.12 us
  transfers between devices with their start and end apart: 20, of which 9 were waited for; matrix products, arithmetic and copies ran while one was open for 0% of the time, Pallas kernels for 10%

profile of v6, /device:TPU:2, one launch (start us, length us, event | category | flops | bytes accessed | tf_op | source)
XLA Modules:
  0.0 106.2 jit_solution(2762572318338722888)
XLA Ops:
  0.0 2.8 %split.1 = (bf16[4,32,384]{2,1,0:T(8,128)(2,1)S(1)}, bf16[3,4,32,384]{3,2,1,0:T(8,128)(2,1)S(1)}, bf16[4,32,384]{2,1,0:T(8,128)(2,1)S(1)}, bf16[3,4,32,384]{3,2,1,0:T(8,128)(2,1)S(1)}, bf16[32,32,640]{2,1,0:T(8,128)(2,1)}) custom-call(s32[1]{0:T(128)} %bitcast.me_ref, bf16[32,32,1024]{2,1,0:T(8,128)(2,1)} %x_hbm.1), custom_call_target="tpu_custom_call" | custom-call | tf_op jit(solution)/shard_map/split/pallas_call | solution.py:126
  2.8 11.6 %all-to-all-start = ((bf16[32,32,640]{2,1,0:T(8,128)(2,1)}), bf16[32,32,640]{2,1,0:T(8,128)(2,1)S(1)}, u32[]{:S(2)}, u32[]{:S(2)}) async-start(bf16[32,32,640]{2,1,0:T(8,128)(2,1)} %get-tuple-element.31), calls=%async_computation | async-start | bytes 2621440 | tf_op jit(solution)/shard_map/all_to_all | solution.py:509
  14.4 0.1 collective-permute-start
  14.5 1.6 %collective-permute-done.got_ref = bf16[3,4,32,384]{3,2,1,0:T(8,128)(2,1)S(1)} collective-permute-done((bf16[3,4,32,384]{3,2,1,0:T(8,128)(2,1)S(1)}, bf16[3,4,32,384]{3,2,1,0:T(8,128)(2,1)S(1)}, u32[]{:S(2)}, u32[]{:S(2)}) %collective-permute-start) | collective-permute-done | bytes 294944 | tf_op jit(solution)/shard_map/ppermute | solution.py:504
  16.1 0.1 join.1
  16.1 1.5 %collective-permute-start.1 = (bf16[2,4,32,384]{3,2,1,0:T(8,128)(2,1)S(1)}, bf16[2,4,32,384]{3,2,1,0:T(8,128)(2,1)S(1)}, u32[]{:S(2)}, u32[]{:S(2)}) collective-permute-start(bf16[2,4,32,384]{3,2,1,0:T(8,128)(2,1)S(1)} %get-tuple-element.36), channel_id=1, source_target_pairs={{0,32},{1,225},{2,34},{3,227},{4,36},{5,229},{6,38},{7,231},{8,40}... | collective-permute-start | bytes 589832 | tf_op jit(solution)/shard_map/ppermute | solution.py:508
  17.7 2.4 %collective-permute-start.2 = (bf16[2,4,32,384]{3,2,1,0:T(8,128)(2,1)S(1)}, bf16[2,4,32,384]{3,2,1,0:T(8,128)(2,1)S(1)}, u32[]{:S(2)}, u32[]{:S(2)}) collective-permute-start(bf16[2,4,32,384]{3,2,1,0:T(8,128)(2,1)S(1)} %get-tuple-element.37), channel_id=1, source_target_pairs={{0,64},{1,193},{2,66},{3,195},{4,68},{5,197},{6,70},{7,199},{8,72}... | collective-permute-start | bytes 589832 | tf_op jit(solution)/shard_map/ppermute | solution.py:508
  20.1 2.7 %collective-permute-start.3 = (bf16[2,4,32,384]{3,2,1,0:T(8,128)(2,1)S(1)}, bf16[2,4,32,384]{3,2,1,0:T(8,128)(2,1)S(1)}, u32[]{:S(2)}, u32[]{:S(2)}) collective-permute-start(bf16[2,4,32,384]{3,2,1,0:T(8,128)(2,1)S(1)} %get-tuple-element.38), channel_id=1, source_target_pairs={{0,96},{1,161},{2,98},{3,163},{4,100},{5,165},{6,102},{7,167},{8,1... | collective-permute-start | bytes 589832 | tf_op jit(solution)/shard_map/ppermute | solution.py:508
  22.8 24.8 %collective-permute-done.1.a = bf16[2,4,32,384]{3,2,1,0:T(8,128)(2,1)S(1)} collective-permute-done((bf16[2,4,32,384]{3,2,1,0:T(8,128)(2,1)S(1)}, bf16[2,4,32,384]{3,2,1,0:T(8,128)(2,1)S(1)}, u32[]{:S(2)}, u32[]{:S(2)}) %collective-permute-start.1) | collective-permute-done | bytes 196640 | tf_op jit(solution)/shard_map/ppermute | solution.py:508
  47.6 4.2 %collective-permute-done.2.b = bf16[2,4,32,384]{3,2,1,0:T(8,128)(2,1)S(1)} collective-permute-done((bf16[2,4,32,384]{3,2,1,0:T(8,128)(2,1)S(1)}, bf16[2,4,32,384]{3,2,1,0:T(8,128)(2,1)S(1)}, u32[]{:S(2)}, u32[]{:S(2)}) %collective-permute-start.2) | collective-permute-done | bytes 196640 | tf_op jit(solution)/shard_map/ppermute | solution.py:508
  51.7 7.3 %collective-permute-done.3.c = bf16[2,4,32,384]{3,2,1,0:T(8,128)(2,1)S(1)} collective-permute-done((bf16[2,4,32,384]{3,2,1,0:T(8,128)(2,1)S(1)}, bf16[2,4,32,384]{3,2,1,0:T(8,128)(2,1)S(1)}, u32[]{:S(2)}, u32[]{:S(2)}) %collective-permute-start.3) | collective-permute-done | bytes 196640 | tf_op jit(solution)/shard_map/ppermute | solution.py:508
  59.1 0.0 copy-start
  59.1 0.1 collective-permute-start.5
  59.2 1.5 %collective-permute-start.4 = (bf16[4,32,384]{2,1,0:T(8,128)(2,1)S(1)}, bf16[4,32,384]{2,1,0:T(8,128)(2,1)S(1)}, u32[]{:S(2)}, u32[]{:S(2)}) collective-permute-start(bf16[4,32,384]{2,1,0:T(8,128)(2,1)S(1)} %get-tuple-element.39), channel_id=1, source_target_pairs={{0,128},{8,136},{16,144},{24,152},{32,160},{40,168},{48,176},{56,1... | collective-permute-start | bytes 294920 | tf_op jit(solution)/shard_map/ppermute | solution.py:505
  60.7 8.3 %collective-permute-done.4.four = bf16[4,32,384]{2,1,0:T(8,128)(2,1)S(1)} collective-permute-done((bf16[4,32,384]{2,1,0:T(8,128)(2,1)S(1)}, bf16[4,32,384]{2,1,0:T(8,128)(2,1)S(1)}, u32[]{:S(2)}, u32[]{:S(2)}) %collective-permute-start.4) | collective-permute-done | bytes 98336 | tf_op jit(solution)/shard_map/ppermute | solution.py:505
  69.0 0.0 collective-permute-done.5.back
  69.0 0.1 regroup.1
  69.1 1.7 %collective-permute-start.6 = (bf16[256,256]{1,0:T(8,128)(2,1)S(1)}, bf16[256,256]{1,0:T(8,128)(2,1)S(1)}, u32[]{:S(2)}, u32[]{:S(2)}) collective-permute-start(bf16[256,256]{1,0:T(8,128)(2,1)S(1)} %get-tuple-element.41), channel_id=1, source_target_pairs={{0,8},{8,16},{16,24},{24,0},{32,40},{40,48},{48,56},{56,32},{64,72... | collective-permute-start | bytes 393224 | tf_op jit(solution)/shard_map/ppermute | solution.py:520
  70.8 2.7 %collective-permute-start.7 = (bf16[256,256]{1,0:T(8,128)(2,1)S(1)}, bf16[256,256]{1,0:T(8,128)(2,1)S(1)}, u32[]{:S(2)}, u32[]{:S(2)}) collective-permute-start(bf16[256,256]{1,0:T(8,128)(2,1)S(1)} %get-tuple-element.42), channel_id=1, source_target_pairs={{0,16},{8,24},{16,0},{24,8},{32,48},{40,56},{48,32},{56,40},{64,80... | collective-permute-start | bytes 393224 | tf_op jit(solution)/shard_map/ppermute | solution.py:520
  73.6 0.3 collective-permute-start.8
  73.9 1.3 %weights.1 = (bf16[1024,512]{1,0:T(8,128)(2,1)S(1)}, bf16[1024,512]{1,0:T(8,128)(2,1)S(1)}) custom-call(s32[1]{0:T(128)} %bitcast.me_ref, bf16[1024,256]{1,0:T(8,128)(2,1)} %ws_hbm.1, bf16[1024,256]{1,0:T(8,128)(2,1)} %wn_hbm.1), custom_call_target="tpu_custom_call" | custom-call | tf_op jit(solution)/shard_map/weights/pallas_call | solution.py:233
  75.2 0.0 collective-permute-done.6.b.refs_1_
  75.2 3.3 %collective-permute-done.7.c.refs_2_ = bf16[256,256]{1,0:T(8,128)(2,1)S(1)} collective-permute-done((bf16[256,256]{1,0:T(8,128)(2,1)S(1)}, bf16[256,256]{1,0:T(8,128)(2,1)S(1)}, u32[]{:S(2)}, u32[]{:S(2)}) %collective-permute-start.7) | collective-permute-done | bytes 131104 | tf_op jit(solution)/shard_map/ppermute | solution.py:520
  78.5 0.8 collective-permute-done.8.d.refs_3_
  79.3 0.3 halo_hidden.1.refs_9_
  79.7 1.7 %collective-permute-start.12 = (bf16[256,256]{1,0:T(8,128)(2,1)S(1)}, bf16[256,256]{1,0:T(8,128)(2,1)S(1)}, u32[]{:S(2)}, u32[]{:S(2)}) collective-permute-start(bf16[256,256]{1,0:T(8,128)(2,1)S(1)} %halo_hidden.1.refs_9_), channel_id=1, source_target_pairs={{0,2},{1,3},{2,4},{3,5},{4,6},{5,7},{6,0},{7,1},{8,10},{9,11},{10,... | collective-permute-start | bytes 393224 | tf_op jit(solution)/shard_map/ppermute | solution.py:525
  81.3 2.9 %collective-permute-start.13 = (bf16[256,256]{1,0:T(8,128)(2,1)S(1)}, bf16[256,256]{1,0:T(8,128)(2,1)S(1)}, u32[]{:S(2)}, u32[]{:S(2)}) collective-permute-start(bf16[256,256]{1,0:T(8,128)(2,1)S(1)} %halo_hidden.1.refs_9_), channel_id=1, source_target_pairs={{0,4},{1,5},{2,6},{3,7},{4,0},{5,1},{6,2},{7,3},{8,12},{9,13},{10,... | collective-permute-start | bytes 393224 | tf_op jit(solution)/shard_map/ppermute | solution.py:525
  84.2 1.3 %collective-permute-start.14 = (bf16[256,256]{1,0:T(8,128)(2,1)S(1)}, bf16[256,256]{1,0:T(8,128)(2,1)S(1)}, u32[]{:S(2)}, u32[]{:S(2)}) collective-permute-start(bf16[256,256]{1,0:T(8,128)(2,1)S(1)} %halo_hidden.1.refs_9_), channel_id=1, source_target_pairs={{0,6},{1,7},{2,0},{3,1},{4,2},{5,3},{6,4},{7,5},{8,14},{9,15},{10,... | collective-permute-start | bytes 393224 | tf_op jit(solution)/shard_map/ppermute | solution.py:525
  85.6 1.1 %collective-permute-start.9 = (bf16[256,128]{1,0:T(8,128)(2,1)S(1)}, bf16[256,128]{1,0:T(8,128)(2,1)S(1)}, u32[]{:S(2)}, u32[]{:S(2)}) collective-permute-start(bf16[256,128]{1,0:T(8,128)(2,1)S(1)} %get-tuple-element.45), channel_id=1, source_target_pairs={{0,8},{8,16},{16,24},{24,0},{32,40},{40,48},{48,56},{56,32},{64,72... | collective-permute-start | bytes 196616 | tf_op jit(solution)/shard_map/ppermute | solution.py:521
  86.7 1.9 %collective-permute-start.10 = (bf16[256,128]{1,0:T(8,128)(2,1)S(1)}, bf16[256,128]{1,0:T(8,128)(2,1)S(1)}, u32[]{:S(2)}, u32[]{:S(2)}) collective-permute-start(bf16[256,128]{1,0:T(8,128)(2,1)S(1)} %get-tuple-element.46), channel_id=1, source_target_pairs={{0,16},{8,24},{16,0},{24,8},{32,48},{40,56},{48,32},{56,40},{64,80... | collective-permute-start | bytes 196616 | tf_op jit(solution)/shard_map/ppermute | solution.py:521
  88.6 1.2 %collective-permute-done.9.refs_5_ = bf16[256,128]{1,0:T(8,128)(2,1)S(1)} collective-permute-done((bf16[256,128]{1,0:T(8,128)(2,1)S(1)}, bf16[256,128]{1,0:T(8,128)(2,1)S(1)}, u32[]{:S(2)}, u32[]{:S(2)}) %collective-permute-start.9) | collective-permute-done | bytes 65568 | tf_op jit(solution)/shard_map/ppermute | solution.py:521
  89.8 0.0 collective-permute-start.15
  89.9 0.5 collective-permute-start.16
  90.4 0.1 collective-permute-start.17
  90.5 0.4 collective-permute-start.18
  90.9 1.6 %collective-permute-done.10.refs_6_ = bf16[256,128]{1,0:T(8,128)(2,1)S(1)} collective-permute-done((bf16[256,128]{1,0:T(8,128)(2,1)S(1)}, bf16[256,128]{1,0:T(8,128)(2,1)S(1)}, u32[]{:S(2)}, u32[]{:S(2)}) %collective-permute-start.10) | collective-permute-done | bytes 65568 | tf_op jit(solution)/shard_map/ppermute | solution.py:521
  92.5 0.9 collective-permute-start.11
  93.4 4.8 %mask_tiles.1 = (bf16[1024,256]{1,0:T(8,128)(2,1)S(1)}, bf16[1024,128]{1,0:T(8,128)(2,1)S(1)}, bf16[1024,640]{1,0:T(8,128)(2,1)}, bf16[1024,768]{1,0:T(8,128)(2,...) custom-call(s32[1]{0:T(128)} %bitcast.me_ref, s32[8,22]{1,0:T(8,128)S(1)} %copy-done, ...), custom_call_target="tpu_custom_call" | custom-call | tf_op jit(solution)/shard_map/mask_tiles/pallas_call | solution.py:377
  98.1 0.0 collective-permute-done.11.refs_7_
  98.2 1.5 %mid_hidden.1 = (f32[384,256]{1,0:T(8,128)}, f32[1024,256]{1,0:T(8,128)S(1)}) custom-call(bf16[256,256]{1,0:T(8,128)(2,1)S(1)} %get-tuple-element.40.a.refs_0_, bf16[256,256]{1,0:T(8,128)(2,1)S(1)} %collective-permute-done.6.b.refs_1_, bf16[256,256]{1,0:T(8,128)(2,1)S(1)} %collective-permute-done.7.c.refs_2_, ...), custom_call_target="tpu_custom_call" | custom-call | tf_op jit(solution)/shard_map/mid_hidden/pallas_call | solution.py:307
  99.6 1.1 %shard_map.73.acc_ref = f32[1024,256]{1,0:T(8,128)S(1)} custom-call(f32[1024,256]{1,0:T(8,128)S(1)} %get-tuple-element.51.acc_ref, bf16[1024,768]{1,0:T(8,128)(2,1)S(1)} %get-tuple-element.52.live_ref, bf16[256,256]{1,0:T(8,128)(2,1)S(1)} %collective-permute-done.12.rest_0_, bf16[256,256]{1,0:T(8,128)(2,1)S(1)} %collective-permute-done.13.rest_1_, ...), custom_call_target="tpu_custom_call" | custom-call | tf_op jit(solution)/shard_map/pallas_call | solution.py:427
  100.7 0.0 collective-permute-done.15.rest_0_
  100.8 0.0 collective-permute-done.17.rest_2_
  100.8 0.0 collective-permute-done.18.rest_3_
  100.8 0.0 copy-start.1
  100.8 1.3 %shard_map.74.acc_ref = f32[1024,256]{1,0:T(8,128)S(1)} custom-call(f32[1024,256]{1,0:T(8,128)S(1)} %shard_map.73.acc_ref, bf16[1024,1024]{1,0:T(8,128)(2,1)S(1)} %get-tuple-element.53.live_ref, bf16[256,256]{1,0:T(8,128)(2,1)S(1)} %collective-permute-done.15.rest_0_, bf16[256,256]{1,0:T(8,128)(2,1)S(1)} %collective-permute-done.16.rest_1_, ...), custom_call_target="tpu_custom_call" | custom-call | tf_op jit(solution)/shard_map/pallas_call | solution.py:427
  102.1 0.0 all-to-all-done
  102.1 3.9 %last_step.1 = bf16[1024,256]{1,0:T(8,128)(2,1)} custom-call(bf16[1024,640]{1,0:T(8,128)(2,1)S(1)} %bitcast.3, bf16[1024,512]{1,0:T(8,128)(2,1)S(1)} %get-tuple-element.32.w_ref, f32[1024,256]{1,0:T(8,128)S(1)} %shard_map.74.acc_ref, bf16[1024,640]{1,0:T(8,128)(2,1)} %get-tuple-element.54.tail_hbm, f32[1024,128]{1,0:T(8,128)} %get-tuple-element.55.scale_hbm, ...), custom_call_target="tpu_custom_call" | custom-call | tf_op jit(solution)/shard_map/last_step/pallas_call | solution.py:479
  (7 shorter events, 0.0 us)
Async XLA Ops:
  2.8 99.3 %all-to-all-start = ((bf16[32,32,640]{2,1,0:T(8,128)(2,1)}), bf16[32,32,640]{2,1,0:T(8,128)(2,1)S(1)}, u32[]{:S(2)}, u32[]{:S(2)}) async-start(bf16[32,32,640]{2,1,0:T(8,128)(2,1)} %get-tuple-element.31), calls=%async_computation | async-start | bytes 2621440 | tf_op jit(solution)/shard_map/all_to_all | solution.py:509
  14.4 1.7 %collective-permute-start = (bf16[3,4,32,384]{3,2,1,0:T(8,128)(2,1)S(1)}, bf16[3,4,32,384]{3,2,1,0:T(8,128)(2,1)S(1)}, u32[]{:S(2)}, u32[]{:S(2)}) collective-permute-start(bf16[3,4,32,384]{3,2,1,0:T(8,128)(2,1)S(1)} %get-tuple-element.35), channel_id=1, source_target_pairs={{0,1},{1,0},{2,3},{3,2},{4,5},{5,4},{6,7},{7,6},{8,9},{9,8},{10,11... | collective-permute-start | bytes 884744 | tf_op jit(solution)/shard_map/ppermute | solution.py:504
  16.1 31.4 %collective-permute-start.1 = (bf16[2,4,32,384]{3,2,1,0:T(8,128)(2,1)S(1)}, bf16[2,4,32,384]{3,2,1,0:T(8,128)(2,1)S(1)}, u32[]{:S(2)}, u32[]{:S(2)}) collective-permute-start(bf16[2,4,32,384]{3,2,1,0:T(8,128)(2,1)S(1)} %get-tuple-element.36), channel_id=1, source_target_pairs={{0,32},{1,225},{2,34},{3,227},{4,36},{5,229},{6,38},{7,231},{8,40}... | collective-permute-start | bytes 589832 | tf_op jit(solution)/shard_map/ppermute | solution.py:508
  17.7 34.1 %collective-permute-start.2 = (bf16[2,4,32,384]{3,2,1,0:T(8,128)(2,1)S(1)}, bf16[2,4,32,384]{3,2,1,0:T(8,128)(2,1)S(1)}, u32[]{:S(2)}, u32[]{:S(2)}) collective-permute-start(bf16[2,4,32,384]{3,2,1,0:T(8,128)(2,1)S(1)} %get-tuple-element.37), channel_id=1, source_target_pairs={{0,64},{1,193},{2,66},{3,195},{4,68},{5,197},{6,70},{7,199},{8,72}... | collective-permute-start | bytes 589832 | tf_op jit(solution)/shard_map/ppermute | solution.py:508
  20.1 39.0 %collective-permute-start.3 = (bf16[2,4,32,384]{3,2,1,0:T(8,128)(2,1)S(1)}, bf16[2,4,32,384]{3,2,1,0:T(8,128)(2,1)S(1)}, u32[]{:S(2)}, u32[]{:S(2)}) collective-permute-start(bf16[2,4,32,384]{3,2,1,0:T(8,128)(2,1)S(1)} %get-tuple-element.38), channel_id=1, source_target_pairs={{0,96},{1,161},{2,98},{3,163},{4,100},{5,165},{6,102},{7,167},{8,1... | collective-permute-start | bytes 589832 | tf_op jit(solution)/shard_map/ppermute | solution.py:508
  59.1 34.3 %copy-start = (s32[8,22]{1,0:T(8,128)S(1)}, s32[8,22]{1,0:T(8,128)}, u32[]{:S(2)}) copy-start(s32[8,22]{1,0:T(8,128)} %mask_ref.1) | copy-start | bytes 2116
  59.1 9.9 %collective-permute-start.5 = (bf16[3,4,32,384]{3,2,1,0:T(8,128)(2,1)S(1)}, bf16[3,4,32,384]{3,2,1,0:T(8,128)(2,1)S(1)}, u32[]{:S(2)}, u32[]{:S(2)}) collective-permute-start(bf16[3,4,32,384]{3,2,1,0:T(8,128)(2,1)S(1)} %pack.1), channel_id=1, source_target_pairs={{0,1},{1,0},{2,3},{3,2},{4,5},{5,4},{6,7},{7,6},{8,9},{9,8},{10,11... | collective-permute-start | bytes 884744 | tf_op jit(solution)/shard_map/ppermute | solution.py:516
  59.2 9.8 %collective-permute-start.4 = (bf16[4,32,384]{2,1,0:T(8,128)(2,1)S(1)}, bf16[4,32,384]{2,1,0:T(8,128)(2,1)S(1)}, u32[]{:S(2)}, u32[]{:S(2)}) collective-permute-start(bf16[4,32,384]{2,1,0:T(8,128)(2,1)S(1)} %get-tuple-element.39), channel_id=1, source_target_pairs={{0,128},{8,136},{16,144},{24,152},{32,160},{40,168},{48,176},{56,1... | collective-permute-start | bytes 294920 | tf_op jit(solution)/shard_map/ppermute | solution.py:505
  69.1 6.1 %collective-permute-start.6 = (bf16[256,256]{1,0:T(8,128)(2,1)S(1)}, bf16[256,256]{1,0:T(8,128)(2,1)S(1)}, u32[]{:S(2)}, u32[]{:S(2)}) collective-permute-start(bf16[256,256]{1,0:T(8,128)(2,1)S(1)} %get-tuple-element.41), channel_id=1, source_target_pairs={{0,8},{8,16},{16,24},{24,0},{32,40},{40,48},{48,56},{56,32},{64,72... | collective-permute-start | bytes 393224 | tf_op jit(solution)/shard_map/ppermute | solution.py:520
  70.8 7.7 %collective-permute-start.7 = (bf16[256,256]{1,0:T(8,128)(2,1)S(1)}, bf16[256,256]{1,0:T(8,128)(2,1)S(1)}, u32[]{:S(2)}, u32[]{:S(2)}) collective-permute-start(bf16[256,256]{1,0:T(8,128)(2,1)S(1)} %get-tuple-element.42), channel_id=1, source_target_pairs={{0,16},{8,24},{16,0},{24,8},{32,48},{40,56},{48,32},{56,40},{64,80... | collective-permute-start | bytes 393224 | tf_op jit(solution)/shard_map/ppermute | solution.py:520
  73.6 5.8 %collective-permute-start.8 = (bf16[256,256]{1,0:T(8,128)(2,1)S(1)}, bf16[256,256]{1,0:T(8,128)(2,1)S(1)}, u32[]{:S(2)}, u32[]{:S(2)}) collective-permute-start(bf16[256,256]{1,0:T(8,128)(2,1)S(1)} %get-tuple-element.43), channel_id=1, source_target_pairs={{0,24},{8,0},{16,8},{24,16},{32,56},{40,32},{48,40},{56,48},{64,88... | collective-permute-start | bytes 393224 | tf_op jit(solution)/shard_map/ppermute | solution.py:520
  79.7 10.2 %collective-permute-start.12 = (bf16[256,256]{1,0:T(8,128)(2,1)S(1)}, bf16[256,256]{1,0:T(8,128)(2,1)S(1)}, u32[]{:S(2)}, u32[]{:S(2)}) collective-permute-start(bf16[256,256]{1,0:T(8,128)(2,1)S(1)} %halo_hidden.1.refs_9_), channel_id=1, source_target_pairs={{0,2},{1,3},{2,4},{3,5},{4,6},{5,7},{6,0},{7,1},{8,10},{9,11},{10,... | collective-permute-start | bytes 393224 | tf_op jit(solution)/shard_map/ppermute | solution.py:525
  81.3 9.0 %collective-permute-start.13 = (bf16[256,256]{1,0:T(8,128)(2,1)S(1)}, bf16[256,256]{1,0:T(8,128)(2,1)S(1)}, u32[]{:S(2)}, u32[]{:S(2)}) collective-permute-start(bf16[256,256]{1,0:T(8,128)(2,1)S(1)} %halo_hidden.1.refs_9_), channel_id=1, source_target_pairs={{0,4},{1,5},{2,6},{3,7},{4,0},{5,1},{6,2},{7,3},{8,12},{9,13},{10,... | collective-permute-start | bytes 393224 | tf_op jit(solution)/shard_map/ppermute | solution.py:525
  84.2 6.2 %collective-permute-start.14 = (bf16[256,256]{1,0:T(8,128)(2,1)S(1)}, bf16[256,256]{1,0:T(8,128)(2,1)S(1)}, u32[]{:S(2)}, u32[]{:S(2)}) collective-permute-start(bf16[256,256]{1,0:T(8,128)(2,1)S(1)} %halo_hidden.1.refs_9_), channel_id=1, source_target_pairs={{0,6},{1,7},{2,0},{3,1},{4,2},{5,3},{6,4},{7,5},{8,14},{9,15},{10,... | collective-permute-start | bytes 393224 | tf_op jit(solution)/shard_map/ppermute | solution.py:525
  85.6 4.3 %collective-permute-start.9 = (bf16[256,128]{1,0:T(8,128)(2,1)S(1)}, bf16[256,128]{1,0:T(8,128)(2,1)S(1)}, u32[]{:S(2)}, u32[]{:S(2)}) collective-permute-start(bf16[256,128]{1,0:T(8,128)(2,1)S(1)} %get-tuple-element.45), channel_id=1, source_target_pairs={{0,8},{8,16},{16,24},{24,0},{32,40},{40,48},{48,56},{56,32},{64,72... | collective-permute-start | bytes 196616 | tf_op jit(solution)/shard_map/ppermute | solution.py:521
  86.7 5.8 %collective-permute-start.10 = (bf16[256,128]{1,0:T(8,128)(2,1)S(1)}, bf16[256,128]{1,0:T(8,128)(2,1)S(1)}, u32[]{:S(2)}, u32[]{:S(2)}) collective-permute-start(bf16[256,128]{1,0:T(8,128)(2,1)S(1)} %get-tuple-element.46), channel_id=1, source_target_pairs={{0,16},{8,24},{16,0},{24,8},{32,48},{40,56},{48,32},{56,40},{64,80... | collective-permute-start | bytes 196616 | tf_op jit(solution)/shard_map/ppermute | solution.py:521
  89.8 10.9 %collective-permute-start.15 = (bf16[256,256]{1,0:T(8,128)(2,1)S(1)}, bf16[256,256]{1,0:T(8,128)(2,1)S(1)}, u32[]{:S(2)}, u32[]{:S(2)}) collective-permute-start(bf16[256,256]{1,0:T(8,128)(2,1)S(1)} %halo_hidden.1.refs_9_), channel_id=1, source_target_pairs={{0,1},{1,0},{2,3},{3,2},{4,5},{5,4},{6,7},{7,6},{8,9},{9,8},{10,11... | collective-permute-start | bytes 393224 | tf_op jit(solution)/shard_map/ppermute | solution.py:526
  89.9 10.9 %collective-permute-start.16 = (bf16[256,256]{1,0:T(8,128)(2,1)S(1)}, bf16[256,256]{1,0:T(8,128)(2,1)S(1)}, u32[]{:S(2)}, u32[]{:S(2)}) collective-permute-start(bf16[256,256]{1,0:T(8,128)(2,1)S(1)} %collective-permute-done.12.rest_0_), channel_id=1, source_target_pairs={{0,1},{1,0},{2,3},{3,2},{4,5},{5,4},{6,7},{7,6},{8,9},{9,8},{10,11... | collective-permute-start | bytes 393224 | tf_op jit(solution)/shard_map/ppermute | solution.py:526
  90.4 10.4 %collective-permute-start.17 = (bf16[256,256]{1,0:T(8,128)(2,1)S(1)}, bf16[256,256]{1,0:T(8,128)(2,1)S(1)}, u32[]{:S(2)}, u32[]{:S(2)}) collective-permute-start(bf16[256,256]{1,0:T(8,128)(2,1)S(1)} %collective-permute-done.13.rest_1_), channel_id=1, source_target_pairs={{0,1},{1,0},{2,3},{3,2},{4,5},{5,4},{6,7},{7,6},{8,9},{9,8},{10,11... | collective-permute-start | bytes 393224 | tf_op jit(solution)/shard_map/ppermute | solution.py:526
  90.5 10.3 %collective-permute-start.18 = (bf16[256,256]{1,0:T(8,128)(2,1)S(1)}, bf16[256,256]{1,0:T(8,128)(2,1)S(1)}, u32[]{:S(2)}, u32[]{:S(2)}) collective-permute-start(bf16[256,256]{1,0:T(8,128)(2,1)S(1)} %collective-permute-done.14.rest_2_), channel_id=1, source_target_pairs={{0,1},{1,0},{2,3},{3,2},{4,5},{5,4},{6,7},{7,6},{8,9},{9,8},{10,11... | collective-permute-start | bytes 393224 | tf_op jit(solution)/shard_map/ppermute | solution.py:526
  92.5 5.7 %collective-permute-start.11 = (bf16[256,128]{1,0:T(8,128)(2,1)S(1)}, bf16[256,128]{1,0:T(8,128)(2,1)S(1)}, u32[]{:S(2)}, u32[]{:S(2)}) collective-permute-start(bf16[256,128]{1,0:T(8,128)(2,1)S(1)} %get-tuple-element.47), channel_id=1, source_target_pairs={{0,24},{8,0},{16,8},{24,16},{32,56},{40,32},{48,40},{56,48},{64,88... | collective-permute-start | bytes 196616 | tf_op jit(solution)/shard_map/ppermute | solution.py:521
  100.8 1.3 %copy-start.1 = (f32[256]{0:T(256)S(1)}, f32[256]{0:T(256)}, u32[]{:S(2)}) copy-start(f32[256]{0:T(256)} %param.13) | copy-start | bytes 3076

commit v7 on v5

--- a/solution.py
+++ b/solution.py
@@ -82,8 +82,8 @@
     outs = []
     for i, f0 in enumerate(chunks):
         late[i].wait()
-        for n0 in range(early, n, 2 * TILE):
-            at = slice(n0, min(n0 + 2 * TILE, n))
+        for n0 in range(early, n, n - early):
+            at = slice(n0, n)
             to = slice(at.start - early, at.stop - early)
             tail_ref[:, f0 : f0 + 16, to] = swapped(plain, x_ref, f0, at)
         at = (slice(None), pl.ds(f0, 16), slice(None))
@@ -91,8 +91,8 @@
         outs[-1].start()
     for i, f0 in enumerate(chunks):
         soon[i].wait()
-        for n0 in range(0, early, 2 * TILE):
-            at = slice(n0, min(n0 + 2 * TILE, early))
+        for n0 in range(0, early, early):
+            at = slice(n0, early)
             block = swapped(turned, x_ref, f0, at)
             for dz in range(NZ):
                 heads[dz][:, f0 : f0 + 16, at] = block[dz * NX : (dz + 1) * NX]

time: 102 us -> 102 us (level)
  no operation moved by 1% of the time
where the time goes in v7:
time: 102 us; the launch traced here: 100 us
  starting transfers between devices  42.1 us (41%)
  waiting for transfers between devices  40.8 us (40%)
  Pallas kernels  17 us (17%)
    ppermute x7, waiting for transfers between devices, shards(): landed.append(lax.ppermute(head[dz], 'feat', feat_shift(dz, 0)))  33.9 us
    ppermute x7, starting transfers between devices, shards(): landed.append(lax.ppermute(head[dz], 'feat', feat_shift(dz, 0)))  15.2 us
    all_to_all x1, starting transfers between devices, shards(): rest = lax.all_to_all(rest, 'feat', split_axis=0, concat_axis=0, tiled=True)  11.6 us
    ppermute x3, starting transfers between devices, shards(): same.append(lax.ppermute(h_head, 'blk', blk_shift(dy, 0)))  5.9 us
    ppermute x3, starting transfers between devices, shards(): parts.append(lax.ppermute(rows[j], 'feat', feat_shift(0, j)))  4.8 us
    pallas_call x1, Pallas kernels, mask_tiles(): pl.pallas_call(mask_kernel, grid_spec=pltpu.PrefetchScalarGridSpec(num_sc...  4.76 us
    pallas_call x1, Pallas kernels, last_step(): pl.pallas_call(last_kernel, grid=(1,), in_specs=[full(x.shape), full(turn...  3.98 us
    ppermute x3, waiting for transfers between devices, shards(): parts.append(lax.ppermute(rows[j], 'feat', feat_shift(0, j)))  3.59 us
  transfers between devices with their start and end apart: 21, of which 8 were waited for; matrix products, arithmetic and copies ran while one was open for 0% of the time, Pallas kernels for 10%

profile of v7, /device:TPU:2, one launch (start us, length us, event | category | flops | bytes accessed | tf_op | source)
XLA Modules:
  0.0 100.3 jit_solution(8284637112413334713)
XLA Ops:
  0.0 2.8 %split.1 = (bf16[4,32,384]{2,1,0:T(8,128)(2,1)S(1)}, bf16[4,32,384]{2,1,0:T(8,128)(2,1)S(1)}, bf16[4,32,384]{2,1,0:T(8,128)(2,1)S(1)}, bf16[4,32,384]{2,1,0:T(8,...) custom-call(s32[1]{0:T(128)} %bitcast.me_ref, ...), custom_call_target="tpu_custom_call" | custom-call | tf_op jit(solution)/shard_map/split/pallas_call | solution.py:106
  2.8 11.6 %all-to-all-start = ((bf16[32,32,640]{2,1,0:T(8,128)(2,1)}), bf16[32,32,640]{2,1,0:T(8,128)(2,1)S(1)}, u32[]{:S(2)}, u32[]{:S(2)}) async-start(bf16[32,32,640]{2,1,0:T(8,128)(2,1)} %get-tuple-element.32), calls=%async_computation | async-start | bytes 2621440 | tf_op jit(solution)/shard_map/all_to_all | solution.py:448
  14.4 0.0 copy-start
  14.4 1.5 %collective-permute-start = (bf16[4,32,384]{2,1,0:T(8,128)(2,1)S(1)}, bf16[4,32,384]{2,1,0:T(8,128)(2,1)S(1)}, u32[]{:S(2)}, u32[]{:S(2)}) collective-permute-start(bf16[4,32,384]{2,1,0:T(8,128)(2,1)S(1)} %get-tuple-element.35), channel_id=1, source_target_pairs={{0,32},{8,40},{16,48},{24,56},{32,64},{40,72},{48,80},{56,88},{64,... | collective-permute-start | bytes 294920 | tf_op jit(solution)/shard_map/ppermute | solution.py:447
  16.0 2.4 %collective-permute-start.1 = (bf16[4,32,384]{2,1,0:T(8,128)(2,1)S(1)}, bf16[4,32,384]{2,1,0:T(8,128)(2,1)S(1)}, u32[]{:S(2)}, u32[]{:S(2)}) collective-permute-start(bf16[4,32,384]{2,1,0:T(8,128)(2,1)S(1)} %get-tuple-element.36), channel_id=1, source_target_pairs={{0,64},{8,72},{16,80},{24,88},{32,96},{40,104},{48,112},{56,120},{... | collective-permute-start | bytes 294920 | tf_op jit(solution)/shard_map/ppermute | solution.py:447
  18.3 2.7 %collective-permute-start.2 = (bf16[4,32,384]{2,1,0:T(8,128)(2,1)S(1)}, bf16[4,32,384]{2,1,0:T(8,128)(2,1)S(1)}, u32[]{:S(2)}, u32[]{:S(2)}) collective-permute-start(bf16[4,32,384]{2,1,0:T(8,128)(2,1)S(1)} %get-tuple-element.37), channel_id=1, source_target_pairs={{0,96},{8,104},{16,112},{24,120},{32,128},{40,136},{48,144},{56,15... | collective-permute-start | bytes 294920 | tf_op jit(solution)/shard_map/ppermute | solution.py:447
  21.0 2.3 %collective-permute-start.3 = (bf16[4,32,384]{2,1,0:T(8,128)(2,1)S(1)}, bf16[4,32,384]{2,1,0:T(8,128)(2,1)S(1)}, u32[]{:S(2)}, u32[]{:S(2)}) collective-permute-start(bf16[4,32,384]{2,1,0:T(8,128)(2,1)S(1)} %get-tuple-element.38), channel_id=1, source_target_pairs={{0,128},{8,136},{16,144},{24,152},{32,160},{40,168},{48,176},{56,1... | collective-permute-start | bytes 294920 | tf_op jit(solution)/shard_map/ppermute | solution.py:447
  23.4 2.7 %collective-permute-start.4 = (bf16[4,32,384]{2,1,0:T(8,128)(2,1)S(1)}, bf16[4,32,384]{2,1,0:T(8,128)(2,1)S(1)}, u32[]{:S(2)}, u32[]{:S(2)}) collective-permute-start(bf16[4,32,384]{2,1,0:T(8,128)(2,1)S(1)} %get-tuple-element.39), channel_id=1, source_target_pairs={{0,160},{8,168},{16,176},{24,184},{32,192},{40,200},{48,208},{56,2... | collective-permute-start | bytes 294920 | tf_op jit(solution)/shard_map/ppermute | solution.py:447
  26.1 23.1 %collective-permute-done.refs_1_ = bf16[4,32,384]{2,1,0:T(8,128)(2,1)S(1)} collective-permute-done((bf16[4,32,384]{2,1,0:T(8,128)(2,1)S(1)}, bf16[4,32,384]{2,1,0:T(8,128)(2,1)S(1)}, u32[]{:S(2)}, u32[]{:S(2)}) %collective-permute-start) | collective-permute-done | bytes 98336 | tf_op jit(solution)/shard_map/ppermute | solution.py:447
  49.2 2.1 %collective-permute-start.5 = (bf16[4,32,384]{2,1,0:T(8,128)(2,1)S(1)}, bf16[4,32,384]{2,1,0:T(8,128)(2,1)S(1)}, u32[]{:S(2)}, u32[]{:S(2)}) collective-permute-start(bf16[4,32,384]{2,1,0:T(8,128)(2,1)S(1)} %get-tuple-element.40), channel_id=1, source_target_pairs={{0,192},{8,200},{16,208},{24,216},{32,224},{40,232},{48,240},{56,2... | collective-permute-start | bytes 294920 | tf_op jit(solution)/shard_map/ppermute | solution.py:447
  51.3 3.3 %collective-permute-done.1.refs_2_ = bf16[4,32,384]{2,1,0:T(8,128)(2,1)S(1)} collective-permute-done((bf16[4,32,384]{2,1,0:T(8,128)(2,1)S(1)}, bf16[4,32,384]{2,1,0:T(8,128)(2,1)S(1)}, u32[]{:S(2)}, u32[]{:S(2)}) %collective-permute-start.1) | collective-permute-done | bytes 98336 | tf_op jit(solution)/shard_map/ppermute | solution.py:447
  54.6 1.4 %collective-permute-start.6 = (bf16[4,32,384]{2,1,0:T(8,128)(2,1)S(1)}, bf16[4,32,384]{2,1,0:T(8,128)(2,1)S(1)}, u32[]{:S(2)}, u32[]{:S(2)}) collective-permute-start(bf16[4,32,384]{2,1,0:T(8,128)(2,1)S(1)} %get-tuple-element.41), channel_id=1, source_target_pairs={{0,224},{8,232},{16,240},{24,248},{32,0},{40,8},{48,16},{56,24},{6... | collective-permute-start | bytes 294920 | tf_op jit(solution)/shard_map/ppermute | solution.py:447
  56.0 3.7 %collective-permute-done.2.refs_3_ = bf16[4,32,384]{2,1,0:T(8,128)(2,1)S(1)} collective-permute-done((bf16[4,32,384]{2,1,0:T(8,128)(2,1)S(1)}, bf16[4,32,384]{2,1,0:T(8,128)(2,1)S(1)}, u32[]{:S(2)}, u32[]{:S(2)}) %collective-permute-start.2) | collective-permute-done | bytes 98336 | tf_op jit(solution)/shard_map/ppermute | solution.py:447
  59.7 3.8 %collective-permute-done.3.refs_4_ = bf16[4,32,384]{2,1,0:T(8,128)(2,1)S(1)} collective-permute-done((bf16[4,32,384]{2,1,0:T(8,128)(2,1)S(1)}, bf16[4,32,384]{2,1,0:T(8,128)(2,1)S(1)}, u32[]{:S(2)}, u32[]{:S(2)}) %collective-permute-start.3) | collective-permute-done | bytes 98336 | tf_op jit(solution)/shard_map/ppermute | solution.py:447
  63.5 0.0 collective-permute-done.4.refs_5_
  63.6 0.0 collective-permute-done.5.refs_6_
  63.6 0.1 regroup.1
  63.6 1.5 %collective-permute-start.7 = (bf16[256,256]{1,0:T(8,128)(2,1)S(1)}, bf16[256,256]{1,0:T(8,128)(2,1)S(1)}, u32[]{:S(2)}, u32[]{:S(2)}) collective-permute-start(bf16[256,256]{1,0:T(8,128)(2,1)S(1)} %get-tuple-element.43), channel_id=1, source_target_pairs={{0,8},{8,16},{16,24},{24,0},{32,40},{40,48},{48,56},{56,32},{64,72... | collective-permute-start | bytes 393224 | tf_op jit(solution)/shard_map/ppermute | solution.py:458
  65.2 1.1 %collective-permute-start.8 = (bf16[256,256]{1,0:T(8,128)(2,1)S(1)}, bf16[256,256]{1,0:T(8,128)(2,1)S(1)}, u32[]{:S(2)}, u32[]{:S(2)}) collective-permute-start(bf16[256,256]{1,0:T(8,128)(2,1)S(1)} %get-tuple-element.44), channel_id=1, source_target_pairs={{0,16},{8,24},{16,0},{24,8},{32,48},{40,56},{48,32},{56,40},{64,80... | collective-permute-start | bytes 393224 | tf_op jit(solution)/shard_map/ppermute | solution.py:458
  66.3 2.1 %collective-permute-start.9 = (bf16[256,256]{1,0:T(8,128)(2,1)S(1)}, bf16[256,256]{1,0:T(8,128)(2,1)S(1)}, u32[]{:S(2)}, u32[]{:S(2)}) collective-permute-start(bf16[256,256]{1,0:T(8,128)(2,1)S(1)} %get-tuple-element.45), channel_id=1, source_target_pairs={{0,24},{8,0},{16,8},{24,16},{32,56},{40,32},{48,40},{56,48},{64,88... | collective-permute-start | bytes 393224 | tf_op jit(solution)/shard_map/ppermute | solution.py:458
  68.4 1.3 %weights.1 = (bf16[1024,512]{1,0:T(8,128)(2,1)S(1)}, bf16[1024,512]{1,0:T(8,128)(2,1)S(1)}) custom-call(s32[1]{0:T(128)} %bitcast.me_ref, bf16[1024,256]{1,0:T(8,128)(2,1)} %ws_hbm.1, bf16[1024,256]{1,0:T(8,128)(2,1)} %wn_hbm.1), custom_call_target="tpu_custom_call" | custom-call | tf_op jit(solution)/shard_map/weights/pallas_call | solution.py:174
  69.8 3.0 %collective-permute-done.8.c.refs_2_ = bf16[256,256]{1,0:T(8,128)(2,1)S(1)} collective-permute-done((bf16[256,256]{1,0:T(8,128)(2,1)S(1)}, bf16[256,256]{1,0:T(8,128)(2,1)S(1)}, u32[]{:S(2)}, u32[]{:S(2)}) %collective-permute-start.8) | collective-permute-done | bytes 131104 | tf_op jit(solution)/shard_map/ppermute | solution.py:458
  72.7 0.6 collective-permute-done.9.d.refs_3_
  73.3 0.3 halo_hidden.1.refs_9_
  73.7 1.7 %collective-permute-start.13 = (bf16[256,256]{1,0:T(8,128)(2,1)S(1)}, bf16[256,256]{1,0:T(8,128)(2,1)S(1)}, u32[]{:S(2)}, u32[]{:S(2)}) collective-permute-start(bf16[256,256]{1,0:T(8,128)(2,1)S(1)} %halo_hidden.1.refs_9_), channel_id=1, source_target_pairs={{0,2},{1,3},{2,4},{3,5},{4,6},{5,7},{6,0},{7,1},{8,10},{9,11},{10,... | collective-permute-start | bytes 393224 | tf_op jit(solution)/shard_map/ppermute | solution.py:463
  75.4 2.9 %collective-permute-start.14 = (bf16[256,256]{1,0:T(8,128)(2,1)S(1)}, bf16[256,256]{1,0:T(8,128)(2,1)S(1)}, u32[]{:S(2)}, u32[]{:S(2)}) collective-permute-start(bf16[256,256]{1,0:T(8,128)(2,1)S(1)} %halo_hidden.1.refs_9_), channel_id=1, source_target_pairs={{0,4},{1,5},{2,6},{3,7},{4,0},{5,1},{6,2},{7,3},{8,12},{9,13},{10,... | collective-permute-start | bytes 393224 | tf_op jit(solution)/shard_map/ppermute | solution.py:463
  78.2 1.3 %collective-permute-start.15 = (bf16[256,256]{1,0:T(8,128)(2,1)S(1)}, bf16[256,256]{1,0:T(8,128)(2,1)S(1)}, u32[]{:S(2)}, u32[]{:S(2)}) collective-permute-start(bf16[256,256]{1,0:T(8,128)(2,1)S(1)} %halo_hidden.1.refs_9_), channel_id=1, source_target_pairs={{0,6},{1,7},{2,0},{3,1},{4,2},{5,3},{6,4},{7,5},{8,14},{9,15},{10,... | collective-permute-start | bytes 393224 | tf_op jit(solution)/shard_map/ppermute | solution.py:463
  79.6 1.4 %collective-permute-start.10 = (bf16[256,128]{1,0:T(8,128)(2,1)S(1)}, bf16[256,128]{1,0:T(8,128)(2,1)S(1)}, u32[]{:S(2)}, u32[]{:S(2)}) collective-permute-start(bf16[256,128]{1,0:T(8,128)(2,1)S(1)} %get-tuple-element.47), channel_id=1, source_target_pairs={{0,8},{8,16},{16,24},{24,0},{32,40},{40,48},{48,56},{56,32},{64,72... | collective-permute-start | bytes 196616 | tf_op jit(solution)/shard_map/ppermute | solution.py:459
  81.0 1.5 %collective-permute-start.11 = (bf16[256,128]{1,0:T(8,128)(2,1)S(1)}, bf16[256,128]{1,0:T(8,128)(2,1)S(1)}, u32[]{:S(2)}, u32[]{:S(2)}) collective-permute-start(bf16[256,128]{1,0:T(8,128)(2,1)S(1)} %get-tuple-element.48), channel_id=1, source_target_pairs={{0,16},{8,24},{16,0},{24,8},{32,48},{40,56},{48,32},{56,40},{64,80... | collective-permute-start | bytes 196616 | tf_op jit(solution)/shard_map/ppermute | solution.py:459
  82.5 2.0 %collective-permute-done.10.refs_5_ = bf16[256,128]{1,0:T(8,128)(2,1)S(1)} collective-permute-done((bf16[256,128]{1,0:T(8,128)(2,1)S(1)}, bf16[256,128]{1,0:T(8,128)(2,1)S(1)}, u32[]{:S(2)}, u32[]{:S(2)}) %collective-permute-start.10) | collective-permute-done | bytes 65568 | tf_op jit(solution)/shard_map/ppermute | solution.py:459
  84.4 0.0 collective-permute-start.16
  84.4 0.0 collective-permute-done.13.rest_0_
  84.4 0.5 collective-permute-start.17
  85.0 0.1 collective-permute-start.18
  85.1 0.0 collective-permute-done.15.rest_2_
  85.1 0.4 collective-permute-start.19
  85.5 1.3 %collective-permute-done.11.refs_6_ = bf16[256,128]{1,0:T(8,128)(2,1)S(1)} collective-permute-done((bf16[256,128]{1,0:T(8,128)(2,1)S(1)}, bf16[256,128]{1,0:T(8,128)(2,1)S(1)}, u32[]{:S(2)}, u32[]{:S(2)}) %collective-permute-start.11) | collective-permute-done | bytes 65568 | tf_op jit(solution)/shard_map/ppermute | solution.py:459
  86.7 0.7 collective-permute-start.12
  87.4 4.8 %mask_tiles.1 = (bf16[1024,256]{1,0:T(8,128)(2,1)S(1)}, bf16[1024,128]{1,0:T(8,128)(2,1)S(1)}, bf16[1024,640]{1,0:T(8,128)(2,1)}, bf16[1024,768]{1,0:T(8,128)(2,...) custom-call(s32[1]{0:T(128)} %bitcast.me_ref, s32[8,22]{1,0:T(8,128)S(1)} %copy-done, ...), custom_call_target="tpu_custom_call" | custom-call | tf_op jit(solution)/shard_map/mask_tiles/pallas_call | solution.py:318
  92.2 0.0 collective-permute-done.12.refs_7_
  92.2 1.5 %mid_hidden.1 = (f32[384,256]{1,0:T(8,128)}, f32[1024,256]{1,0:T(8,128)S(1)}) custom-call(bf16[256,256]{1,0:T(8,128)(2,1)S(1)} %get-tuple-element.42.a.refs_0_, bf16[256,256]{1,0:T(8,128)(2,1)S(1)} %collective-permute-done.7.b.refs_1_, bf16[256,256]{1,0:T(8,128)(2,1)S(1)} %collective-permute-done.8.c.refs_2_, ...), custom_call_target="tpu_custom_call" | custom-call | tf_op jit(solution)/shard_map/mid_hidden/pallas_call | solution.py:248
  93.7 1.1 %shard_map.73.acc_ref = f32[1024,256]{1,0:T(8,128)S(1)} custom-call(f32[1024,256]{1,0:T(8,128)S(1)} %get-tuple-element.53.acc_ref, bf16[1024,768]{1,0:T(8,128)(2,1)S(1)} %get-tuple-element.54.live_ref, bf16[256,256]{1,0:T(8,128)(2,1)S(1)} %collective-permute-done.13.rest_0_, bf16[256,256]{1,0:T(8,128)(2,1)S(1)} %collective-permute-done.14.rest_1_, ...), custom_call_target="tpu_custom_call" | custom-call | tf_op jit(solution)/shard_map/pallas_call | solution.py:368
  94.8 0.0 collective-permute-done.16.rest_0_
  94.8 0.0 collective-permute-done.17.rest_1_
  94.8 0.0 collective-permute-done.19.rest_3_
  94.8 0.0 copy-start.1
  94.8 1.3 %shard_map.74.acc_ref = f32[1024,256]{1,0:T(8,128)S(1)} custom-call(f32[1024,256]{1,0:T(8,128)S(1)} %shard_map.73.acc_ref, bf16[1024,1024]{1,0:T(8,128)(2,1)S(1)} %get-tuple-element.55.live_ref, bf16[256,256]{1,0:T(8,128)(2,1)S(1)} %collective-permute-done.16.rest_0_, bf16[256,256]{1,0:T(8,128)(2,1)S(1)} %collective-permute-done.17.rest_1_, ...), custom_call_target="tpu_custom_call" | custom-call | tf_op jit(solution)/shard_map/pallas_call | solution.py:368
  96.1 4.0 %last_step.1 = bf16[1024,256]{1,0:T(8,128)(2,1)} custom-call(bf16[1024,640]{1,0:T(8,128)(2,1)S(1)} %bitcast.3, bf16[1024,512]{1,0:T(8,128)(2,1)S(1)} %get-tuple-element.33.w_ref, f32[1024,256]{1,0:T(8,128)S(1)} %shard_map.74.acc_ref, bf16[1024,640]{1,0:T(8,128)(2,1)} %get-tuple-element.56.tail_hbm, f32[1024,128]{1,0:T(8,128)} %get-tuple-element.57.scale_hbm, ...), custom_call_target="tpu_custom_call" | custom-call | tf_op jit(solution)/shard_map/last_step/pallas_call | solution.py:420
  (7 shorter events, 0.0 us)
Async XLA Ops:
  2.8 93.3 %all-to-all-start = ((bf16[32,32,640]{2,1,0:T(8,128)(2,1)}), bf16[32,32,640]{2,1,0:T(8,128)(2,1)S(1)}, u32[]{:S(2)}, u32[]{:S(2)}) async-start(bf16[32,32,640]{2,1,0:T(8,128)(2,1)} %get-tuple-element.32), calls=%async_computation | async-start | bytes 2621440 | tf_op jit(solution)/shard_map/all_to_all | solution.py:448
  14.4 73.0 %copy-start = (s32[8,22]{1,0:T(8,128)S(1)}, s32[8,22]{1,0:T(8,128)}, u32[]{:S(2)}) copy-start(s32[8,22]{1,0:T(8,128)} %mask_ref.1) | copy-start | bytes 2116
  14.4 34.8 %collective-permute-start = (bf16[4,32,384]{2,1,0:T(8,128)(2,1)S(1)}, bf16[4,32,384]{2,1,0:T(8,128)(2,1)S(1)}, u32[]{:S(2)}, u32[]{:S(2)}) collective-permute-start(bf16[4,32,384]{2,1,0:T(8,128)(2,1)S(1)} %get-tuple-element.35), channel_id=1, source_target_pairs={{0,32},{8,40},{16,48},{24,56},{32,64},{40,72},{48,80},{56,88},{64,... | collective-permute-start | bytes 294920 | tf_op jit(solution)/shard_map/ppermute | solution.py:447
  16.0 38.7 %collective-permute-start.1 = (bf16[4,32,384]{2,1,0:T(8,128)(2,1)S(1)}, bf16[4,32,384]{2,1,0:T(8,128)(2,1)S(1)}, u32[]{:S(2)}, u32[]{:S(2)}) collective-permute-start(bf16[4,32,384]{2,1,0:T(8,128)(2,1)S(1)} %get-tuple-element.36), channel_id=1, source_target_pairs={{0,64},{8,72},{16,80},{24,88},{32,96},{40,104},{48,112},{56,120},{... | collective-permute-start | bytes 294920 | tf_op jit(solution)/shard_map/ppermute | solution.py:447
  18.3 41.4 %collective-permute-start.2 = (bf16[4,32,384]{2,1,0:T(8,128)(2,1)S(1)}, bf16[4,32,384]{2,1,0:T(8,128)(2,1)S(1)}, u32[]{:S(2)}, u32[]{:S(2)}) collective-permute-start(bf16[4,32,384]{2,1,0:T(8,128)(2,1)S(1)} %get-tuple-element.37), channel_id=1, source_target_pairs={{0,96},{8,104},{16,112},{24,120},{32,128},{40,136},{48,144},{56,15... | collective-permute-start | bytes 294920 | tf_op jit(solution)/shard_map/ppermute | solution.py:447
  21.0 42.5 %collective-permute-start.3 = (bf16[4,32,384]{2,1,0:T(8,128)(2,1)S(1)}, bf16[4,32,384]{2,1,0:T(8,128)(2,1)S(1)}, u32[]{:S(2)}, u32[]{:S(2)}) collective-permute-start(bf16[4,32,384]{2,1,0:T(8,128)(2,1)S(1)} %get-tuple-element.38), channel_id=1, source_target_pairs={{0,128},{8,136},{16,144},{24,152},{32,160},{40,168},{48,176},{56,1... | collective-permute-start | bytes 294920 | tf_op jit(solution)/shard_map/ppermute | solution.py:447
  23.4 40.2 %collective-permute-start.4 = (bf16[4,32,384]{2,1,0:T(8,128)(2,1)S(1)}, bf16[4,32,384]{2,1,0:T(8,128)(2,1)S(1)}, u32[]{:S(2)}, u32[]{:S(2)}) collective-permute-start(bf16[4,32,384]{2,1,0:T(8,128)(2,1)S(1)} %get-tuple-element.39), channel_id=1, source_target_pairs={{0,160},{8,168},{16,176},{24,184},{32,192},{40,200},{48,208},{56,2... | collective-permute-start | bytes 294920 | tf_op jit(solution)/shard_map/ppermute | solution.py:447
  49.2 14.4 %collective-permute-start.5 = (bf16[4,32,384]{2,1,0:T(8,128)(2,1)S(1)}, bf16[4,32,384]{2,1,0:T(8,128)(2,1)S(1)}, u32[]{:S(2)}, u32[]{:S(2)}) collective-permute-start(bf16[4,32,384]{2,1,0:T(8,128)(2,1)S(1)} %get-tuple-element.40), channel_id=1, source_target_pairs={{0,192},{8,200},{16,208},{24,216},{32,224},{40,232},{48,240},{56,2... | collective-permute-start | bytes 294920 | tf_op jit(solution)/shard_map/ppermute | solution.py:447
  54.6 8.9 %collective-permute-start.6 = (bf16[4,32,384]{2,1,0:T(8,128)(2,1)S(1)}, bf16[4,32,384]{2,1,0:T(8,128)(2,1)S(1)}, u32[]{:S(2)}, u32[]{:S(2)}) collective-permute-start(bf16[4,32,384]{2,1,0:T(8,128)(2,1)S(1)} %get-tuple-element.41), channel_id=1, source_target_pairs={{0,224},{8,232},{16,240},{24,248},{32,0},{40,8},{48,16},{56,24},{6... | collective-permute-start | bytes 294920 | tf_op jit(solution)/shard_map/ppermute | solution.py:447
  63.6 6.1 %collective-permute-start.7 = (bf16[256,256]{1,0:T(8,128)(2,1)S(1)}, bf16[256,256]{1,0:T(8,128)(2,1)S(1)}, u32[]{:S(2)}, u32[]{:S(2)}) collective-permute-start(bf16[256,256]{1,0:T(8,128)(2,1)S(1)} %get-tuple-element.43), channel_id=1, source_target_pairs={{0,8},{8,16},{16,24},{24,0},{32,40},{40,48},{48,56},{56,32},{64,72... | collective-permute-start | bytes 393224 | tf_op jit(solution)/shard_map/ppermute | solution.py:458
  65.2 7.6 %collective-permute-start.8 = (bf16[256,256]{1,0:T(8,128)(2,1)S(1)}, bf16[256,256]{1,0:T(8,128)(2,1)S(1)}, u32[]{:S(2)}, u32[]{:S(2)}) collective-permute-start(bf16[256,256]{1,0:T(8,128)(2,1)S(1)} %get-tuple-element.44), channel_id=1, source_target_pairs={{0,16},{8,24},{16,0},{24,8},{32,48},{40,56},{48,32},{56,40},{64,80... | collective-permute-start | bytes 393224 | tf_op jit(solution)/shard_map/ppermute | solution.py:458
  66.3 7.0 %collective-permute-start.9 = (bf16[256,256]{1,0:T(8,128)(2,1)S(1)}, bf16[256,256]{1,0:T(8,128)(2,1)S(1)}, u32[]{:S(2)}, u32[]{:S(2)}) collective-permute-start(bf16[256,256]{1,0:T(8,128)(2,1)S(1)} %get-tuple-element.45), channel_id=1, source_target_pairs={{0,24},{8,0},{16,8},{24,16},{32,56},{40,32},{48,40},{56,48},{64,88... | collective-permute-start | bytes 393224 | tf_op jit(solution)/shard_map/ppermute | solution.py:458
  73.7 10.8 %collective-permute-start.13 = (bf16[256,256]{1,0:T(8,128)(2,1)S(1)}, bf16[256,256]{1,0:T(8,128)(2,1)S(1)}, u32[]{:S(2)}, u32[]{:S(2)}) collective-permute-start(bf16[256,256]{1,0:T(8,128)(2,1)S(1)} %halo_hidden.1.refs_9_), channel_id=1, source_target_pairs={{0,2},{1,3},{2,4},{3,5},{4,6},{5,7},{6,0},{7,1},{8,10},{9,11},{10,... | collective-permute-start | bytes 393224 | tf_op jit(solution)/shard_map/ppermute | solution.py:463
  75.4 9.6 %collective-permute-start.14 = (bf16[256,256]{1,0:T(8,128)(2,1)S(1)}, bf16[256,256]{1,0:T(8,128)(2,1)S(1)}, u32[]{:S(2)}, u32[]{:S(2)}) collective-permute-start(bf16[256,256]{1,0:T(8,128)(2,1)S(1)} %halo_hidden.1.refs_9_), channel_id=1, source_target_pairs={{0,4},{1,5},{2,6},{3,7},{4,0},{5,1},{6,2},{7,3},{8,12},{9,13},{10,... | collective-permute-start | bytes 393224 | tf_op jit(solution)/shard_map/ppermute | solution.py:463
  78.2 6.8 %collective-permute-start.15 = (bf16[256,256]{1,0:T(8,128)(2,1)S(1)}, bf16[256,256]{1,0:T(8,128)(2,1)S(1)}, u32[]{:S(2)}, u32[]{:S(2)}) collective-permute-start(bf16[256,256]{1,0:T(8,128)(2,1)S(1)} %halo_hidden.1.refs_9_), channel_id=1, source_target_pairs={{0,6},{1,7},{2,0},{3,1},{4,2},{5,3},{6,4},{7,5},{8,14},{9,15},{10,... | collective-permute-start | bytes 393224 | tf_op jit(solution)/shard_map/ppermute | solution.py:463
  79.6 4.8 %collective-permute-start.10 = (bf16[256,128]{1,0:T(8,128)(2,1)S(1)}, bf16[256,128]{1,0:T(8,128)(2,1)S(1)}, u32[]{:S(2)}, u32[]{:S(2)}) collective-permute-start(bf16[256,128]{1,0:T(8,128)(2,1)S(1)} %get-tuple-element.47), channel_id=1, source_target_pairs={{0,8},{8,16},{16,24},{24,0},{32,40},{40,48},{48,56},{56,32},{64,72... | collective-permute-start | bytes 196616 | tf_op jit(solution)/shard_map/ppermute | solution.py:459
  81.0 5.8 %collective-permute-start.11 = (bf16[256,128]{1,0:T(8,128)(2,1)S(1)}, bf16[256,128]{1,0:T(8,128)(2,1)S(1)}, u32[]{:S(2)}, u32[]{:S(2)}) collective-permute-start(bf16[256,128]{1,0:T(8,128)(2,1)S(1)} %get-tuple-element.48), channel_id=1, source_target_pairs={{0,16},{8,24},{16,0},{24,8},{32,48},{40,56},{48,32},{56,40},{64,80... | collective-permute-start | bytes 196616 | tf_op jit(solution)/shard_map/ppermute | solution.py:459
  84.4 10.3 %collective-permute-start.16 = (bf16[256,256]{1,0:T(8,128)(2,1)S(1)}, bf16[256,256]{1,0:T(8,128)(2,1)S(1)}, u32[]{:S(2)}, u32[]{:S(2)}) collective-permute-start(bf16[256,256]{1,0:T(8,128)(2,1)S(1)} %halo_hidden.1.refs_9_), channel_id=1, source_target_pairs={{0,1},{1,0},{2,3},{3,2},{4,5},{5,4},{6,7},{7,6},{8,9},{9,8},{10,11... | collective-permute-start | bytes 393224 | tf_op jit(solution)/shard_map/ppermute | solution.py:464
  84.4 10.3 %collective-permute-start.17 = (bf16[256,256]{1,0:T(8,128)(2,1)S(1)}, bf16[256,256]{1,0:T(8,128)(2,1)S(1)}, u32[]{:S(2)}, u32[]{:S(2)}) collective-permute-start(bf16[256,256]{1,0:T(8,128)(2,1)S(1)} %collective-permute-done.13.rest_0_), channel_id=1, source_target_pairs={{0,1},{1,0},{2,3},{3,2},{4,5},{5,4},{6,7},{7,6},{8,9},{9,8},{10,11... | collective-permute-start | bytes 393224 | tf_op jit(solution)/shard_map/ppermute | solution.py:464
  85.0 9.8 %collective-permute-start.18 = (bf16[256,256]{1,0:T(8,128)(2,1)S(1)}, bf16[256,256]{1,0:T(8,128)(2,1)S(1)}, u32[]{:S(2)}, u32[]{:S(2)}) collective-permute-start(bf16[256,256]{1,0:T(8,128)(2,1)S(1)} %collective-permute-done.14.rest_1_), channel_id=1, source_target_pairs={{0,1},{1,0},{2,3},{3,2},{4,5},{5,4},{6,7},{7,6},{8,9},{9,8},{10,11... | collective-permute-start | bytes 393224 | tf_op jit(solution)/shard_map/ppermute | solution.py:464
  85.1 9.8 %collective-permute-start.19 = (bf16[256,256]{1,0:T(8,128)(2,1)S(1)}, bf16[256,256]{1,0:T(8,128)(2,1)S(1)}, u32[]{:S(2)}, u32[]{:S(2)}) collective-permute-start(bf16[256,256]{1,0:T(8,128)(2,1)S(1)} %collective-permute-done.15.rest_2_), channel_id=1, source_target_pairs={{0,1},{1,0},{2,3},{3,2},{4,5},{5,4},{6,7},{7,6},{8,9},{9,8},{10,11... | collective-permute-start | bytes 393224 | tf_op jit(solution)/shard_map/ppermute | solution.py:464
  86.7 5.5 %collective-permute-start.12 = (bf16[256,128]{1,0:T(8,128)(2,1)S(1)}, bf16[256,128]{1,0:T(8,128)(2,1)S(1)}, u32[]{:S(2)}, u32[]{:S(2)}) collective-permute-start(bf16[256,128]{1,0:T(8,128)(2,1)S(1)} %get-tuple-element.49), channel_id=1, source_target_pairs={{0,24},{8,0},{16,8},{24,16},{32,56},{40,32},{48,40},{56,48},{64,88... | collective-permute-start | bytes 196616 | tf_op jit(solution)/shard_map/ppermute | solution.py:459
  94.8 1.3 %copy-start.1 = (f32[256]{0:T(256)S(1)}, f32[256]{0:T(256)}, u32[]{:S(2)}) copy-start(f32[256]{0:T(256)} %param.13) | copy-start | bytes 3076
